TPU v7x, 32 devices: a whole 2x2x4 slice. The times are simulated.
32 devices in a mesh: frame: 8 (over y, x, core), space: 4 (over z).
Axes of the slice: x: 2, y: 2, z: 4, core: 2. Of those that a mesh axis runs over, the one named last changes fastest.
Arguments:
- query_vectors: bfloat16 [32, 12, 12, 1024], P('frame', 'space'), may hold values from -6 to 6
- key_vectors: bfloat16 [32, 12, 12, 1024], P('frame', 'space'), may hold values from -6 to 6
- value_vectors: bfloat16 [32, 12, 12, 1024], P('frame', 'space'), may hold values from -6 to 6
- out_cotangent: bfloat16 [32, 12, 12, 1024], P('frame', 'space'), may hold values from -6 to 6
- partner_mask: int32 [32, 3], replicated, may hold values 0 or 1
Outputs:
- attended: bfloat16 [32, 12, 12, 1024], P('frame', 'space')
- query_grad: bfloat16 [32, 12, 12, 1024], P('frame', 'space')
- key_grad: bfloat16 [32, 12, 12, 1024], P('frame', 'space')
- value_grad: bfloat16 [32, 12, 12, 1024], P('frame', 'space')
All inputs are finite; a program needn't handle non-finite values.
Results may differ from a plain program's by a relative error of at most 0.011.
Values may be sent and summed in bfloat16 or wider, within the bound.
No kernel may reach another device: no remote copies, remote signals or barrier semaphores. Data moves between devices by JAX's collectives and lax.ppermute only.
A program may use at most 128 MiB of HBM per device.

v0:
```python
import functools

import jax
import jax.numpy as jnp
from jax import lax
from jax.experimental import pallas as pl
from jax.experimental.pallas import tpu as pltpu
from jax.sharding import PartitionSpec as P


HEAD_DIM = 64
SCALE = 0.125
NEG = -1e30
PAIR = 2 * HEAD_DIM
PAIRS = 2
PART = PAIRS * PAIR
CHUNK = 16
BF16 = jnp.bfloat16
F32 = jnp.float32


def swap(value, bit):
    size = lax.axis_size("frame")
    return lax.ppermute(value, "frame", [(i, i ^ 1 << bit) for i in range(size)])


def swaps(value, bits):
    return [swap(value, bit) for bit in range(bits)]


def exchange(value, side):
    pairs = []
    for low in range(side, lax.axis_size("space") - 1, 2):
        pairs += [(low, low + 1), (low + 1, low)]
    return lax.ppermute(value, "space", pairs)


def struct(*shape, dtype=BF16):
    return jax.ShapeDtypeStruct(shape, dtype)


def call(kernel, outs, ins, flops=0, exps=0, scratch=(), limit=4 << 20, table=None, to_hbm=()):
    size = sum(a.size * a.dtype.itemsize for a in ins) + sum(
        o.size * jnp.dtype(o.dtype).itemsize for o in outs
    )
    ins = [pltpu.with_memory_space_constraint(a, pltpu.VMEM) for a in ins]
    specs = [pl.BlockSpec(memory_space=pltpu.VMEM) for _ in ins]
    if table is not None:
        ins = ins + [table]
        specs = specs + [pl.BlockSpec(memory_space=pltpu.SMEM)]
    return pl.pallas_call(
        kernel,
        out_shape=tuple(
            o if i in to_hbm else pltpu.VMEM(o.shape, o.dtype) for i, o in enumerate(outs)
        ),
        in_specs=specs,
        out_specs=tuple(pl.BlockSpec(memory_space=pltpu.VMEM) for _ in outs),
        scratch_shapes=list(scratch),
        compiler_params=pltpu.CompilerParams(vmem_limit_bytes=limit),
        cost_estimate=pl.CostEstimate(flops=flops, bytes_accessed=size, transcendentals=exps),
    )(*ins)


def edge_rows(rows):
    odd = lax.rem(lax.axis_index("space"), 2)
    return (rows - 1) * (1 - odd), (rows - 1) * odd


def pack_kernel(n, *refs):
    sources, (packed, *edges) = refs[:n], refs[-3:]
    rows, columns, frames, width = sources[0].shape
    for at, source in enumerate(sources):
        for row in range(rows):
            packed[at * rows + row] = source[row].reshape(columns * frames, width)
        for edge, row in zip(edges, edge_rows(rows)):
            edge[at] = source[row].reshape(columns * frames, width)


def pack(sources, after=()):
    rows, columns, frames, width = sources[0].shape
    edge = struct(len(sources), columns * frames, width)
    outs = [struct(len(sources) * rows, columns * frames, width), edge, edge]
    kernel = functools.partial(pack_kernel, len(sources))
    return call(kernel, outs, sources + list(after))


def join_kernel(*refs):
    sources, target = refs[:-1], refs[-1]
    for at, source in enumerate(sources):
        for slot in range(source.shape[0]):
            target[at * source.shape[0] + slot] = source[slot]


def join(sources):
    shape = (len(sources) * sources[0].shape[0],) + sources[0].shape[1:]
    return call(join_kernel, [struct(*shape, dtype=sources[0].dtype)], sources)[0]


def head_rows(value, lane_head):
    zero = jnp.zeros_like(value)
    return jnp.concatenate([jnp.where(lane_head == h, value, zero) for h in range(2)], axis=0)


def head_lanes(stacked, lane_head):
    tokens = stacked.shape[0] // 2
    return jnp.where(lane_head == 0, stacked[:tokens], stacked[tokens:])


def nt(a, b):
    return lax.dot_general(a, b, (((1,), (1,)), ((), ())), preferred_element_type=F32)


def nn(a, b):
    return jnp.dot(a, b, preferred_element_type=F32)


class Pieces:
    def __init__(self, refs, rows, mids, rim_slots):
        self.rows = rows
        self.mids = [(refs[i], s) for i, s in mids]
        self.rims = [[(refs[i], s) for i, s in side] for side in rim_slots]

    def window(self, kind, lanes):
        out = []
        for at in range(3):
            for block, (mid, base) in enumerate(self.mids):
                if isinstance(kind, int):
                    out.append(mid[base + kind - 1 + at, :, lanes])
                elif at == 0:
                    ref, slot = self.rims[int(kind)][block]
                    out.append(ref[slot, :, lanes])
                else:
                    edge = edge_rows(self.rows)[int(kind)]
                    inner = jnp.where(edge == 0, 1, edge - 1)
                    out.append(mid[base + (edge if at == 1 else inner), :, lanes])
        return jnp.concatenate(out, axis=0)


def row_of(kind, rows):
    return kind if isinstance(kind, int) else edge_rows(rows)[int(kind)]


def rim_open(side):
    band, size = lax.axis_index("space"), lax.axis_size("space")
    odd = lax.rem(band, 2)
    up = (odd == 0) if side == 0 else (odd == 1)
    other = jnp.where(up, band + 1, band - 1)
    return (other >= 0) & (other < size)


def build_masks(mask_ref, kinds, blocks, frames, tokens, table, queries_here):
    shape = (8, blocks * tokens)
    lane = lax.broadcasted_iota(jnp.int32, shape, 1)
    sub = lax.broadcasted_iota(jnp.int32, shape, 0)
    bad = NEG if queries_here else -NEG
    which = sub if queries_here else lane
    which = lax.rem(which, frames)
    group = lane // tokens
    here = lax.axis_index("frame")
    value = jnp.zeros(shape, F32)
    for block in range(1, blocks):
        owner = here if queries_here else jnp.bitwise_xor(here, 1 << (block - 1))
        for frame in range(frames):
            off = jnp.where(table[block - 1, owner * frames + frame] == 1, 0.0, bad)
            value = jnp.where((group == block) & (which == frame), off.astype(F32), value)
    for slot, kind in enumerate(kinds):
        first = value
        if not isinstance(kind, int):
            first = value + jnp.where(rim_open(int(kind)), 0.0, bad).astype(F32)
        mask_ref[slot] = jnp.concatenate([first, value, value], axis=1)


def forward_kernel(layout, kinds, carried, *refs):
    qg = refs[layout["own"]]
    rows = qg.shape[0] // 2
    keys, values = (Pieces(refs, rows, *layout[name]) for name in ("k", "v"))
    n_in = layout["n_in"]
    table = refs[n_in]
    out, dq, stats = refs[n_in + 1 :][:3]
    mask, s_scr, d_scr, p_scr = refs[-4:]
    tokens, width = qg.shape[1:]
    columns, frames = out.shape[1:3]
    count = len(keys.mids)
    if carried:
        for target, source in zip((out, dq), refs[n_in - 3 : n_in - 1]):
            for at, row in enumerate(carried):
                target[row] = source[at]
        for at in range(len(carried)):
            stats[at] = refs[n_in - 1][at]
    build_masks(mask, kinds, count, frames, tokens, table, True)
    lane_head = lax.broadcasted_iota(jnp.int32, (tokens, PAIR), 1) // HEAD_DIM
    lane = lax.broadcasted_iota(jnp.int32, (2 * tokens, 128), 1)
    slot_of = lambda row: row if carried else row - 1
    units = [(slot, pair) for slot in range(len(kinds)) for pair in range(PAIRS)]

    def step(group, _):
        starts = [pl.multiple_of(group * PART + pair * PAIR, PAIR) for pair in range(PAIRS)]
        lanes_of = [pl.ds(start, PAIR) for start in starts]
        for unit, (slot, pair) in enumerate(units):
            lanes, kind = lanes_of[pair], kinds[slot]
            row = row_of(kind, rows)
            s_scr[unit] = nt(head_rows(qg[row, :, lanes] * SCALE, lane_head), keys.window(kind, lanes))
            d_scr[unit] = nt(head_rows(qg[rows + row, :, lanes], lane_head), values.window(kind, lanes))
        tops, totals = [], []
        for unit, (slot, pair) in enumerate(units):
            top_parts, total_parts = [], []
            bias = jnp.concatenate([mask[slot]] * (CHUNK // 8), axis=0)
            for start in range(0, 2 * tokens, CHUNK):
                scores = s_scr[unit, start : start + CHUNK, :] + bias
                top = jnp.max(scores, axis=1, keepdims=True)
                raw = jnp.exp(scores - top)
                s_scr[unit, start : start + CHUNK, :] = raw
                p_scr[unit, start : start + CHUNK, :] = raw.astype(BF16)
                top_parts.append(top)
                total_parts.append(jnp.sum(raw, axis=1, keepdims=True))
            tops.append(jnp.concatenate(top_parts, axis=0))
            totals.append(jnp.concatenate(total_parts, axis=0))
        cols = jnp.zeros((2 * tokens, 128), F32)
        deltas, scales = [], []
        for unit, (slot, pair) in enumerate(units):
            lanes, kind = lanes_of[pair], kinds[slot]
            row = row_of(kind, rows)
            scale = 1.0 / totals[unit]
            wide = nn(p_scr[unit], values.window(kind, lanes)) * scale
            attended = head_lanes(wide, lane_head).astype(BF16)
            out[slot_of(row), :, :, lanes] = attended.reshape(columns, frames, PAIR)
            prod = qg[rows + row, :, lanes].astype(F32) * attended.astype(F32)
            delta = jnp.sum(head_rows(prod, lane_head), axis=1, keepdims=True)
            deltas.append(delta)
            scales.append(scale)
            cols = jnp.where(lane == 2 * unit, tops[unit] + jnp.log(totals[unit]), cols)
            cols = jnp.where(lane == 2 * unit + 1, delta, cols)
        for unit, (slot, pair) in enumerate(units):
            for start in range(0, 2 * tokens, CHUNK):
                part = slice(start, start + CHUNK)
                grad_scores = s_scr[unit, part, :] * (d_scr[unit, part, :] - deltas[unit][part])
                p_scr[unit, part, :] = grad_scores.astype(BF16)
        for unit, (slot, pair) in enumerate(units):
            lanes, kind = lanes_of[pair], kinds[slot]
            wide = nn(p_scr[unit], keys.window(kind, lanes)) * (scales[unit] * SCALE)
            grad_q = head_lanes(wide, lane_head).astype(BF16)
            dq[slot_of(row_of(kind, rows)), :, :, lanes] = grad_q.reshape(columns, frames, PAIR)
        turned = cols.T
        for unit, (slot, pair) in enumerate(units):
            for which in range(2):
                line = turned[2 * unit + which : 2 * unit + which + 1]
                for h in range(2):
                    to = which * 2 * PAIRS + pair * 2 + h
                    stats[len(carried) + slot, group, to : to + 1, :] = line[:, h * tokens : (h + 1) * tokens]
        return 0

    lax.fori_loop(0, width // PART, step, 0)


def backward_kernel(layout, kinds, carried, *refs):
    kv = refs[layout["own"]]
    rows = kv.shape[0] // 2
    queries, grads = (Pieces(refs, rows, *layout[name]) for name in ("q", "g"))
    n_in = layout["n_in"]
    table = refs[n_in]
    dk, dv = refs[n_in + 1 :][:2]
    mask, s_scr, d_scr, p_scr, t_scr = refs[-5:]
    tokens, width = kv.shape[1:]
    columns, frames = dk.shape[1:3]
    count = len(queries.mids)
    for target, source in zip((dk, dv), refs[n_in - 2 : n_in]):
        for at, row in enumerate(carried):
            target[row] = source[at]
    build_masks(mask, kinds, count, frames, tokens, table, False)
    lane_head = lax.broadcasted_iota(jnp.int32, (tokens, PAIR), 1) // HEAD_DIM
    slot_of = lambda row: row if carried else row - 1
    units = [(slot, pair) for slot in range(len(kinds)) for pair in range(PAIRS)]

    def stat_window(kind, group):
        out = []
        mids, rim = layout["s"]
        inner = rows - 2

        def stat_at(block, row):
            if isinstance(row, int) and 0 < row < rows - 1:
                return refs[mids[block]][row - 1, group]
            first, _ = edge_rows(rows)
            return refs[mids[block]][jnp.where(first == row, inner, inner + 1), group]

        for at in range(3):
            for block in range(count):
                if isinstance(kind, int):
                    out.append(stat_at(block, kind - 1 + at))
                elif at == 0:
                    index, slot = rim[int(kind)][block]
                    out.append(refs[index][slot, group])
                elif at == 1:
                    out.append(refs[mids[block]][inner + int(kind), group])
                else:
                    place = edge_rows(rows)[int(kind)]
                    out.append(refs[mids[block]][jnp.where(place == 0, 1, place - 1) - 1, group])
        return jnp.concatenate(out, axis=1)

    def step(group, _):
        lanes_of = [pl.ds(pl.multiple_of(group * PART + pair * PAIR, PAIR), PAIR) for pair in range(PAIRS)]
        for unit, (slot, pair) in enumerate(units):
            lanes, kind = lanes_of[pair], kinds[slot]
            row = row_of(kind, rows)
            s_scr[unit] = nt(head_rows(kv[row, :, lanes] * SCALE, lane_head), queries.window(kind, lanes))
            d_scr[unit] = nt(head_rows(kv[rows + row, :, lanes], lane_head), grads.window(kind, lanes))
        stats = [stat_window(kind, group) for kind in kinds]
        for unit, (slot, pair) in enumerate(units):
            stat = stats[slot]
            for h in range(2):
                at = pair * 2 + h
                lse = stat[at : at + 1] + mask[slot, 0:1]
                delta = stat[2 * PAIRS + at : 2 * PAIRS + at + 1]
                for start in range(h * tokens, (h + 1) * tokens, CHUNK):
                    part = slice(start, start + CHUNK)
                    probs = jnp.exp(s_scr[unit, part, :] - lse)
                    p_scr[unit, part, :] = probs.astype(BF16)
                    t_scr[unit, part, :] = (probs * (d_scr[unit, part, :] - delta)).astype(BF16)
        for unit, (slot, pair) in enumerate(units):
            lanes, kind = lanes_of[pair], kinds[slot]
            row = row_of(kind, rows)
            grad_v = head_lanes(nn(p_scr[unit], grads.window(kind, lanes)), lane_head).astype(BF16)
            dv[slot_of(row), :, :, lanes] = grad_v.reshape(columns, frames, PAIR)
            grad_k = head_lanes(nn(t_scr[unit], queries.window(kind, lanes)), lane_head) * SCALE
            dk[slot_of(row), :, :, lanes] = grad_k.astype(BF16).reshape(columns, frames, PAIR)
        return 0

    lax.fori_loop(0, width // PART, step, 0)


def per_device(query_vectors, key_vectors, value_vectors, out_cotangent, partner_mask):
    frames, rows, columns, width = query_vectors.shape
    bits = min(4, lax.axis_size("frame").bit_length() - 1)
    count = bits + 1
    tokens = frames * columns
    groups = width // PART
    window = 3 * count * tokens
    table = partner_mask.T
    turn = lambda a: jnp.transpose(a, (1, 2, 0, 3))
    back = lambda a: jnp.transpose(a, (2, 0, 1, 3))

    kv, kv_edge0, kv_edge1 = pack([turn(key_vectors), turn(value_vectors)])
    kvs = [kv] + swaps(kv, bits)
    kv_rims = [exchange(kv_edge0, 0), exchange(kv_edge1, 1)]
    kv_rims_of = swaps(join(kv_rims), bits)
    qg, qg_edge0, qg_edge1 = pack([turn(query_vectors), turn(out_cotangent)], [kv_edge0])
    qg_rims = [exchange(qg_edge0, 0), exchange(qg_edge1, 1)]
    qgs = [qg] + swaps(qg, bits)
    qg_rims_of = swaps(join(qg_rims), bits)

    inner_kinds = list(range(1, rows - 1))
    edge_kinds = ["0", "1"]
    inner = len(inner_kinds)
    work = 4 * 2 * (width // PAIR) * 2 * tokens * window * PAIR
    exps = (width // HEAD_DIM) * tokens * window
    line = lambda n: struct(n, columns, frames, width)

    def scratches(n, extra):
        units = n * PAIRS
        wide = [pltpu.VMEM((n, 8, window), F32)]
        wide += [pltpu.VMEM((units, 2 * tokens, window), F32)] * 2
        return wide + [pltpu.VMEM((units, 2 * tokens, window), BF16)] * extra

    def gathered(at, rim_at, tensor):
        mids = [(at + block, tensor * rows) for block in range(count)]
        if rim_at is None:
            return mids, []
        sides = []
        for side in range(2):
            own = [(rim_at + side, tensor)]
            sides.append(own + [(rim_at + 2 + bit, 2 * side + tensor) for bit in range(bits)])
        return mids, sides

    stat = lambda n: struct(n, groups, 4 * PAIRS, tokens, dtype=F32)
    ins = [qg] + kvs
    layout = {"n_in": len(ins), "own": 0, "k": gathered(1, None, 0), "v": gathered(1, None, 1)}
    inner_out = call(
        functools.partial(forward_kernel, layout, inner_kinds, ()),
        [line(inner), line(inner), stat(inner)], ins,
        flops=work * inner, exps=exps * inner, scratch=scratches(inner, 1), limit=10 << 20, table=table,
    )
    rim_at = len(ins)
    ins = ins + kv_rims + kv_rims_of + list(inner_out)
    layout = {"n_in": len(ins), "own": 0, "k": gathered(1, rim_at, 0), "v": gathered(1, rim_at, 1)}
    attended, dq, stats = call(
        functools.partial(forward_kernel, layout, edge_kinds, inner_kinds),
        [line(rows), line(rows), stat(rows)], ins, to_hbm=(0, 1),
        flops=work * 2, exps=exps * 2, scratch=scratches(2, 1), limit=10 << 20, table=table,
    )
    ss = [stats] + swaps(stats, bits)

    def stat_edge_kernel(*refs):
        for slot, source in enumerate(refs[:-2]):
            for side in range(2):
                refs[len(refs) - 2 + side][slot] = source[inner + side]

    s_rims = call(stat_edge_kernel, [stat(count)] * 2, ss)
    s_rims = [exchange(edge, side) for side, edge in enumerate(s_rims)]

    ins = [kv] + qgs + ss
    mids = range(1 + count, 1 + 2 * count)
    layout = {"n_in": len(ins), "own": 0, "q": gathered(1, None, 0), "g": gathered(1, None, 1), "s": (mids, None)}
    inner_out = call(
        functools.partial(backward_kernel, layout, inner_kinds, ()),
        [line(inner), line(inner)], ins,
        flops=work * inner, exps=exps * inner, scratch=scratches(inner, 2), limit=10 << 20, table=table,
    )
    rim_at = len(ins)
    ins = ins + qg_rims + qg_rims_of + s_rims + list(inner_out)
    rim = [[(rim_at + 2 + bits + side, block) for block in range(count)] for side in range(2)]
    layout = {"n_in": len(ins), "own": 0, "q": gathered(1, rim_at, 0), "g": gathered(1, rim_at, 1), "s": (mids, rim)}
    dk, dv = call(
        functools.partial(backward_kernel, layout, edge_kinds, inner_kinds),
        [line(rows), line(rows)], ins, to_hbm=(0, 1),
        flops=work * 2, exps=exps * 2, scratch=scratches(2, 2), limit=10 << 20, table=table,
    )
    return back(attended), back(dq), back(dk), back(dv)


def solution(mesh):
    spec = P("frame", "space", None, None)

    return jax.shard_map(
        per_device,
        mesh=mesh,
        in_specs=(spec, spec, spec, spec, P()),
        out_specs=(spec, spec, spec, spec),
        check_vma=False,
    )
```

profile of v0, /device:TPU:0, one launch (start us, length us, event | category | flops | bytes accessed | tf_op | source)
XLA Modules:
  0.0 75.3 jit_solution(15861743619555413134)
XLA Ops:
  0.6 0.0 copy-start.2
  0.6 1.0 %copy-done.2 = bf16[4,3,12,1024]{3,0,2,1:T(4,128)(2,1)S(1)} copy-done((bf16[4,3,12,1024]{3,0,2,1:T(4,128)(2,1)S(1)}, bf16[4,3,12,1024]{3,0,2,1:T(4,128)(2,1)}, u32[]{:S(2)}) %copy-start.2) | copy-done | bytes 294936
  1.6 0.0 copy-start.3
  1.6 1.0 %copy-done.3 = bf16[4,3,12,1024]{3,0,2,1:T(4,128)(2,1)S(1)} copy-done((bf16[4,3,12,1024]{3,0,2,1:T(4,128)(2,1)S(1)}, bf16[4,3,12,1024]{3,0,2,1:T(4,128)(2,1)}, u32[]{:S(2)}) %copy-start.3) | copy-done | bytes 294936
  2.6 0.1 shard_map.84
  2.7 0.7 collective-permute-start.4
  3.4 0.0 copy-start
  3.4 0.0 copy-start.1
  3.4 5.9 %collective-permute-start.3 = (bf16[2,48,1024]{2,1,0:T(8,128)(2,1)S(1)}, bf16[2,48,1024]{2,1,0:T(8,128)(2,1)S(1)}, u32[]{:S(2)}, u32[]{:S(2)}) collective-permute-start(bf16[2,48,1024]{2,1,0:T(8,128)(2,1)S(1)} %get-tuple-element.22.refs_2_), channel_id=1, source_target_pairs={{0,1},{1,0},{2,3},{3,2},{4,5},{5,4},{6,7},{7,6},{8,9},{9,8},{10,11... | collective-permute-start | bytes 589832 | tf_op jit(solution)/shard_map/ppermute | solution.py:35
  9.3 0.0 collective-permute-done.4.refs_1_.refs_6_
  9.3 4.6 %collective-permute-done.3.refs_0_.refs_5_ = bf16[2,48,1024]{2,1,0:T(8,128)(2,1)S(1)} collective-permute-done((bf16[2,48,1024]{2,1,0:T(8,128)(2,1)S(1)}, bf16[2,48,1024]{2,1,0:T(8,128)(2,1)S(1)}, u32[]{:S(2)}, u32[]{:S(2)}) %collective-permute-start.3) | collective-permute-done | bytes 196640 | tf_op jit(solution)/shard_map/ppermute | solution.py:35
  14.0 1.6 %collective-permute-start.7 = (bf16[4,48,1024]{2,1,0:T(8,128)(2,1)S(1)}, bf16[4,48,1024]{2,1,0:T(8,128)(2,1)S(1)}, u32[]{:S(2)}, u32[]{:S(2)}) collective-permute-start(bf16[4,48,1024]{2,1,0:T(8,128)(2,1)S(1)} %shard_map.86), channel_id=1, source_target_pairs={{0,16},{4,20},{8,24},{12,28},{16,0},{20,4},{24,8},{28,12},{1,17},{... | collective-permute-start | bytes 1179656 | tf_op jit(solution)/shard_map/ppermute | solution.py:24
  15.5 1.5 %collective-permute-start.6 = (bf16[4,48,1024]{2,1,0:T(8,128)(2,1)S(1)}, bf16[4,48,1024]{2,1,0:T(8,128)(2,1)S(1)}, u32[]{:S(2)}, u32[]{:S(2)}) collective-permute-start(bf16[4,48,1024]{2,1,0:T(8,128)(2,1)S(1)} %shard_map.86), channel_id=1, source_target_pairs={{0,8},{4,12},{8,0},{12,4},{16,24},{20,28},{24,16},{28,20},{1,9},{5... | collective-permute-start | bytes 1179656 | tf_op jit(solution)/shard_map/ppermute | solution.py:24
  17.0 0.5 collective-permute-start.2
  17.5 0.5 collective-permute-start.1
  18.1 0.0 collective-permute-start
  18.1 7.9 %collective-permute-done.7.refs_9_ = bf16[4,48,1024]{2,1,0:T(8,128)(2,1)S(1)} collective-permute-done((bf16[4,48,1024]{2,1,0:T(8,128)(2,1)S(1)}, bf16[4,48,1024]{2,1,0:T(8,128)(2,1)S(1)}, u32[]{:S(2)}, u32[]{:S(2)}) %collective-permute-start.7) | collective-permute-done | bytes 393248 | tf_op jit(solution)/shard_map/ppermute | solution.py:24
  26.0 0.0 collective-permute-start.5
  26.0 0.0 copy-done
  26.0 0.0 copy-done.1
  26.0 0.1 shard_map.85
  26.1 1.4 %collective-permute-done.6.refs_8_ = bf16[4,48,1024]{2,1,0:T(8,128)(2,1)S(1)} collective-permute-done((bf16[4,48,1024]{2,1,0:T(8,128)(2,1)S(1)}, bf16[4,48,1024]{2,1,0:T(8,128)(2,1)S(1)}, u32[]{:S(2)}, u32[]{:S(2)}) %collective-permute-start.6) | collective-permute-done | bytes 393248 | tf_op jit(solution)/shard_map/ppermute | solution.py:24
  27.5 0.5 collective-permute-start.10
  28.0 0.0 collective-permute-done.5.refs_7_
  28.0 1.5 %collective-permute-start.9 = (bf16[6,48,1024]{2,1,0:T(8,128)(2,1)S(1)}, bf16[6,48,1024]{2,1,0:T(8,128)(2,1)S(1)}, u32[]{:S(2)}, u32[]{:S(2)}) collective-permute-start(bf16[6,48,1024]{2,1,0:T(8,128)(2,1)S(1)} %get-tuple-element.23.refs_0_.refs_1_), channel_id=1, source_target_pairs={{0,8},{4,12},{8,0},{12,4},{16,24},{20,28},{24,16},{28,20},{1,9},{5... | collective-permute-start | bytes 1769480 | tf_op jit(solution)/shard_map/ppermute | solution.py:24
  29.5 9.1 %collective-permute-done.2.refs_4_ = bf16[6,48,1024]{2,1,0:T(8,128)(2,1)S(1)} collective-permute-done((bf16[6,48,1024]{2,1,0:T(8,128)(2,1)S(1)}, bf16[6,48,1024]{2,1,0:T(8,128)(2,1)S(1)}, u32[]{:S(2)}, u32[]{:S(2)}) %collective-permute-start.2) | collective-permute-done | bytes 589856 | tf_op jit(solution)/shard_map/ppermute | solution.py:24
  38.6 0.0 collective-permute-start.8
  38.7 1.5 %collective-permute-done.1.refs_3_ = bf16[6,48,1024]{2,1,0:T(8,128)(2,1)S(1)} collective-permute-done((bf16[6,48,1024]{2,1,0:T(8,128)(2,1)S(1)}, bf16[6,48,1024]{2,1,0:T(8,128)(2,1)S(1)}, u32[]{:S(2)}, u32[]{:S(2)}) %collective-permute-start.1) | collective-permute-done | bytes 589856 | tf_op jit(solution)/shard_map/ppermute | solution.py:24
  40.2 0.0 copy-start.4
  40.2 1.7 %collective-permute-start.14 = (bf16[2,48,1024]{2,1,0:T(8,128)(2,1)S(1)}, bf16[2,48,1024]{2,1,0:T(8,128)(2,1)S(1)}, u32[]{:S(2)}, u32[]{:S(2)}) collective-permute-start(bf16[2,48,1024]{2,1,0:T(8,128)(2,1)S(1)} %get-tuple-element.32), channel_id=1, source_target_pairs={{0,1},{1,0},{2,3},{3,2},{4,5},{5,4},{6,7},{7,6},{8,9},{9,8},{10,11... | collective-permute-start | bytes 589832 | tf_op jit(solution)/shard_map/ppermute | solution.py:35
  41.9 0.0 collective-permute-done.refs_2_
  41.9 0.7 collective-permute-start.15
  42.6 0.0 copy-done.4
  42.6 4.5 %shard_map.87 = (bf16[1,12,4,1024]{3,2,1,0:T(4,128)(2,1)S(1)}, bf16[1,12,4,1024]{3,2,1,0:T(4,128)(2,1)S(1)}, f32[1,4,8,48]{3,2,1,0:T(8,128)S(1)}) custom-call(bf16[6,48,1024]{2,1,0:T(8,128)(2,1)S(1)} %get-tuple-element.23.refs_0_.refs_1_, bf16[6,48,1024]{2,1,0:T(8,128)(2,1)S(1)} %get-tuple-element.24.refs_1_.refs_0_, ...), custom_call_target="tpu_custom_call" | custom-call | flops 452984832 | bytes 3151872 | tf_op jit(solution)/shard_map/pallas_call | solution.py:51
  47.1 7.6 %shard_map.88 = (bf16[3,12,4,1024]{3,2,1,0:T(4,128)(2,1)}, bf16[3,12,4,1024]{3,2,1,0:T(4,128)(2,1)}, f32[3,4,8,48]{3,2,1,0:T(8,128)S(1)}) custom-call(bf16[6,48,1024]{2,1,0:T(8,128)(2,1)S(1)} %get-tuple-element.23.refs_0_.refs_1_, bf16[6,48,1024]{2,1,0:T(8,128)(2,1)S(1)} %get-tuple-element.24.refs_1_.refs_0_, ...), custom_call_target="tpu_custom_call" | custom-call | flops 905969664 | bytes 5332992 | tf_op jit(solution)/shard_map/pallas_call | solution.py:51
  54.7 0.0 collective-permute-done.14.refs_0_.refs_9_
  54.7 0.5 collective-permute-start.13
  55.2 0.0 collective-permute-done.15.refs_1_.refs_10_
  55.2 1.5 %collective-permute-start.12 = (f32[3,4,8,48]{3,2,1,0:T(8,128)S(1)}, f32[3,4,8,48]{3,2,1,0:T(8,128)S(1)}, u32[]{:S(2)}, u32[]{:S(2)}) collective-permute-start(f32[3,4,8,48]{3,2,1,0:T(8,128)S(1)} %get-tuple-element.31.refs_0_.refs_5_), channel_id=1, source_target_pairs={{0,8},{4,12},{8,0},{12,4},{16,24},{20,28},{24,16},{28,20},{1,9},{5... | collective-permute-start | bytes 55304 | tf_op jit(solution)/shard_map/ppermute | solution.py:24
  56.7 0.0 collective-permute-done.10.refs_4_
  56.7 0.0 collective-permute-start.11
  56.7 2.1 %collective-permute-done.13.refs_3_.refs_8_ = f32[3,4,8,48]{3,2,1,0:T(8,128)S(1)} collective-permute-done((f32[3,4,8,48]{3,2,1,0:T(8,128)S(1)}, f32[3,4,8,48]{3,2,1,0:T(8,128)S(1)}, u32[]{:S(2)}, u32[]{:S(2)}) %collective-permute-start.13) | collective-permute-done | bytes 18464 | tf_op jit(solution)/shard_map/ppermute | solution.py:24
  58.8 0.5 collective-permute-start.18
  59.3 0.0 collective-permute-done.12.refs_2_.refs_7_
  59.3 1.5 %collective-permute-start.17 = (bf16[4,48,1024]{2,1,0:T(8,128)(2,1)S(1)}, bf16[4,48,1024]{2,1,0:T(8,128)(2,1)S(1)}, u32[]{:S(2)}, u32[]{:S(2)}) collective-permute-start(bf16[4,48,1024]{2,1,0:T(8,128)(2,1)S(1)} %shard_map.89), channel_id=1, source_target_pairs={{0,8},{4,12},{8,0},{12,4},{16,24},{20,28},{24,16},{28,20},{1,9},{5... | collective-permute-start | bytes 1179656 | tf_op jit(solution)/shard_map/ppermute | solution.py:24
  60.8 0.0 collective-permute-done.11.refs_1_.refs_6_
  60.8 0.0 collective-permute-start.16
  60.8 0.0 collective-permute-done.9.refs_3_
  60.8 2.0 %collective-permute-start.19 = (f32[4,4,8,48]{3,2,1,0:T(8,128)S(1)}, f32[4,4,8,48]{3,2,1,0:T(8,128)S(1)}, u32[]{:S(2)}, u32[]{:S(2)}) collective-permute-start(f32[4,4,8,48]{3,2,1,0:T(8,128)S(1)} %get-tuple-element.34), channel_id=1, source_target_pairs={{0,1},{1,0},{2,3},{3,2},{4,5},{5,4},{6,7},{7,6},{8,9},{9,8},{10,11... | collective-permute-start | bytes 73736 | tf_op jit(solution)/shard_map/ppermute | solution.py:35
  62.9 0.0 collective-permute-done.8.refs_2_
  62.9 0.7 collective-permute-start.20
  63.5 3.1 %shard_map.91 = (bf16[1,12,4,1024]{3,2,1,0:T(4,128)(2,1)S(1)}, bf16[1,12,4,1024]{3,2,1,0:T(4,128)(2,1)S(1)}) custom-call(bf16[6,48,1024]{2,1,0:T(8,128)(2,1)S(1)} %get-tuple-element.24.refs_1_.refs_0_, bf16[6,48,1024]{2,1,0:T(8,128)(2,1)S(1)} %get-tuple-element.23.refs_0_.refs_1_, bf16[6,48,1024]{2,1,0:T(8,128)(2,1)S(1)} %collective-permute-done.8.refs_2_, ...), custom_call_target="tpu_custom_call" | custom-call | flops 452984832 | bytes 3219456 | tf_op jit(solution)/shard_map/pallas_call | solution.py:51
  66.6 1.7 %collective-permute-done.18.refs_13_ = bf16[4,48,1024]{2,1,0:T(8,128)(2,1)S(1)} collective-permute-done((bf16[4,48,1024]{2,1,0:T(8,128)(2,1)S(1)}, bf16[4,48,1024]{2,1,0:T(8,128)(2,1)S(1)}, u32[]{:S(2)}, u32[]{:S(2)}) %collective-permute-start.18) | collective-permute-done | bytes 393248 | tf_op jit(solution)/shard_map/ppermute | solution.py:24
  68.3 1.2 %collective-permute-done.17.refs_12_ = bf16[4,48,1024]{2,1,0:T(8,128)(2,1)S(1)} collective-permute-done((bf16[4,48,1024]{2,1,0:T(8,128)(2,1)S(1)}, bf16[4,48,1024]{2,1,0:T(8,128)(2,1)S(1)}, u32[]{:S(2)}, u32[]{:S(2)}) %collective-permute-start.17) | collective-permute-done | bytes 393248 | tf_op jit(solution)/shard_map/ppermute | solution.py:24
  69.6 0.0 collective-permute-done.16.refs_11_
  69.6 0.0 collective-permute-done.19.refs_14_
  69.6 0.0 collective-permute-done.20.refs_15_
  69.6 5.7 %shard_map.92 = (bf16[3,12,4,1024]{3,2,1,0:T(4,128)(2,1)}, bf16[3,12,4,1024]{3,2,1,0:T(4,128)(2,1)}) custom-call(bf16[6,48,1024]{2,1,0:T(8,128)(2,1)S(1)} %get-tuple-element.24.refs_1_.refs_0_, bf16[6,48,1024]{2,1,0:T(8,128)(2,1)S(1)} %get-tuple-element.23.refs_0_.refs_1_, bf16[6,48,1024]{2,1,0:T(8,128)(2,1)S(1)} %collective-permute-done.8.refs_2_, ...), custom_call_target="tpu_custom_call" | custom-call | flops 905969664 | bytes 5431296 | tf_op jit(solution)/shard_map/pallas_call | solution.py:51
  (3 shorter events, 0.1 us)
Async XLA Ops:
  0.6 1.0 %copy-start.2 = (bf16[4,3,12,1024]{3,0,2,1:T(4,128)(2,1)S(1)}, bf16[4,3,12,1024]{3,0,2,1:T(4,128)(2,1)}, u32[]{:S(2)}) copy-start(bf16[4,3,12,1024]{3,0,2,1:T(4,128)(2,1)} %param.6) | copy-start | bytes 884740
  1.6 1.0 %copy-start.3 = (bf16[4,3,12,1024]{3,0,2,1:T(4,128)(2,1)S(1)}, bf16[4,3,12,1024]{3,0,2,1:T(4,128)(2,1)}, u32[]{:S(2)}) copy-start(bf16[4,3,12,1024]{3,0,2,1:T(4,128)(2,1)} %param.7) | copy-start | bytes 884740
  2.7 6.6 %collective-permute-start.4 = (bf16[2,48,1024]{2,1,0:T(8,128)(2,1)S(1)}, bf16[2,48,1024]{2,1,0:T(8,128)(2,1)S(1)}, u32[]{:S(2)}, u32[]{:S(2)}) collective-permute-start(bf16[2,48,1024]{2,1,0:T(8,128)(2,1)S(1)} %get-tuple-element.25), channel_id=1, source_target_pairs={{1,2},{2,1},{5,6},{6,5},{9,10},{10,9},{13,14},{14,13},{17,18},{18,... | collective-permute-start | bytes 589832 | tf_op jit(solution)/shard_map/ppermute | solution.py:35
  3.4 22.7 %copy-start = (bf16[4,3,12,1024]{3,0,2,1:T(4,128)(2,1)S(1)}, bf16[4,3,12,1024]{3,0,2,1:T(4,128)(2,1)}, u32[]{:S(2)}) copy-start(bf16[4,3,12,1024]{3,0,2,1:T(4,128)(2,1)} %param.5) | copy-start | bytes 884740
  3.4 22.7 %copy-start.1 = (bf16[4,3,12,1024]{3,0,2,1:T(4,128)(2,1)S(1)}, bf16[4,3,12,1024]{3,0,2,1:T(4,128)(2,1)}, u32[]{:S(2)}) copy-start(bf16[4,3,12,1024]{3,0,2,1:T(4,128)(2,1)} %param.8) | copy-start | bytes 884740
  3.4 10.6 %collective-permute-start.3 = (bf16[2,48,1024]{2,1,0:T(8,128)(2,1)S(1)}, bf16[2,48,1024]{2,1,0:T(8,128)(2,1)S(1)}, u32[]{:S(2)}, u32[]{:S(2)}) collective-permute-start(bf16[2,48,1024]{2,1,0:T(8,128)(2,1)S(1)} %get-tuple-element.22.refs_2_), channel_id=1, source_target_pairs={{0,1},{1,0},{2,3},{3,2},{4,5},{5,4},{6,7},{7,6},{8,9},{9,8},{10,11... | collective-permute-start | bytes 589832 | tf_op jit(solution)/shard_map/ppermute | solution.py:35
  14.0 12.1 %collective-permute-start.7 = (bf16[4,48,1024]{2,1,0:T(8,128)(2,1)S(1)}, bf16[4,48,1024]{2,1,0:T(8,128)(2,1)S(1)}, u32[]{:S(2)}, u32[]{:S(2)}) collective-permute-start(bf16[4,48,1024]{2,1,0:T(8,128)(2,1)S(1)} %shard_map.86), channel_id=1, source_target_pairs={{0,16},{4,20},{8,24},{12,28},{16,0},{20,4},{24,8},{28,12},{1,17},{... | collective-permute-start | bytes 1179656 | tf_op jit(solution)/shard_map/ppermute | solution.py:24
  15.5 12.0 %collective-permute-start.6 = (bf16[4,48,1024]{2,1,0:T(8,128)(2,1)S(1)}, bf16[4,48,1024]{2,1,0:T(8,128)(2,1)S(1)}, u32[]{:S(2)}, u32[]{:S(2)}) collective-permute-start(bf16[4,48,1024]{2,1,0:T(8,128)(2,1)S(1)} %shard_map.86), channel_id=1, source_target_pairs={{0,8},{4,12},{8,0},{12,4},{16,24},{20,28},{24,16},{28,20},{1,9},{5... | collective-permute-start | bytes 1179656 | tf_op jit(solution)/shard_map/ppermute | solution.py:24
  17.0 21.6 %collective-permute-start.2 = (bf16[6,48,1024]{2,1,0:T(8,128)(2,1)S(1)}, bf16[6,48,1024]{2,1,0:T(8,128)(2,1)S(1)}, u32[]{:S(2)}, u32[]{:S(2)}) collective-permute-start(bf16[6,48,1024]{2,1,0:T(8,128)(2,1)S(1)} %get-tuple-element.24.refs_1_.refs_0_), channel_id=1, source_target_pairs={{0,16},{4,20},{8,24},{12,28},{16,0},{20,4},{24,8},{28,12},{1,17},{... | collective-permute-start | bytes 1769480 | tf_op jit(solution)/shard_map/ppermute | solution.py:24
  17.5 22.6 %collective-permute-start.1 = (bf16[6,48,1024]{2,1,0:T(8,128)(2,1)S(1)}, bf16[6,48,1024]{2,1,0:T(8,128)(2,1)S(1)}, u32[]{:S(2)}, u32[]{:S(2)}) collective-permute-start(bf16[6,48,1024]{2,1,0:T(8,128)(2,1)S(1)} %get-tuple-element.24.refs_1_.refs_0_), channel_id=1, source_target_pairs={{0,8},{4,12},{8,0},{12,4},{16,24},{20,28},{24,16},{28,20},{1,9},{5... | collective-permute-start | bytes 1769480 | tf_op jit(solution)/shard_map/ppermute | solution.py:24
  18.1 23.8 %collective-permute-start = (bf16[6,48,1024]{2,1,0:T(8,128)(2,1)S(1)}, bf16[6,48,1024]{2,1,0:T(8,128)(2,1)S(1)}, u32[]{:S(2)}, u32[]{:S(2)}) collective-permute-start(bf16[6,48,1024]{2,1,0:T(8,128)(2,1)S(1)} %get-tuple-element.24.refs_1_.refs_0_), channel_id=1, source_target_pairs={{0,4},{4,0},{8,12},{12,8},{16,20},{20,16},{24,28},{28,24},{1,5},{5... | collective-permute-start | bytes 1769480 | tf_op jit(solution)/shard_map/ppermute | solution.py:24
  26.0 2.0 %collective-permute-start.5 = (bf16[4,48,1024]{2,1,0:T(8,128)(2,1)S(1)}, bf16[4,48,1024]{2,1,0:T(8,128)(2,1)S(1)}, u32[]{:S(2)}, u32[]{:S(2)}) collective-permute-start(bf16[4,48,1024]{2,1,0:T(8,128)(2,1)S(1)} %shard_map.86), channel_id=1, source_target_pairs={{0,4},{4,0},{8,12},{12,8},{16,20},{20,16},{24,28},{28,24},{1,5},{5... | collective-permute-start | bytes 1179656 | tf_op jit(solution)/shard_map/ppermute | solution.py:24
  27.5 29.2 %collective-permute-start.10 = (bf16[6,48,1024]{2,1,0:T(8,128)(2,1)S(1)}, bf16[6,48,1024]{2,1,0:T(8,128)(2,1)S(1)}, u32[]{:S(2)}, u32[]{:S(2)}) collective-permute-start(bf16[6,48,1024]{2,1,0:T(8,128)(2,1)S(1)} %get-tuple-element.23.refs_0_.refs_1_), channel_id=1, source_target_pairs={{0,16},{4,20},{8,24},{12,28},{16,0},{20,4},{24,8},{28,12},{1,17},{... | collective-permute-start | bytes 1769480 | tf_op jit(solution)/shard_map/ppermute | solution.py:24
  28.0 32.8 %collective-permute-start.9 = (bf16[6,48,1024]{2,1,0:T(8,128)(2,1)S(1)}, bf16[6,48,1024]{2,1,0:T(8,128)(2,1)S(1)}, u32[]{:S(2)}, u32[]{:S(2)}) collective-permute-start(bf16[6,48,1024]{2,1,0:T(8,128)(2,1)S(1)} %get-tuple-element.23.refs_0_.refs_1_), channel_id=1, source_target_pairs={{0,8},{4,12},{8,0},{12,4},{16,24},{20,28},{24,16},{28,20},{1,9},{5... | collective-permute-start | bytes 1769480 | tf_op jit(solution)/shard_map/ppermute | solution.py:24
  38.6 24.2 %collective-permute-start.8 = (bf16[6,48,1024]{2,1,0:T(8,128)(2,1)S(1)}, bf16[6,48,1024]{2,1,0:T(8,128)(2,1)S(1)}, u32[]{:S(2)}, u32[]{:S(2)}) collective-permute-start(bf16[6,48,1024]{2,1,0:T(8,128)(2,1)S(1)} %get-tuple-element.23.refs_0_.refs_1_), channel_id=1, source_target_pairs={{0,4},{4,0},{8,12},{12,8},{16,20},{20,16},{24,28},{28,24},{1,5},{5... | collective-permute-start | bytes 1769480 | tf_op jit(solution)/shard_map/ppermute | solution.py:24
  40.2 2.4 %copy-start.4 = (s32[32,3]{0,1:T(4,128)S(1)}, s32[32,3]{0,1:T(4,128)}, u32[]{:S(2)}) copy-start(s32[32,3]{0,1:T(4,128)} %param.9) | copy-start | bytes 1156
  40.2 14.5 %collective-permute-start.14 = (bf16[2,48,1024]{2,1,0:T(8,128)(2,1)S(1)}, bf16[2,48,1024]{2,1,0:T(8,128)(2,1)S(1)}, u32[]{:S(2)}, u32[]{:S(2)}) collective-permute-start(bf16[2,48,1024]{2,1,0:T(8,128)(2,1)S(1)} %get-tuple-element.32), channel_id=1, source_target_pairs={{0,1},{1,0},{2,3},{3,2},{4,5},{5,4},{6,7},{7,6},{8,9},{9,8},{10,11... | collective-permute-start | bytes 589832 | tf_op jit(solution)/shard_map/ppermute | solution.py:35
  41.9 13.3 %collective-permute-start.15 = (bf16[2,48,1024]{2,1,0:T(8,128)(2,1)S(1)}, bf16[2,48,1024]{2,1,0:T(8,128)(2,1)S(1)}, u32[]{:S(2)}, u32[]{:S(2)}) collective-permute-start(bf16[2,48,1024]{2,1,0:T(8,128)(2,1)S(1)} %get-tuple-element.33), channel_id=1, source_target_pairs={{1,2},{2,1},{5,6},{6,5},{9,10},{10,9},{13,14},{14,13},{17,18},{18,... | collective-permute-start | bytes 589832 | tf_op jit(solution)/shard_map/ppermute | solution.py:35
  54.7 4.1 %collective-permute-start.13 = (f32[3,4,8,48]{3,2,1,0:T(8,128)S(1)}, f32[3,4,8,48]{3,2,1,0:T(8,128)S(1)}, u32[]{:S(2)}, u32[]{:S(2)}) collective-permute-start(f32[3,4,8,48]{3,2,1,0:T(8,128)S(1)} %get-tuple-element.31.refs_0_.refs_5_), channel_id=1, source_target_pairs={{0,16},{4,20},{8,24},{12,28},{16,0},{20,4},{24,8},{28,12},{1,17},{... | collective-permute-start | bytes 55304 | tf_op jit(solution)/shard_map/ppermute | solution.py:24
  55.2 4.1 %collective-permute-start.12 = (f32[3,4,8,48]{3,2,1,0:T(8,128)S(1)}, f32[3,4,8,48]{3,2,1,0:T(8,128)S(1)}, u32[]{:S(2)}, u32[]{:S(2)}) collective-permute-start(f32[3,4,8,48]{3,2,1,0:T(8,128)S(1)} %get-tuple-element.31.refs_0_.refs_5_), channel_id=1, source_target_pairs={{0,8},{4,12},{8,0},{12,4},{16,24},{20,28},{24,16},{28,20},{1,9},{5... | collective-permute-start | bytes 55304 | tf_op jit(solution)/shard_map/ppermute | solution.py:24
  56.7 4.1 %collective-permute-start.11 = (f32[3,4,8,48]{3,2,1,0:T(8,128)S(1)}, f32[3,4,8,48]{3,2,1,0:T(8,128)S(1)}, u32[]{:S(2)}, u32[]{:S(2)}) collective-permute-start(f32[3,4,8,48]{3,2,1,0:T(8,128)S(1)} %get-tuple-element.31.refs_0_.refs_5_), channel_id=1, source_target_pairs={{0,4},{4,0},{8,12},{12,8},{16,20},{20,16},{24,28},{28,24},{1,5},{5... | collective-permute-start | bytes 55304 | tf_op jit(solution)/shard_map/ppermute | solution.py:24
  58.8 9.6 %collective-permute-start.18 = (bf16[4,48,1024]{2,1,0:T(8,128)(2,1)S(1)}, bf16[4,48,1024]{2,1,0:T(8,128)(2,1)S(1)}, u32[]{:S(2)}, u32[]{:S(2)}) collective-permute-start(bf16[4,48,1024]{2,1,0:T(8,128)(2,1)S(1)} %shard_map.89), channel_id=1, source_target_pairs={{0,16},{4,20},{8,24},{12,28},{16,0},{20,4},{24,8},{28,12},{1,17},{... | collective-permute-start | bytes 1179656 | tf_op jit(solution)/shard_map/ppermute | solution.py:24
  59.3 10.3 %collective-permute-start.17 = (bf16[4,48,1024]{2,1,0:T(8,128)(2,1)S(1)}, bf16[4,48,1024]{2,1,0:T(8,128)(2,1)S(1)}, u32[]{:S(2)}, u32[]{:S(2)}) collective-permute-start(bf16[4,48,1024]{2,1,0:T(8,128)(2,1)S(1)} %shard_map.89), channel_id=1, source_target_pairs={{0,8},{4,12},{8,0},{12,4},{16,24},{20,28},{24,16},{28,20},{1,9},{5... | collective-permute-start | bytes 1179656 | tf_op jit(solution)/shard_map/ppermute | solution.py:24
  60.8 8.8 %collective-permute-start.16 = (bf16[4,48,1024]{2,1,0:T(8,128)(2,1)S(1)}, bf16[4,48,1024]{2,1,0:T(8,128)(2,1)S(1)}, u32[]{:S(2)}, u32[]{:S(2)}) collective-permute-start(bf16[4,48,1024]{2,1,0:T(8,128)(2,1)S(1)} %shard_map.89), channel_id=1, source_target_pairs={{0,4},{4,0},{8,12},{12,8},{16,20},{20,16},{24,28},{28,24},{1,5},{5... | collective-permute-start | bytes 1179656 | tf_op jit(solution)/shard_map/ppermute | solution.py:24
  60.8 8.8 %collective-permute-start.19 = (f32[4,4,8,48]{3,2,1,0:T(8,128)S(1)}, f32[4,4,8,48]{3,2,1,0:T(8,128)S(1)}, u32[]{:S(2)}, u32[]{:S(2)}) collective-permute-start(f32[4,4,8,48]{3,2,1,0:T(8,128)S(1)} %get-tuple-element.34), channel_id=1, source_target_pairs={{0,1},{1,0},{2,3},{3,2},{4,5},{5,4},{6,7},{7,6},{8,9},{9,8},{10,11... | collective-permute-start | bytes 73736 | tf_op jit(solution)/shard_map/ppermute | solution.py:35
  62.9 6.7 %collective-permute-start.20 = (f32[4,4,8,48]{3,2,1,0:T(8,128)S(1)}, f32[4,4,8,48]{3,2,1,0:T(8,128)S(1)}, u32[]{:S(2)}, u32[]{:S(2)}) collective-permute-start(f32[4,4,8,48]{3,2,1,0:T(8,128)S(1)} %get-tuple-element.35), channel_id=1, source_target_pairs={{1,2},{2,1},{5,6},{6,5},{9,10},{10,9},{13,14},{14,13},{17,18},{18,... | collective-permute-start | bytes 73736 | tf_op jit(solution)/shard_map/ppermute | solution.py:35
where the time goes:
time: 75.6 us; the launch traced here: 75.3 us
  waiting for transfers between devices  29.6 us (39%)
  starting transfers between devices  21.8 us (29%)
  Pallas kernels  21.2 us (28%)
  local copies, waits for them, and re-layouts  1.93 us (3%)
  between operations  0.76 us (1%)
    ppermute x15, waiting for transfers between devices, swap(): lax.ppermute(value, 'frame', [(i, i ^ 1 << bit) for i in range(size)])  25 us
    pallas_call x9, Pallas kernels, call(): pl.pallas_call(kernel, out_shape=tuple((o if i in to_hbm else pltpu.VMEM(...  21.2 us
    ppermute x6, starting transfers between devices, exchange(): return lax.ppermute(value, 'space', pairs)  11.7 us
    ppermute x15, starting transfers between devices, swap(): lax.ppermute(value, 'frame', [(i, i ^ 1 << bit) for i in range(size)])  10.1 us
    ppermute x6, waiting for transfers between devices, exchange(): return lax.ppermute(value, 'space', pairs)  4.63 us
    unnamed x10, local copies, waits for them, and re-layouts  1.93 us
  transfers between devices with their start and end apart: 21, of which 8 were waited for; matrix products, arithmetic and copies ran while one was open for 0% of the time, Pallas kernels for 20%

commit v1 on v0

--- a/solution.py
+++ b/solution.py
@@ -148,7 +148,7 @@
     return (other >= 0) & (other < size)
 
 
-def build_masks(mask_ref, kinds, blocks, frames, tokens, table, queries_here):
+def build_masks(mask_ref, blocks, frames, tokens, table, queries_here):
     shape = (8, blocks * tokens)
     lane = lax.broadcasted_iota(jnp.int32, shape, 1)
     sub = lax.broadcasted_iota(jnp.int32, shape, 0)
@@ -163,11 +163,10 @@
         for frame in range(frames):
             off = jnp.where(table[block - 1, owner * frames + frame] == 1, 0.0, bad)
             value = jnp.where((group == block) & (which == frame), off.astype(F32), value)
-    for slot, kind in enumerate(kinds):
-        first = value
-        if not isinstance(kind, int):
-            first = value + jnp.where(rim_open(int(kind)), 0.0, bad).astype(F32)
-        mask_ref[slot] = jnp.concatenate([first, value, value], axis=1)
+    mask_ref[0] = value
+    if queries_here:
+        for side in range(2):
+            mask_ref[1 + side] = value + jnp.where(rim_open(side), 0.0, bad).astype(F32)
 
 
 def forward_kernel(layout, kinds, carried, *refs):
@@ -187,7 +186,7 @@
                 target[row] = source[at]
         for at in range(len(carried)):
             stats[at] = refs[n_in - 1][at]
-    build_masks(mask, kinds, count, frames, tokens, table, True)
+    build_masks(mask, count, frames, tokens, table, True)
     lane_head = lax.broadcasted_iota(jnp.int32, (tokens, PAIR), 1) // HEAD_DIM
     lane = lax.broadcasted_iota(jnp.int32, (2 * tokens, 128), 1)
     slot_of = lambda row: row if carried else row - 1
@@ -204,7 +203,9 @@
         tops, totals = [], []
         for unit, (slot, pair) in enumerate(units):
             top_parts, total_parts = [], []
-            bias = jnp.concatenate([mask[slot]] * (CHUNK // 8), axis=0)
+            first = mask[0] if isinstance(kinds[slot], int) else mask[1 + int(kinds[slot])]
+            bias = jnp.concatenate([first, mask[0], mask[0]], axis=1)
+            bias = jnp.concatenate([bias] * (CHUNK // 8), axis=0)
             for start in range(0, 2 * tokens, CHUNK):
                 scores = s_scr[unit, start : start + CHUNK, :] + bias
                 top = jnp.max(scores, axis=1, keepdims=True)
@@ -252,79 +253,105 @@
     lax.fori_loop(0, width // PART, step, 0)
 
 
-def backward_kernel(layout, kinds, carried, *refs):
-    kv = refs[layout["own"]]
+def backward_kernel(layout, kinds, *refs):
+    n_in, count = layout["n_in"], layout["count"]
+    kv = refs[0]
+    qgs, stats_of = refs[1 : 1 + count], refs[1 + count : 1 + 2 * count]
+    rims = refs[1 + 2 * count : n_in]
+    table, *outs = refs[n_in:-5]
+    mask, s_scr, d_scr, p_scr, t_scr = refs[-5:]
     rows = kv.shape[0] // 2
-    queries, grads = (Pieces(refs, rows, *layout[name]) for name in ("q", "g"))
-    n_in = layout["n_in"]
-    table = refs[n_in]
-    dk, dv = refs[n_in + 1 :][:2]
-    mask, s_scr, d_scr, p_scr, t_scr = refs[-5:]
     tokens, width = kv.shape[1:]
-    columns, frames = dk.shape[1:3]
-    count = len(queries.mids)
-    for target, source in zip((dk, dv), refs[n_in - 2 : n_in]):
-        for at, row in enumerate(carried):
-            target[row] = source[at]
-    build_masks(mask, kinds, count, frames, tokens, table, False)
+    part = count * tokens
+    build_masks(mask, count, layout["frames"], tokens, table, False)
     lane_head = lax.broadcasted_iota(jnp.int32, (tokens, PAIR), 1) // HEAD_DIM
-    slot_of = lambda row: row if carried else row - 1
-    units = [(slot, pair) for slot in range(len(kinds)) for pair in range(PAIRS)]
-
-    def stat_window(kind, group):
-        out = []
-        mids, rim = layout["s"]
+    units = [(kind, pair) for kind in kinds for pair in range(PAIRS)]
+
+    def query_rows(kind):
         inner = rows - 2
-
-        def stat_at(block, row):
-            if isinstance(row, int) and 0 < row < rows - 1:
-                return refs[mids[block]][row - 1, group]
+        if isinstance(kind, int):
             first, _ = edge_rows(rows)
-            return refs[mids[block]][jnp.where(first == row, inner, inner + 1), group]
-
-        for at in range(3):
-            for block in range(count):
-                if isinstance(kind, int):
-                    out.append(stat_at(block, kind - 1 + at))
-                elif at == 0:
-                    index, slot = rim[int(kind)][block]
-                    out.append(refs[index][slot, group])
-                elif at == 1:
-                    out.append(refs[mids[block]][inner + int(kind), group])
+            out = []
+            for row in (kind - 1, kind, kind + 1):
+                if 0 < row < rows - 1:
+                    out.append((row, row - 1))
                 else:
-                    place = edge_rows(rows)[int(kind)]
-                    out.append(refs[mids[block]][jnp.where(place == 0, 1, place - 1) - 1, group])
-        return jnp.concatenate(out, axis=1)
+                    out.append((row, jnp.where(first == row, inner, inner + 1)))
+            return out
+        side = int(kind[-1])
+        edge = edge_rows(rows)[side]
+        if kind[0] == "r":
+            return [(edge, inner + side)]
+        near = jnp.where(edge == 0, 1, edge - 1)
+        return [(edge, inner + side), (near, near - 1)]
+
+    def key_rows(kind, tensor, lanes):
+        if isinstance(kind, int):
+            return kv[tensor * rows + kind, :, lanes]
+        side = int(kind[-1])
+        if kind[0] == "r":
+            return rims[side][tensor, :, lanes]
+        return kv[tensor * rows + edge_rows(rows)[side], :, lanes]
+
+    def window(kind, tensor, lanes):
+        found = [qg[tensor * rows + row, :, lanes] for row, _ in query_rows(kind) for qg in qgs]
+        return jnp.concatenate(found, axis=0)
 
     def step(group, _):
         lanes_of = [pl.ds(pl.multiple_of(group * PART + pair * PAIR, PAIR), PAIR) for pair in range(PAIRS)]
-        for unit, (slot, pair) in enumerate(units):
-            lanes, kind = lanes_of[pair], kinds[slot]
-            row = row_of(kind, rows)
-            s_scr[unit] = nt(head_rows(kv[row, :, lanes] * SCALE, lane_head), queries.window(kind, lanes))
-            d_scr[unit] = nt(head_rows(kv[rows + row, :, lanes], lane_head), grads.window(kind, lanes))
-        stats = [stat_window(kind, group) for kind in kinds]
-        for unit, (slot, pair) in enumerate(units):
-            stat = stats[slot]
+        for unit, (kind, pair) in enumerate(units):
+            lanes = lanes_of[pair]
+            size = len(query_rows(kind)) * part
+            s_scr[unit, :, :size] = nt(
+                head_rows(key_rows(kind, 0, lanes) * SCALE, lane_head), window(kind, 0, lanes)
+            )
+            d_scr[unit, :, :size] = nt(
+                head_rows(key_rows(kind, 1, lanes), lane_head), window(kind, 1, lanes)
+            )
+        stats = {
+            kind: jnp.concatenate(
+                [ref[slot, group] for _, slot in query_rows(kind) for ref in stats_of], axis=1
+            )
+            for kind in kinds
+        }
+        for unit, (kind, pair) in enumerate(units):
+            stat = stats[kind]
+            size = stat.shape[1]
+            bias = jnp.concatenate([mask[0, 0:1]] * (size // part), axis=1)
             for h in range(2):
                 at = pair * 2 + h
-                lse = stat[at : at + 1] + mask[slot, 0:1]
+                lse = stat[at : at + 1] + bias
                 delta = stat[2 * PAIRS + at : 2 * PAIRS + at + 1]
                 for start in range(h * tokens, (h + 1) * tokens, CHUNK):
-                    part = slice(start, start + CHUNK)
-                    probs = jnp.exp(s_scr[unit, part, :] - lse)
-                    p_scr[unit, part, :] = probs.astype(BF16)
-                    t_scr[unit, part, :] = (probs * (d_scr[unit, part, :] - delta)).astype(BF16)
-        for unit, (slot, pair) in enumerate(units):
-            lanes, kind = lanes_of[pair], kinds[slot]
-            row = row_of(kind, rows)
-            grad_v = head_lanes(nn(p_scr[unit], grads.window(kind, lanes)), lane_head).astype(BF16)
-            dv[slot_of(row), :, :, lanes] = grad_v.reshape(columns, frames, PAIR)
-            grad_k = head_lanes(nn(t_scr[unit], queries.window(kind, lanes)), lane_head) * SCALE
-            dk[slot_of(row), :, :, lanes] = grad_k.astype(BF16).reshape(columns, frames, PAIR)
+                    rows_at = slice(start, start + CHUNK)
+                    probs = jnp.exp(s_scr[unit, rows_at, :size] - lse)
+                    p_scr[unit, rows_at, :size] = probs.astype(BF16)
+                    grad_scores = probs * (d_scr[unit, rows_at, :size] - delta)
+                    t_scr[unit, rows_at, :size] = grad_scores.astype(BF16)
+        for unit, (kind, pair) in enumerate(units):
+            lanes = lanes_of[pair]
+            size = len(query_rows(kind)) * part
+            grad_v = head_lanes(nn(p_scr[unit, :, :size], window(kind, 1, lanes)), lane_head)
+            grad_k = head_lanes(nn(t_scr[unit, :, :size], window(kind, 0, lanes)), lane_head) * SCALE
+            for tensor, value in enumerate((grad_k, grad_v)):
+                if isinstance(kind, str) and kind[0] == "r":
+                    outs[int(kind[-1])][tensor, :, lanes] = value.astype(BF16)
+                else:
+                    row = row_of(kind, rows)
+                    outs[0][tensor * rows + row, :, lanes] = value
         return 0
 
     lax.fori_loop(0, width // PART, step, 0)
+
+
+def finish_kernel(total, part0, part1, dk, dv):
+    rows, columns, frames, width = dk.shape
+    for tensor, out in enumerate((dk, dv)):
+        for row in range(1, rows - 1):
+            out[row] = total[tensor * rows + row].astype(BF16).reshape(columns, frames, width)
+        for part, row in zip((part0, part1), edge_rows(rows)):
+            value = total[tensor * rows + row] + part[tensor].astype(F32)
+            out[row] = value.astype(BF16).reshape(columns, frames, width)
 
 
 def per_device(query_vectors, key_vectors, value_vectors, out_cotangent, partner_mask):
@@ -342,10 +369,8 @@
     kvs = [kv] + swaps(kv, bits)
     kv_rims = [exchange(kv_edge0, 0), exchange(kv_edge1, 1)]
     kv_rims_of = swaps(join(kv_rims), bits)
-    qg, qg_edge0, qg_edge1 = pack([turn(query_vectors), turn(out_cotangent)], [kv_edge0])
-    qg_rims = [exchange(qg_edge0, 0), exchange(qg_edge1, 1)]
+    qg, _, _ = pack([turn(query_vectors), turn(out_cotangent)], [kv_edge0])
     qgs = [qg] + swaps(qg, bits)
-    qg_rims_of = swaps(join(qg_rims), bits)
 
     inner_kinds = list(range(1, rows - 1))
     edge_kinds = ["0", "1"]
@@ -356,7 +381,7 @@
 
     def scratches(n, extra):
         units = n * PAIRS
-        wide = [pltpu.VMEM((n, 8, window), F32)]
+        wide = [pltpu.VMEM((3, 8, count * tokens), F32)]
         wide += [pltpu.VMEM((units, 2 * tokens, window), F32)] * 2
         return wide + [pltpu.VMEM((units, 2 * tokens, window), BF16)] * extra
 
@@ -388,31 +413,22 @@
     )
     ss = [stats] + swaps(stats, bits)
 
-    def stat_edge_kernel(*refs):
-        for slot, source in enumerate(refs[:-2]):
-            for side in range(2):
-                refs[len(refs) - 2 + side][slot] = source[inner + side]
-
-    s_rims = call(stat_edge_kernel, [stat(count)] * 2, ss)
-    s_rims = [exchange(edge, side) for side, edge in enumerate(s_rims)]
-
-    ins = [kv] + qgs + ss
-    mids = range(1 + count, 1 + 2 * count)
-    layout = {"n_in": len(ins), "own": 0, "q": gathered(1, None, 0), "g": gathered(1, None, 1), "s": (mids, None)}
-    inner_out = call(
-        functools.partial(backward_kernel, layout, inner_kinds, ()),
-        [line(inner), line(inner)], ins,
-        flops=work * inner, exps=exps * inner, scratch=scratches(inner, 2), limit=10 << 20, table=table,
-    )
-    rim_at = len(ins)
-    ins = ins + qg_rims + qg_rims_of + s_rims + list(inner_out)
-    rim = [[(rim_at + 2 + bits + side, block) for block in range(count)] for side in range(2)]
-    layout = {"n_in": len(ins), "own": 0, "q": gathered(1, rim_at, 0), "g": gathered(1, rim_at, 1), "s": (mids, rim)}
-    dk, dv = call(
-        functools.partial(backward_kernel, layout, edge_kinds, inner_kinds),
-        [line(rows), line(rows)], ins, to_hbm=(0, 1),
-        flops=work * 2, exps=exps * 2, scratch=scratches(2, 2), limit=10 << 20, table=table,
-    )
+    ins = [kv] + qgs + ss + kv_rims
+    layout = {"n_in": len(ins), "count": count, "frames": frames}
+    edge = struct(2, tokens, width)
+    parts = call(
+        functools.partial(backward_kernel, layout, ["r0", "r1"]),
+        [edge, edge], ins,
+        flops=work, exps=exps, scratch=scratches(2, 2), limit=10 << 20, table=table,
+    )
+    parts = [exchange(value, side) for side, value in enumerate(parts)]
+    (total,) = call(
+        functools.partial(backward_kernel, layout, inner_kinds + edge_kinds),
+        [struct(2 * rows, tokens, width, dtype=F32)], ins,
+        flops=2 * work, exps=2 * exps, scratch=scratches(rows, 2), limit=12 << 20, table=table,
+    )
+    full = struct(rows, columns, frames, width)
+    dk, dv = call(finish_kernel, [full, full], [total] + parts, to_hbm=(0, 1))
     return back(attended), back(dq), back(dk), back(dv)
 
 

time: 75.6 us -> 78.4 us (1.037)
  waiting for transfers between devices: 29.6 us -> 34.9 us
  starting transfers between devices: 21.8 us -> 18.3 us
  Pallas kernels: 21.2 us -> 22.2 us
    ppermute x15 -> x12, waiting for transfers between devices: 25 us -> 33.3 us  [swap(): lax.ppermute(value, 'frame', [(i, i ^ 1 << bit) for i in range(size)])]
    ppermute x6 -> x4, starting transfers between devices: 11.7 us -> 7.97 us  [exchange(): return lax.ppermute(value, 'space', pairs)]
    ppermute x6 -> x4, waiting for transfers between devices: 4.63 us -> 1.61 us  [exchange(): return lax.ppermute(value, 'space', pairs)]
    pallas_call x9 -> x8, Pallas kernels: 21.2 us -> 22.2 us  [call(): pl.pallas_call(kernel, out_shape=tuple((o if i in to_hbm else pltpu.VMEM(...]
    ppermute x15 -> x12, starting transfers between devices: 10.1 us -> 10.4 us  [swap(): lax.ppermute(value, 'frame', [(i, i ^ 1 << bit) for i in range(size)])]
  transfers between devices with their start and end apart: 21 -> 16, of which waited for: 8 -> 5; matrix products, arithmetic and copies ran while one was open for 0% -> 0% of each run, Pallas kernels for 20% -> 23%
where the time goes in v1:
time: 78.4 us; the launch traced here: 78.2 us
  waiting for transfers between devices  34.9 us (45%)
  Pallas kernels  22.2 us (28%)
  starting transfers between devices  18.3 us (23%)
  local copies, waits for them, and re-layouts  1.99 us (3%)
    ppermute x12, waiting for transfers between devices, swap(): lax.ppermute(value, 'frame', [(i, i ^ 1 << bit) for i in range(size)])  33.3 us
    pallas_call x8, Pallas kernels, call(): pl.pallas_call(kernel, out_shape=tuple((o if i in to_hbm else pltpu.VMEM(...  22.2 us
    ppermute x12, starting transfers between devices, swap(): lax.ppermute(value, 'frame', [(i, i ^ 1 << bit) for i in range(size)])  10.4 us
    ppermute x4, starting transfers between devices, exchange(): return lax.ppermute(value, 'space', pairs)  7.97 us
    unnamed x10, local copies, waits for them, and re-layouts  1.99 us
    ppermute x4, waiting for transfers between devices, exchange(): return lax.ppermute(value, 'space', pairs)  1.61 us
  transfers between devices with their start and end apart: 16, of which 5 were waited for; matrix products, arithmetic and copies ran while one was open for 0% of the time, Pallas kernels for 23%

profile of v1, /device:TPU:0, one launch (start us, length us, event | category | flops | bytes accessed | tf_op | source)
XLA Modules:
  0.0 78.2 jit_solution(15788845778812019240)
XLA Ops:
  0.6 0.0 copy-start.1
  0.6 0.0 copy-start
  0.7 0.0 copy-start.2
  0.7 1.0 %copy-done.2 = bf16[4,3,12,1024]{3,0,2,1:T(4,128)(2,1)S(1)} copy-done((bf16[4,3,12,1024]{3,0,2,1:T(4,128)(2,1)S(1)}, bf16[4,3,12,1024]{3,0,2,1:T(4,128)(2,1)}, u32[]{:S(2)}) %copy-start.2) | copy-done | bytes 294936
  1.7 0.0 copy-start.3
  1.7 1.0 %copy-done.3 = bf16[4,3,12,1024]{3,0,2,1:T(4,128)(2,1)S(1)} copy-done((bf16[4,3,12,1024]{3,0,2,1:T(4,128)(2,1)S(1)}, bf16[4,3,12,1024]{3,0,2,1:T(4,128)(2,1)}, u32[]{:S(2)}) %copy-start.3) | copy-done | bytes 294936
  2.6 0.0 copy-start.4
  2.6 0.1 shard_map.84
  2.8 0.7 collective-permute-start.4
  3.4 5.9 %collective-permute-start.3 = (bf16[2,48,1024]{2,1,0:T(8,128)(2,1)S(1)}, bf16[2,48,1024]{2,1,0:T(8,128)(2,1)S(1)}, u32[]{:S(2)}, u32[]{:S(2)}) collective-permute-start(bf16[2,48,1024]{2,1,0:T(8,128)(2,1)S(1)} %get-tuple-element.18.refs_2_), channel_id=1, source_target_pairs={{0,1},{1,0},{2,3},{3,2},{4,5},{5,4},{6,7},{7,6},{8,9},{9,8},{10,11... | collective-permute-start | bytes 589832 | tf_op jit(solution)/shard_map/ppermute | solution.py:35
  9.4 1.5 %collective-permute-start.2 = (bf16[6,48,1024]{2,1,0:T(8,128)(2,1)S(1)}, bf16[6,48,1024]{2,1,0:T(8,128)(2,1)S(1)}, u32[]{:S(2)}, u32[]{:S(2)}) collective-permute-start(bf16[6,48,1024]{2,1,0:T(8,128)(2,1)S(1)} %get-tuple-element.20.refs_1_.refs_0_), channel_id=1, source_target_pairs={{0,16},{4,20},{8,24},{12,28},{16,0},{20,4},{24,8},{28,12},{1,17},{... | collective-permute-start | bytes 1769480 | tf_op jit(solution)/shard_map/ppermute | solution.py:24
  10.9 1.5 %collective-permute-start.1 = (bf16[6,48,1024]{2,1,0:T(8,128)(2,1)S(1)}, bf16[6,48,1024]{2,1,0:T(8,128)(2,1)S(1)}, u32[]{:S(2)}, u32[]{:S(2)}) collective-permute-start(bf16[6,48,1024]{2,1,0:T(8,128)(2,1)S(1)} %get-tuple-element.20.refs_1_.refs_0_), channel_id=1, source_target_pairs={{0,8},{4,12},{8,0},{12,4},{16,24},{20,28},{24,16},{28,20},{1,9},{5... | collective-permute-start | bytes 1769480 | tf_op jit(solution)/shard_map/ppermute | solution.py:24
  12.4 0.0 collective-permute-start
  12.4 0.0 collective-permute-done.4.refs_1_.refs_6_.refs_10_
  12.4 1.6 %collective-permute-done.3.refs_0_.refs_5_.refs_9_ = bf16[2,48,1024]{2,1,0:T(8,128)(2,1)S(1)} collective-permute-done((bf16[2,48,1024]{2,1,0:T(8,128)(2,1)S(1)}, bf16[2,48,1024]{2,1,0:T(8,128)(2,1)S(1)}, u32[]{:S(2)}, u32[]{:S(2)}) %collective-permute-start.3) | collective-permute-done | bytes 196640 | tf_op jit(solution)/shard_map/ppermute | solution.py:35
  14.0 1.6 %collective-permute-start.7 = (bf16[4,48,1024]{2,1,0:T(8,128)(2,1)S(1)}, bf16[4,48,1024]{2,1,0:T(8,128)(2,1)S(1)}, u32[]{:S(2)}, u32[]{:S(2)}) collective-permute-start(bf16[4,48,1024]{2,1,0:T(8,128)(2,1)S(1)} %shard_map.86), channel_id=1, source_target_pairs={{0,16},{4,20},{8,24},{12,28},{16,0},{20,4},{24,8},{28,12},{1,17},{... | collective-permute-start | bytes 1179656 | tf_op jit(solution)/shard_map/ppermute | solution.py:24
  15.6 0.0 copy-done.1
  15.6 0.0 copy-done
  15.6 0.9 %shard_map.85 = (bf16[6,48,1024]{2,1,0:T(8,128)(2,1)S(1)}, bf16[2,48,1024]{2,1,0:T(8,128)(2,1)}, bf16[2,48,1024]{2,1,0:T(8,128)(2,1)}) custom-call(bf16[3,12,4,1024]{3,2,1,0:T(4,128)(2,1)S(1)} %bitcast.9, bf16[3,12,4,1024]{3,2,1,0:T(4,128)(2,1)S(1)} %bitcast.10, bf16[2,48,1024]{2,1,0:T(8,128)(2,1)S(1)} %get-tuple-element.18.refs_2_), custom_call_target="tpu_custom_call" | custom-call | bytes 1769472 | tf_op jit(solution)/shard_map/pallas_call | solution.py:51
  16.5 0.5 collective-permute-start.10
  17.0 17.0 %collective-permute-done.7.refs_9_ = bf16[4,48,1024]{2,1,0:T(8,128)(2,1)S(1)} collective-permute-done((bf16[4,48,1024]{2,1,0:T(8,128)(2,1)S(1)}, bf16[4,48,1024]{2,1,0:T(8,128)(2,1)S(1)}, u32[]{:S(2)}, u32[]{:S(2)}) %collective-permute-start.7) | collective-permute-done | bytes 393248 | tf_op jit(solution)/shard_map/ppermute | solution.py:24
  34.0 1.5 %collective-permute-start.9 = (bf16[6,48,1024]{2,1,0:T(8,128)(2,1)S(1)}, bf16[6,48,1024]{2,1,0:T(8,128)(2,1)S(1)}, u32[]{:S(2)}, u32[]{:S(2)}) collective-permute-start(bf16[6,48,1024]{2,1,0:T(8,128)(2,1)S(1)} %get-tuple-element.19.refs_0_.refs_1_), channel_id=1, source_target_pairs={{0,8},{4,12},{8,0},{12,4},{16,24},{20,28},{24,16},{28,20},{1,9},{5... | collective-permute-start | bytes 1769480 | tf_op jit(solution)/shard_map/ppermute | solution.py:24
  35.5 0.0 collective-permute-done.2.refs_4_
  35.5 0.0 collective-permute-start.8
  35.5 0.0 collective-permute-done.1.refs_3_
  35.5 0.6 collective-permute-start.6
  36.1 0.0 collective-permute-done.refs_2_
  36.1 0.2 collective-permute-start.5
  36.3 0.0 copy-done.4
  36.3 4.4 %shard_map.87 = (bf16[1,12,4,1024]{3,2,1,0:T(4,128)(2,1)S(1)}, bf16[1,12,4,1024]{3,2,1,0:T(4,128)(2,1)S(1)}, f32[1,4,8,48]{3,2,1,0:T(8,128)S(1)}) custom-call(bf16[6,48,1024]{2,1,0:T(8,128)(2,1)S(1)} %get-tuple-element.19.refs_0_.refs_1_, bf16[6,48,1024]{2,1,0:T(8,128)(2,1)S(1)} %get-tuple-element.20.refs_1_.refs_0_, ...), custom_call_target="tpu_custom_call" | custom-call | flops 452984832 | bytes 3151872 | tf_op jit(solution)/shard_map/pallas_call | solution.py:51
  40.7 13.7 %collective-permute-done.6.refs_8_ = bf16[4,48,1024]{2,1,0:T(8,128)(2,1)S(1)} collective-permute-done((bf16[4,48,1024]{2,1,0:T(8,128)(2,1)S(1)}, bf16[4,48,1024]{2,1,0:T(8,128)(2,1)S(1)}, u32[]{:S(2)}, u32[]{:S(2)}) %collective-permute-start.6) | collective-permute-done | bytes 393248 | tf_op jit(solution)/shard_map/ppermute | solution.py:24
  54.4 0.0 collective-permute-done.5.refs_7_
  54.4 7.5 %shard_map.88 = (bf16[3,12,4,1024]{3,2,1,0:T(4,128)(2,1)}, bf16[3,12,4,1024]{3,2,1,0:T(4,128)(2,1)}, f32[3,4,8,48]{3,2,1,0:T(8,128)S(1)}) custom-call(bf16[6,48,1024]{2,1,0:T(8,128)(2,1)S(1)} %get-tuple-element.19.refs_0_.refs_1_, bf16[6,48,1024]{2,1,0:T(8,128)(2,1)S(1)} %get-tuple-element.20.refs_1_.refs_0_, ...), custom_call_target="tpu_custom_call" | custom-call | flops 905969664 | bytes 5332992 | tf_op jit(solution)/shard_map/pallas_call | solution.py:51
  61.8 1.5 %collective-permute-start.13 = (f32[3,4,8,48]{3,2,1,0:T(8,128)S(1)}, f32[3,4,8,48]{3,2,1,0:T(8,128)S(1)}, u32[]{:S(2)}, u32[]{:S(2)}) collective-permute-start(f32[3,4,8,48]{3,2,1,0:T(8,128)S(1)} %get-tuple-element.27.refs_5_), channel_id=1, source_target_pairs={{0,16},{4,20},{8,24},{12,28},{16,0},{20,4},{24,8},{28,12},{1,17},{... | collective-permute-start | bytes 55304 | tf_op jit(solution)/shard_map/ppermute | solution.py:24
  63.4 1.5 %collective-permute-start.12 = (f32[3,4,8,48]{3,2,1,0:T(8,128)S(1)}, f32[3,4,8,48]{3,2,1,0:T(8,128)S(1)}, u32[]{:S(2)}, u32[]{:S(2)}) collective-permute-start(f32[3,4,8,48]{3,2,1,0:T(8,128)S(1)} %get-tuple-element.27.refs_5_), channel_id=1, source_target_pairs={{0,8},{4,12},{8,0},{12,4},{16,24},{20,28},{24,16},{28,20},{1,9},{5... | collective-permute-start | bytes 55304 | tf_op jit(solution)/shard_map/ppermute | solution.py:24
  64.8 0.0 collective-permute-done.10.refs_4_
  64.8 0.0 collective-permute-start.11
  64.8 0.0 collective-permute-done.9.refs_3_
  64.9 0.0 collective-permute-done.8.refs_2_
  64.9 1.1 %collective-permute-done.13.refs_8_ = f32[3,4,8,48]{3,2,1,0:T(8,128)S(1)} collective-permute-done((f32[3,4,8,48]{3,2,1,0:T(8,128)S(1)}, f32[3,4,8,48]{3,2,1,0:T(8,128)S(1)}, u32[]{:S(2)}, u32[]{:S(2)}) %collective-permute-start.13) | collective-permute-done | bytes 18464 | tf_op jit(solution)/shard_map/ppermute | solution.py:24
  65.9 1.5 %collective-permute-done.12.refs_7_ = f32[3,4,8,48]{3,2,1,0:T(8,128)S(1)} collective-permute-done((f32[3,4,8,48]{3,2,1,0:T(8,128)S(1)}, f32[3,4,8,48]{3,2,1,0:T(8,128)S(1)}, u32[]{:S(2)}, u32[]{:S(2)}) %collective-permute-start.12) | collective-permute-done | bytes 18464 | tf_op jit(solution)/shard_map/ppermute | solution.py:24
  67.4 0.0 collective-permute-done.11.refs_6_
  67.5 3.0 %shard_map.90 = (bf16[2,48,1024]{2,1,0:T(8,128)(2,1)S(1)}, bf16[2,48,1024]{2,1,0:T(8,128)(2,1)S(1)}) custom-call(bf16[6,48,1024]{2,1,0:T(8,128)(2,1)S(1)} %get-tuple-element.20.refs_1_.refs_0_, bf16[6,48,1024]{2,1,0:T(8,128)(2,1)S(1)} %get-tuple-element.19.refs_0_.refs_1_, bf16[6,48,1024]{2,1,0:T(8,128)(2,1)S(1)} %collective-permute-done.8.refs_2_, ...), custom_call_target="tpu_custom_call" | custom-call | flops 452984832 | bytes 3809280 | tf_op jit(solution)/shard_map/pallas_call | solution.py:51
  70.5 0.7 collective-permute-start.14
  71.2 0.7 collective-permute-start.15
  71.8 5.4 %shard_map.89.total = f32[6,48,1024]{2,1,0:T(8,128)S(1)} custom-call(bf16[6,48,1024]{2,1,0:T(8,128)(2,1)S(1)} %get-tuple-element.20.refs_1_.refs_0_, bf16[6,48,1024]{2,1,0:T(8,128)(2,1)S(1)} %get-tuple-element.19.refs_0_.refs_1_, bf16[6,48,1024]{2,1,0:T(8,128)(2,1)S(1)} %collective-permute-done.8.refs_2_, ...), custom_call_target="tpu_custom_call" | custom-call | flops 905969664 | bytes 4595712 | tf_op jit(solution)/shard_map/pallas_call | solution.py:51
  77.2 0.0 collective-permute-done.14.part0
  77.3 0.0 collective-permute-done.15.part1
  77.3 0.9 %shard_map.91 = (bf16[3,12,4,1024]{3,2,1,0:T(4,128)(2,1)}, bf16[3,12,4,1024]{3,2,1,0:T(4,128)(2,1)}) custom-call(f32[6,48,1024]{2,1,0:T(8,128)S(1)} %shard_map.89.total, bf16[2,48,1024]{2,1,0:T(8,128)(2,1)S(1)} %collective-permute-done.14.part0, bf16[2,48,1024]{2,1,0:T(8,128)(2,1)S(1)} %collective-permute-done.15.part1), custom_call_target="tpu_custom_call" | custom-call | bytes 2162688 | tf_op jit(solution)/shard_map/pallas_call | solution.py:51
  (1 shorter events, 0.0 us)
Async XLA Ops:
  0.6 15.0 %copy-start.1 = (bf16[4,3,12,1024]{3,0,2,1:T(4,128)(2,1)S(1)}, bf16[4,3,12,1024]{3,0,2,1:T(4,128)(2,1)}, u32[]{:S(2)}) copy-start(bf16[4,3,12,1024]{3,0,2,1:T(4,128)(2,1)} %param.8) | copy-start | bytes 884740
  0.6 15.0 %copy-start = (bf16[4,3,12,1024]{3,0,2,1:T(4,128)(2,1)S(1)}, bf16[4,3,12,1024]{3,0,2,1:T(4,128)(2,1)}, u32[]{:S(2)}) copy-start(bf16[4,3,12,1024]{3,0,2,1:T(4,128)(2,1)} %param.5) | copy-start | bytes 884740
  0.7 1.0 %copy-start.2 = (bf16[4,3,12,1024]{3,0,2,1:T(4,128)(2,1)S(1)}, bf16[4,3,12,1024]{3,0,2,1:T(4,128)(2,1)}, u32[]{:S(2)}) copy-start(bf16[4,3,12,1024]{3,0,2,1:T(4,128)(2,1)} %param.6) | copy-start | bytes 884740
  1.7 1.0 %copy-start.3 = (bf16[4,3,12,1024]{3,0,2,1:T(4,128)(2,1)S(1)}, bf16[4,3,12,1024]{3,0,2,1:T(4,128)(2,1)}, u32[]{:S(2)}) copy-start(bf16[4,3,12,1024]{3,0,2,1:T(4,128)(2,1)} %param.7) | copy-start | bytes 884740
  2.6 33.6 %copy-start.4 = (s32[32,3]{0,1:T(4,128)S(1)}, s32[32,3]{0,1:T(4,128)}, u32[]{:S(2)}) copy-start(s32[32,3]{0,1:T(4,128)} %param.9) | copy-start | bytes 1156
  2.8 9.6 %collective-permute-start.4 = (bf16[2,48,1024]{2,1,0:T(8,128)(2,1)S(1)}, bf16[2,48,1024]{2,1,0:T(8,128)(2,1)S(1)}, u32[]{:S(2)}, u32[]{:S(2)}) collective-permute-start(bf16[2,48,1024]{2,1,0:T(8,128)(2,1)S(1)} %get-tuple-element.21), channel_id=1, source_target_pairs={{1,2},{2,1},{5,6},{6,5},{9,10},{10,9},{13,14},{14,13},{17,18},{18,... | collective-permute-start | bytes 589832 | tf_op jit(solution)/shard_map/ppermute | solution.py:35
  3.4 10.6 %collective-permute-start.3 = (bf16[2,48,1024]{2,1,0:T(8,128)(2,1)S(1)}, bf16[2,48,1024]{2,1,0:T(8,128)(2,1)S(1)}, u32[]{:S(2)}, u32[]{:S(2)}) collective-permute-start(bf16[2,48,1024]{2,1,0:T(8,128)(2,1)S(1)} %get-tuple-element.18.refs_2_), channel_id=1, source_target_pairs={{0,1},{1,0},{2,3},{3,2},{4,5},{5,4},{6,7},{7,6},{8,9},{9,8},{10,11... | collective-permute-start | bytes 589832 | tf_op jit(solution)/shard_map/ppermute | solution.py:35
  9.4 26.1 %collective-permute-start.2 = (bf16[6,48,1024]{2,1,0:T(8,128)(2,1)S(1)}, bf16[6,48,1024]{2,1,0:T(8,128)(2,1)S(1)}, u32[]{:S(2)}, u32[]{:S(2)}) collective-permute-start(bf16[6,48,1024]{2,1,0:T(8,128)(2,1)S(1)} %get-tuple-element.20.refs_1_.refs_0_), channel_id=1, source_target_pairs={{0,16},{4,20},{8,24},{12,28},{16,0},{20,4},{24,8},{28,12},{1,17},{... | collective-permute-start | bytes 1769480 | tf_op jit(solution)/shard_map/ppermute | solution.py:24
  10.9 24.6 %collective-permute-start.1 = (bf16[6,48,1024]{2,1,0:T(8,128)(2,1)S(1)}, bf16[6,48,1024]{2,1,0:T(8,128)(2,1)S(1)}, u32[]{:S(2)}, u32[]{:S(2)}) collective-permute-start(bf16[6,48,1024]{2,1,0:T(8,128)(2,1)S(1)} %get-tuple-element.20.refs_1_.refs_0_), channel_id=1, source_target_pairs={{0,8},{4,12},{8,0},{12,4},{16,24},{20,28},{24,16},{28,20},{1,9},{5... | collective-permute-start | bytes 1769480 | tf_op jit(solution)/shard_map/ppermute | solution.py:24
  12.4 23.7 %collective-permute-start = (bf16[6,48,1024]{2,1,0:T(8,128)(2,1)S(1)}, bf16[6,48,1024]{2,1,0:T(8,128)(2,1)S(1)}, u32[]{:S(2)}, u32[]{:S(2)}) collective-permute-start(bf16[6,48,1024]{2,1,0:T(8,128)(2,1)S(1)} %get-tuple-element.20.refs_1_.refs_0_), channel_id=1, source_target_pairs={{0,4},{4,0},{8,12},{12,8},{16,20},{20,16},{24,28},{28,24},{1,5},{5... | collective-permute-start | bytes 1769480 | tf_op jit(solution)/shard_map/ppermute | solution.py:24
  14.0 20.0 %collective-permute-start.7 = (bf16[4,48,1024]{2,1,0:T(8,128)(2,1)S(1)}, bf16[4,48,1024]{2,1,0:T(8,128)(2,1)S(1)}, u32[]{:S(2)}, u32[]{:S(2)}) collective-permute-start(bf16[4,48,1024]{2,1,0:T(8,128)(2,1)S(1)} %shard_map.86), channel_id=1, source_target_pairs={{0,16},{4,20},{8,24},{12,28},{16,0},{20,4},{24,8},{28,12},{1,17},{... | collective-permute-start | bytes 1179656 | tf_op jit(solution)/shard_map/ppermute | solution.py:24
  16.5 48.4 %collective-permute-start.10 = (bf16[6,48,1024]{2,1,0:T(8,128)(2,1)S(1)}, bf16[6,48,1024]{2,1,0:T(8,128)(2,1)S(1)}, u32[]{:S(2)}, u32[]{:S(2)}) collective-permute-start(bf16[6,48,1024]{2,1,0:T(8,128)(2,1)S(1)} %get-tuple-element.19.refs_0_.refs_1_), channel_id=1, source_target_pairs={{0,16},{4,20},{8,24},{12,28},{16,0},{20,4},{24,8},{28,12},{1,17},{... | collective-permute-start | bytes 1769480 | tf_op jit(solution)/shard_map/ppermute | solution.py:24
  34.0 30.9 %collective-permute-start.9 = (bf16[6,48,1024]{2,1,0:T(8,128)(2,1)S(1)}, bf16[6,48,1024]{2,1,0:T(8,128)(2,1)S(1)}, u32[]{:S(2)}, u32[]{:S(2)}) collective-permute-start(bf16[6,48,1024]{2,1,0:T(8,128)(2,1)S(1)} %get-tuple-element.19.refs_0_.refs_1_), channel_id=1, source_target_pairs={{0,8},{4,12},{8,0},{12,4},{16,24},{20,28},{24,16},{28,20},{1,9},{5... | collective-permute-start | bytes 1769480 | tf_op jit(solution)/shard_map/ppermute | solution.py:24
  35.5 29.4 %collective-permute-start.8 = (bf16[6,48,1024]{2,1,0:T(8,128)(2,1)S(1)}, bf16[6,48,1024]{2,1,0:T(8,128)(2,1)S(1)}, u32[]{:S(2)}, u32[]{:S(2)}) collective-permute-start(bf16[6,48,1024]{2,1,0:T(8,128)(2,1)S(1)} %get-tuple-element.19.refs_0_.refs_1_), channel_id=1, source_target_pairs={{0,4},{4,0},{8,12},{12,8},{16,20},{20,16},{24,28},{28,24},{1,5},{5... | collective-permute-start | bytes 1769480 | tf_op jit(solution)/shard_map/ppermute | solution.py:24
  35.5 18.9 %collective-permute-start.6 = (bf16[4,48,1024]{2,1,0:T(8,128)(2,1)S(1)}, bf16[4,48,1024]{2,1,0:T(8,128)(2,1)S(1)}, u32[]{:S(2)}, u32[]{:S(2)}) collective-permute-start(bf16[4,48,1024]{2,1,0:T(8,128)(2,1)S(1)} %shard_map.86), channel_id=1, source_target_pairs={{0,8},{4,12},{8,0},{12,4},{16,24},{20,28},{24,16},{28,20},{1,9},{5... | collective-permute-start | bytes 1179656 | tf_op jit(solution)/shard_map/ppermute | solution.py:24
  36.1 18.3 %collective-permute-start.5 = (bf16[4,48,1024]{2,1,0:T(8,128)(2,1)S(1)}, bf16[4,48,1024]{2,1,0:T(8,128)(2,1)S(1)}, u32[]{:S(2)}, u32[]{:S(2)}) collective-permute-start(bf16[4,48,1024]{2,1,0:T(8,128)(2,1)S(1)} %shard_map.86), channel_id=1, source_target_pairs={{0,4},{4,0},{8,12},{12,8},{16,20},{20,16},{24,28},{28,24},{1,5},{5... | collective-permute-start | bytes 1179656 | tf_op jit(solution)/shard_map/ppermute | solution.py:24
  61.8 4.1 %collective-permute-start.13 = (f32[3,4,8,48]{3,2,1,0:T(8,128)S(1)}, f32[3,4,8,48]{3,2,1,0:T(8,128)S(1)}, u32[]{:S(2)}, u32[]{:S(2)}) collective-permute-start(f32[3,4,8,48]{3,2,1,0:T(8,128)S(1)} %get-tuple-element.27.refs_5_), channel_id=1, source_target_pairs={{0,16},{4,20},{8,24},{12,28},{16,0},{20,4},{24,8},{28,12},{1,17},{... | collective-permute-start | bytes 55304 | tf_op jit(solution)/shard_map/ppermute | solution.py:24
  63.4 4.1 %collective-permute-start.12 = (f32[3,4,8,48]{3,2,1,0:T(8,128)S(1)}, f32[3,4,8,48]{3,2,1,0:T(8,128)S(1)}, u32[]{:S(2)}, u32[]{:S(2)}) collective-permute-start(f32[3,4,8,48]{3,2,1,0:T(8,128)S(1)} %get-tuple-element.27.refs_5_), channel_id=1, source_target_pairs={{0,8},{4,12},{8,0},{12,4},{16,24},{20,28},{24,16},{28,20},{1,9},{5... | collective-permute-start | bytes 55304 | tf_op jit(solution)/shard_map/ppermute | solution.py:24
  64.8 2.6 %collective-permute-start.11 = (f32[3,4,8,48]{3,2,1,0:T(8,128)S(1)}, f32[3,4,8,48]{3,2,1,0:T(8,128)S(1)}, u32[]{:S(2)}, u32[]{:S(2)}) collective-permute-start(f32[3,4,8,48]{3,2,1,0:T(8,128)S(1)} %get-tuple-element.27.refs_5_), channel_id=1, source_target_pairs={{0,4},{4,0},{8,12},{12,8},{16,20},{20,16},{24,28},{28,24},{1,5},{5... | collective-permute-start | bytes 55304 | tf_op jit(solution)/shard_map/ppermute | solution.py:24
  70.5 6.8 %collective-permute-start.14 = (bf16[2,48,1024]{2,1,0:T(8,128)(2,1)S(1)}, bf16[2,48,1024]{2,1,0:T(8,128)(2,1)S(1)}, u32[]{:S(2)}, u32[]{:S(2)}) collective-permute-start(bf16[2,48,1024]{2,1,0:T(8,128)(2,1)S(1)} %get-tuple-element.28), channel_id=1, source_target_pairs={{0,1},{1,0},{2,3},{3,2},{4,5},{5,4},{6,7},{7,6},{8,9},{9,8},{10,11... | collective-permute-start | bytes 589832 | tf_op jit(solution)/shard_map/ppermute | solution.py:35
  71.2 6.1 %collective-permute-start.15 = (bf16[2,48,1024]{2,1,0:T(8,128)(2,1)S(1)}, bf16[2,48,1024]{2,1,0:T(8,128)(2,1)S(1)}, u32[]{:S(2)}, u32[]{:S(2)}) collective-permute-start(bf16[2,48,1024]{2,1,0:T(8,128)(2,1)S(1)} %get-tuple-element.29), channel_id=1, source_target_pairs={{1,2},{2,1},{5,6},{6,5},{9,10},{10,9},{13,14},{14,13},{17,18},{18,... | collective-permute-start | bytes 589832 | tf_op jit(solution)/shard_map/ppermute | solution.py:35

commit v2 on v1

--- a/solution.py
+++ b/solution.py
@@ -15,6 +15,7 @@
 PAIRS = 2
 PART = PAIRS * PAIR
 CHUNK = 16
+RING = 4
 BF16 = jnp.bfloat16
 F32 = jnp.float32
 
@@ -39,12 +40,12 @@
     return jax.ShapeDtypeStruct(shape, dtype)
 
 
-def call(kernel, outs, ins, flops=0, exps=0, scratch=(), limit=4 << 20, table=None, to_hbm=()):
+def call(kernel, outs, ins, flops=0, exps=0, scratch=(), limit=4 << 20, table=None, to_hbm=(), raw=0):
     size = sum(a.size * a.dtype.itemsize for a in ins) + sum(
         o.size * jnp.dtype(o.dtype).itemsize for o in outs
     )
-    ins = [pltpu.with_memory_space_constraint(a, pltpu.VMEM) for a in ins]
-    specs = [pl.BlockSpec(memory_space=pltpu.VMEM) for _ in ins]
+    ins = [pltpu.with_memory_space_constraint(a, pltpu.HBM) for a in ins[:raw]] + [pltpu.with_memory_space_constraint(a, pltpu.VMEM) for a in ins[raw:]]
+    specs = [pl.BlockSpec(memory_space=pltpu.HBM if i < raw else pltpu.VMEM) for i in range(len(ins))]
     if table is not None:
         ins = ins + [table]
         specs = specs + [pl.BlockSpec(memory_space=pltpu.SMEM)]
@@ -54,7 +55,9 @@
             o if i in to_hbm else pltpu.VMEM(o.shape, o.dtype) for i, o in enumerate(outs)
         ),
         in_specs=specs,
-        out_specs=tuple(pl.BlockSpec(memory_space=pltpu.VMEM) for _ in outs),
+        out_specs=tuple(
+            pl.BlockSpec(memory_space=pl.ANY if i in to_hbm else pltpu.VMEM) for i in range(len(outs))
+        ),
         scratch_shapes=list(scratch),
         compiler_params=pltpu.CompilerParams(vmem_limit_bytes=limit),
         cost_estimate=pl.CostEstimate(flops=flops, bytes_accessed=size, transcendentals=exps),
@@ -67,33 +70,63 @@
 
 
 def pack_kernel(n, *refs):
-    sources, (packed, *edges) = refs[:n], refs[-3:]
+    sources, (packed, edge0, edge1, *held, sems) = refs[:n], refs[-4 - n :]
     rows, columns, frames, width = sources[0].shape
-    for at, source in enumerate(sources):
+    flat = (columns * frames, width)
+    copies = [
+        [pltpu.make_async_copy(source.at[row], held[at].at[row], sems.at[at, row]) for row in range(rows)]
+        for at, source in enumerate(sources)
+    ]
+    for copy in sum(copies, []):
+        copy.start()
+    for at in range(n):
         for row in range(rows):
-            packed[at * rows + row] = source[row].reshape(columns * frames, width)
-        for edge, row in zip(edges, edge_rows(rows)):
-            edge[at] = source[row].reshape(columns * frames, width)
+            copies[at][row].wait()
+            packed[at * rows + row] = held[at][row].reshape(flat)
+    for edge, row in zip((edge0, edge1), edge_rows(rows)):
+        for at in range(n):
+            edge[at] = packed[at * rows + row]
 
 
 def pack(sources, after=()):
+    n = len(sources)
     rows, columns, frames, width = sources[0].shape
-    edge = struct(len(sources), columns * frames, width)
-    outs = [struct(len(sources) * rows, columns * frames, width), edge, edge]
-    kernel = functools.partial(pack_kernel, len(sources))
-    return call(kernel, outs, sources + list(after))
-
-
-def join_kernel(*refs):
-    sources, target = refs[:-1], refs[-1]
-    for at, source in enumerate(sources):
-        for slot in range(source.shape[0]):
-            target[at * source.shape[0] + slot] = source[slot]
-
-
-def join(sources):
-    shape = (len(sources) * sources[0].shape[0],) + sources[0].shape[1:]
-    return call(join_kernel, [struct(*shape, dtype=sources[0].dtype)], sources)[0]
+    edge = struct(n, columns * frames, width)
+    outs = [struct(n * rows, columns * frames, width), edge, edge]
+    kernel = functools.partial(pack_kernel, n)
+    held = [pltpu.VMEM(s.shape, s.dtype) for s in sources]
+    scratch = held + [pltpu.SemaphoreType.DMA((n, rows))]
+    return call(kernel, outs, sources + list(after), scratch=scratch, raw=n)
+
+
+def join_kernel(side0, side1, after, both, keys):
+    for side, source in enumerate((side0, side1)):
+        both[2 * side] = source[0]
+        both[2 * side + 1] = source[1]
+        keys[side] = source[0]
+
+
+def join(sources, after):
+    shape = sources[0].shape[1:]
+    return call(join_kernel, [struct(4, *shape), struct(2, *shape)], sources + after)
+
+
+def edge_kernel(*refs):
+    sources, targets = refs[:-2], refs[-2:]
+    rows = sources[0].shape[0] // 2
+    for slot, source in enumerate(sources):
+        for target, row in zip(targets, edge_rows(rows)):
+            target[slot] = source[rows + row]
+
+
+def value_edges(sources):
+    edge = struct(len(sources), *sources[0].shape[1:])
+    return call(edge_kernel, [edge, edge], sources)
+
+
+def lanes_at(group, pair):
+    start = group * PART + pair * PAIR
+    return slice(start, start + PAIR)
 
 
 def head_rows(value, lane_head):
@@ -148,8 +181,9 @@
     return (other >= 0) & (other < size)
 
 
-def build_masks(mask_ref, blocks, frames, tokens, table, queries_here):
-    shape = (8, blocks * tokens)
+def build_masks(mask_ref, blocks, frames, table, queries_here):
+    shape = mask_ref.shape[1:]
+    tokens = shape[1] // blocks
     lane = lax.broadcasted_iota(jnp.int32, shape, 1)
     sub = lax.broadcasted_iota(jnp.int32, shape, 0)
     bad = NEG if queries_here else -NEG
@@ -169,24 +203,27 @@
             mask_ref[1 + side] = value + jnp.where(rim_open(side), 0.0, bad).astype(F32)
 
 
+def mask_kernel(blocks, frames, after, table, mask_f, mask_b):
+    build_masks(mask_f, blocks, frames, table, True)
+    build_masks(mask_b, blocks, frames, table, False)
+
+
 def forward_kernel(layout, kinds, carried, *refs):
     qg = refs[layout["own"]]
     rows = qg.shape[0] // 2
     keys, values = (Pieces(refs, rows, *layout[name]) for name in ("k", "v"))
     n_in = layout["n_in"]
-    table = refs[n_in]
+    mask = refs[n_in]
     out, dq, stats = refs[n_in + 1 :][:3]
-    mask, s_scr, d_scr, p_scr = refs[-4:]
+    s_scr, d_scr, p_scr, _ = refs[-4:]
     tokens, width = qg.shape[1:]
     columns, frames = out.shape[1:3]
-    count = len(keys.mids)
     if carried:
         for target, source in zip((out, dq), refs[n_in - 3 : n_in - 1]):
             for at, row in enumerate(carried):
                 target[row] = source[at]
         for at in range(len(carried)):
             stats[at] = refs[n_in - 1][at]
-    build_masks(mask, count, frames, tokens, table, True)
     lane_head = lax.broadcasted_iota(jnp.int32, (tokens, PAIR), 1) // HEAD_DIM
     lane = lax.broadcasted_iota(jnp.int32, (2 * tokens, 128), 1)
     slot_of = lambda row: row if carried else row - 1
@@ -258,12 +295,17 @@
     kv = refs[0]
     qgs, stats_of = refs[1 : 1 + count], refs[1 + count : 1 + 2 * count]
     rims = refs[1 + 2 * count : n_in]
-    table, *outs = refs[n_in:-5]
-    mask, s_scr, d_scr, p_scr, t_scr = refs[-5:]
+    mask, *outs = refs[n_in:-4]
+    s_scr, d_scr, p_scr, t_scr = refs[-4:]
     rows = kv.shape[0] // 2
+    copies = []
+    if layout.get("held"):
+        sems = refs[-5]
+        for at, (held, out) in enumerate(zip(refs[n_in - 2 : n_in], outs[1:3])):
+            copies.append(pltpu.make_async_copy(held, out, sems.at[at]))
+            copies[-1].start()
     tokens, width = kv.shape[1:]
     part = count * tokens
-    build_masks(mask, count, layout["frames"], tokens, table, False)
     lane_head = lax.broadcasted_iota(jnp.int32, (tokens, PAIR), 1) // HEAD_DIM
     units = [(kind, pair) for kind in kinds for pair in range(PAIRS)]
 
@@ -297,17 +339,20 @@
         found = [qg[tensor * rows + row, :, lanes] for row, _ in query_rows(kind) for qg in qgs]
         return jnp.concatenate(found, axis=0)
 
-    def step(group, _):
-        lanes_of = [pl.ds(pl.multiple_of(group * PART + pair * PAIR, PAIR), PAIR) for pair in range(PAIRS)]
+    def products(group):
         for unit, (kind, pair) in enumerate(units):
-            lanes = lanes_of[pair]
+            lanes = lanes_at(group, pair)
             size = len(query_rows(kind)) * part
-            s_scr[unit, :, :size] = nt(
+            at = (group % 2) * len(units) + unit
+            s_scr[at, :, :size] = nt(
                 head_rows(key_rows(kind, 0, lanes) * SCALE, lane_head), window(kind, 0, lanes)
             )
-            d_scr[unit, :, :size] = nt(
+            d_scr[at, :, :size] = nt(
                 head_rows(key_rows(kind, 1, lanes), lane_head), window(kind, 1, lanes)
             )
+
+    def finish(group):
+        base = (group % 2) * len(units)
         stats = {
             kind: jnp.concatenate(
                 [ref[slot, group] for _, slot in query_rows(kind) for ref in stats_of], axis=1
@@ -324,34 +369,48 @@
                 delta = stat[2 * PAIRS + at : 2 * PAIRS + at + 1]
                 for start in range(h * tokens, (h + 1) * tokens, CHUNK):
                     rows_at = slice(start, start + CHUNK)
-                    probs = jnp.exp(s_scr[unit, rows_at, :size] - lse)
-                    p_scr[unit, rows_at, :size] = probs.astype(BF16)
-                    grad_scores = probs * (d_scr[unit, rows_at, :size] - delta)
-                    t_scr[unit, rows_at, :size] = grad_scores.astype(BF16)
+                    probs = jnp.exp(s_scr[base + unit, rows_at, :size] - lse)
+                    p_scr[base + unit, rows_at, :size] = probs.astype(BF16)
+                    grad_scores = probs * (d_scr[base + unit, rows_at, :size] - delta)
+                    t_scr[base + unit, rows_at, :size] = grad_scores.astype(BF16)
         for unit, (kind, pair) in enumerate(units):
-            lanes = lanes_of[pair]
+            lanes = lanes_at(group, pair)
             size = len(query_rows(kind)) * part
-            grad_v = head_lanes(nn(p_scr[unit, :, :size], window(kind, 1, lanes)), lane_head)
-            grad_k = head_lanes(nn(t_scr[unit, :, :size], window(kind, 0, lanes)), lane_head) * SCALE
+            grad_v = head_lanes(nn(p_scr[base + unit, :, :size], window(kind, 1, lanes)), lane_head)
+            grad_k = head_lanes(nn(t_scr[base + unit, :, :size], window(kind, 0, lanes)), lane_head) * SCALE
             for tensor, value in enumerate((grad_k, grad_v)):
                 if isinstance(kind, str) and kind[0] == "r":
                     outs[int(kind[-1])][tensor, :, lanes] = value.astype(BF16)
                 else:
                     row = row_of(kind, rows)
                     outs[0][tensor * rows + row, :, lanes] = value
-        return 0
-
-    lax.fori_loop(0, width // PART, step, 0)
-
-
-def finish_kernel(total, part0, part1, dk, dv):
+
+    products(0)
+    for group in range(width // PART):
+        if group + 1 < width // PART:
+            products(group + 1)
+        finish(group)
+    for copy in copies:
+        copy.wait()
+
+
+def finish_kernel(total, part0, part1, dk, dv, dk_held, dv_held, sems):
     rows, columns, frames, width = dk.shape
-    for tensor, out in enumerate((dk, dv)):
+    copies = []
+
+    def send(tensor, row, value):
+        held, out = ((dk_held, dk), (dv_held, dv))[tensor]
+        held[row] = value.astype(BF16).reshape(columns, frames, width)
+        copies.append(pltpu.make_async_copy(held.at[row], out.at[row], sems.at[len(copies)]))
+        copies[-1].start()
+
+    for tensor in range(2):
         for row in range(1, rows - 1):
-            out[row] = total[tensor * rows + row].astype(BF16).reshape(columns, frames, width)
+            send(tensor, row, total[tensor * rows + row])
         for part, row in zip((part0, part1), edge_rows(rows)):
-            value = total[tensor * rows + row] + part[tensor].astype(F32)
-            out[row] = value.astype(BF16).reshape(columns, frames, width)
+            send(tensor, row, total[tensor * rows + row] + part[tensor].astype(F32))
+    for copy in copies:
+        copy.wait()
 
 
 def per_device(query_vectors, key_vectors, value_vectors, out_cotangent, partner_mask):
@@ -368,9 +427,14 @@
     kv, kv_edge0, kv_edge1 = pack([turn(key_vectors), turn(value_vectors)])
     kvs = [kv] + swaps(kv, bits)
     kv_rims = [exchange(kv_edge0, 0), exchange(kv_edge1, 1)]
-    kv_rims_of = swaps(join(kv_rims), bits)
+    mask = lambda n: struct(n, 8, count * tokens, dtype=F32)
+    mask_f, mask_b = call(functools.partial(mask_kernel, count, frames), [mask(3), mask(1)], [kv_edge0], table=table)
+    joined, k_joined = join(kv_rims, [mask_b])
+    core_rims = swap(joined, 0)
+    k_rims_of = [swap(k_joined, bit) for bit in range(1, bits)]
     qg, _, _ = pack([turn(query_vectors), turn(out_cotangent)], [kv_edge0])
     qgs = [qg] + swaps(qg, bits)
+    v_far = [exchange(e, side) for side, e in enumerate(value_edges(kvs[2:]))]
 
     inner_kinds = list(range(1, rows - 1))
     edge_kinds = ["0", "1"]
@@ -380,10 +444,8 @@
     line = lambda n: struct(n, columns, frames, width)
 
     def scratches(n, extra):
-        units = n * PAIRS
-        wide = [pltpu.VMEM((3, 8, count * tokens), F32)]
-        wide += [pltpu.VMEM((units, 2 * tokens, window), F32)] * 2
-        return wide + [pltpu.VMEM((units, 2 * tokens, window), BF16)] * extra
+        wide = [pltpu.VMEM((n, 2 * tokens, window), F32)] * 2
+        return wide + [pltpu.VMEM((n, 2 * tokens, window), BF16)] * extra
 
     def gathered(at, rim_at, tensor):
         mids = [(at + block, tensor * rows) for block in range(count)]
@@ -391,8 +453,12 @@
             return mids, []
         sides = []
         for side in range(2):
-            own = [(rim_at + side, tensor)]
-            sides.append(own + [(rim_at + 2 + bit, 2 * side + tensor) for bit in range(bits)])
+            near = [(rim_at + side, tensor), (rim_at + 2, 2 * side + tensor)]
+            if tensor == 0:
+                far = [(rim_at + 3 + at, side) for at in range(bits - 1)]
+            else:
+                far = [(rim_at + 2 + bits + side, at) for at in range(bits - 1)]
+            sides.append(near + far)
         return mids, sides
 
     stat = lambda n: struct(n, groups, 4 * PAIRS, tokens, dtype=F32)
@@ -400,16 +466,16 @@
     layout = {"n_in": len(ins), "own": 0, "k": gathered(1, None, 0), "v": gathered(1, None, 1)}
     inner_out = call(
         functools.partial(forward_kernel, layout, inner_kinds, ()),
-        [line(inner), line(inner), stat(inner)], ins,
-        flops=work * inner, exps=exps * inner, scratch=scratches(inner, 1), limit=10 << 20, table=table,
+        [line(inner), line(inner), stat(inner)], ins + [mask_f],
+        flops=work * inner, exps=exps * inner, scratch=scratches(RING, 2), limit=14 << 20,
     )
     rim_at = len(ins)
-    ins = ins + kv_rims + kv_rims_of + list(inner_out)
+    ins = ins + kv_rims + [core_rims] + k_rims_of + v_far + list(inner_out)
     layout = {"n_in": len(ins), "own": 0, "k": gathered(1, rim_at, 0), "v": gathered(1, rim_at, 1)}
     attended, dq, stats = call(
         functools.partial(forward_kernel, layout, edge_kinds, inner_kinds),
-        [line(rows), line(rows), stat(rows)], ins, to_hbm=(0, 1),
-        flops=work * 2, exps=exps * 2, scratch=scratches(2, 1), limit=10 << 20, table=table,
+        [line(rows), line(rows), stat(rows)], ins + [mask_f],
+        flops=work * 2, exps=exps * 2, scratch=scratches(RING, 2), limit=14 << 20,
     )
     ss = [stats] + swaps(stats, bits)
 
@@ -418,17 +484,23 @@
     edge = struct(2, tokens, width)
     parts = call(
         functools.partial(backward_kernel, layout, ["r0", "r1"]),
-        [edge, edge], ins,
-        flops=work, exps=exps, scratch=scratches(2, 2), limit=10 << 20, table=table,
+        [edge, edge], ins + [mask_b],
+        flops=work, exps=exps, scratch=scratches(4 * PAIRS, 2), limit=14 << 20,
     )
     parts = [exchange(value, side) for side, value in enumerate(parts)]
-    (total,) = call(
+    full = struct(rows, columns, frames, width)
+    ins = ins + [attended, dq]
+    layout = {"n_in": len(ins), "count": count, "frames": frames, "held": 2}
+    total, attended, dq = call(
         functools.partial(backward_kernel, layout, inner_kinds + edge_kinds),
-        [struct(2 * rows, tokens, width, dtype=F32)], ins,
-        flops=2 * work, exps=2 * exps, scratch=scratches(rows, 2), limit=12 << 20, table=table,
-    )
-    full = struct(rows, columns, frames, width)
-    dk, dv = call(finish_kernel, [full, full], [total] + parts, to_hbm=(0, 1))
+        [struct(2 * rows, tokens, width, dtype=F32), full, full], ins + [mask_b], to_hbm=(1, 2),
+        flops=2 * work, exps=2 * exps, limit=18 << 20,
+        scratch=[pltpu.SemaphoreType.DMA((2,))] + scratches(2 * rows * PAIRS, 2),
+    )
+    dk, dv = call(
+        finish_kernel, [full, full], [total] + parts, to_hbm=(0, 1),
+        scratch=[pltpu.VMEM(full.shape, BF16)] * 2 + [pltpu.SemaphoreType.DMA((2 * rows,))],
+    )
     return back(attended), back(dq), back(dk), back(dv)
 
 

time: 78.4 us -> 59.9 us (0.76)
  waiting for transfers between devices: 34.9 us -> 16.7 us
  starting transfers between devices: 18.3 us -> 20.2 us
  local copies, waits for them, and re-layouts: 1.99 us -> 0.68 us
  Pallas kernels: 22.2 us -> 21.3 us
    ppermute x12, waiting for transfers between devices: 33.3 us -> 14 us  [swap(): lax.ppermute(value, 'frame', [(i, i ^ 1 << bit) for i in range(size)])]
    ppermute x4 -> x6, starting transfers between devices: 7.97 us -> 9.87 us  [exchange(): return lax.ppermute(value, 'space', pairs)]
    unnamed x10 -> x2, local copies, waits for them, and re-layouts: 1.99 us -> 0.68 us
    ppermute x4 -> x6, waiting for transfers between devices: 1.61 us -> 2.71 us  [exchange(): return lax.ppermute(value, 'space', pairs)]
    pallas_call x8 -> x10, Pallas kernels: 22.2 us -> 21.3 us  [call(): pl.pallas_call(kernel, out_shape=tuple((o if i in to_hbm else pltpu.VMEM(...]
  transfers between devices with their start and end apart: 16 -> 18, of which waited for: 5 -> 5; matrix products, arithmetic and copies ran while one was open for 0% -> 0% of each run, Pallas kernels for 23% -> 29%
where the time goes in v2:
time: 59.9 us; the launch traced here: 59.7 us
  Pallas kernels  21.3 us (36%)
  starting transfers between devices  20.2 us (34%)
  waiting for transfers between devices  16.7 us (28%)
  between operations  0.78 us (1%)
  local copies, waits for them, and re-layouts  0.68 us (1%)
    pallas_call x10, Pallas kernels, call(): pl.pallas_call(kernel, out_shape=tuple((o if i in to_hbm else pltpu.VMEM(...  21.3 us
    ppermute x12, waiting for transfers between devices, swap(): lax.ppermute(value, 'frame', [(i, i ^ 1 << bit) for i in range(size)])  14 us
    ppermute x12, starting transfers between devices, swap(): lax.ppermute(value, 'frame', [(i, i ^ 1 << bit) for i in range(size)])  10.3 us
    ppermute x6, starting transfers between devices, exchange(): return lax.ppermute(value, 'space', pairs)  9.87 us
    ppermute x6, waiting for transfers between devices, exchange(): return lax.ppermute(value, 'space', pairs)  2.71 us
  transfers between devices with their start and end apart: 18, of which 5 were waited for; matrix products, arithmetic and copies ran while one was open for 0% of the time, Pallas kernels for 29%

profile of v2, /device:TPU:0, one launch (start us, length us, event | category | flops | bytes accessed | tf_op | source)
XLA Modules:
  0.0 59.7 jit_solution(2959011224987615808)
XLA Ops:
  0.6 1.2 %shard_map.84 = (bf16[6,48,1024]{2,1,0:T(8,128)(2,1)S(1)}, bf16[2,48,1024]{2,1,0:T(8,128)(2,1)S(1)}, bf16[2,48,1024]{2,1,0:T(8,128)(2,1)S(1)}) custom-call(bf16[3,12,4,1024]{3,2,1,0:T(4,128)(2,1)} %bitcast.12, bf16[3,12,4,1024]{3,2,1,0:T(4,128)(2,1)} %bitcast.13), custom_call_target="tpu_custom_call" | custom-call | bytes 1572864 | tf_op jit(solution)/shard_map/pallas_call | solution.py:52
  1.9 3.0 %collective-permute-start.4 = (bf16[6,48,1024]{2,1,0:T(8,128)(2,1)S(1)}, bf16[6,48,1024]{2,1,0:T(8,128)(2,1)S(1)}, u32[]{:S(2)}, u32[]{:S(2)}) collective-permute-start(bf16[6,48,1024]{2,1,0:T(8,128)(2,1)S(1)} %get-tuple-element.27.refs_1_.refs_0_), channel_id=1, source_target_pairs={{0,8},{4,12},{8,0},{12,4},{16,24},{20,28},{24,16},{28,20},{1,9},{5... | collective-permute-start | bytes 1769480 | tf_op jit(solution)/shard_map/ppermute | solution.py:25
  4.9 1.5 %collective-permute-start.5 = (bf16[6,48,1024]{2,1,0:T(8,128)(2,1)S(1)}, bf16[6,48,1024]{2,1,0:T(8,128)(2,1)S(1)}, u32[]{:S(2)}, u32[]{:S(2)}) collective-permute-start(bf16[6,48,1024]{2,1,0:T(8,128)(2,1)S(1)} %get-tuple-element.27.refs_1_.refs_0_), channel_id=1, source_target_pairs={{0,16},{4,20},{8,24},{12,28},{16,0},{20,4},{24,8},{28,12},{1,17},{... | collective-permute-start | bytes 1769480 | tf_op jit(solution)/shard_map/ppermute | solution.py:25
  6.4 1.6 %collective-permute-start.6 = (bf16[2,48,1024]{2,1,0:T(8,128)(2,1)S(1)}, bf16[2,48,1024]{2,1,0:T(8,128)(2,1)S(1)}, u32[]{:S(2)}, u32[]{:S(2)}) collective-permute-start(bf16[2,48,1024]{2,1,0:T(8,128)(2,1)S(1)} %get-tuple-element.28.refs_2_.after), channel_id=1, source_target_pairs={{0,1},{1,0},{2,3},{3,2},{4,5},{5,4},{6,7},{7,6},{8,9},{9,8},{10,11... | collective-permute-start | bytes 589832 | tf_op jit(solution)/shard_map/ppermute | solution.py:36
  8.0 0.7 %collective-permute-start.7 = (bf16[2,48,1024]{2,1,0:T(8,128)(2,1)S(1)}, bf16[2,48,1024]{2,1,0:T(8,128)(2,1)S(1)}, u32[]{:S(2)}, u32[]{:S(2)}) collective-permute-start(bf16[2,48,1024]{2,1,0:T(8,128)(2,1)S(1)} %get-tuple-element.30), channel_id=1, source_target_pairs={{1,2},{2,1},{5,6},{6,5},{9,10},{10,9},{13,14},{14,13},{17,18},{18,... | collective-permute-start | bytes 589832 | tf_op jit(solution)/shard_map/ppermute | solution.py:36
  8.7 0.1 collective-permute-start.3
  8.7 0.0 copy-start
  8.7 0.7 %copy-done = s32[32,3]{0,1:T(4,128)S(1)} copy-done((s32[32,3]{0,1:T(4,128)S(1)}, s32[32,3]{0,1:T(4,128)}, u32[]{:S(2)}) %copy-start) | copy-done | bytes 408
  9.4 0.6 %shard_map.86 = (f32[3,8,192]{2,1,0:T(8,128)S(1)}, f32[1,8,192]{2,1,0:T(8,128)S(1)}) custom-call(bf16[2,48,1024]{2,1,0:T(8,128)(2,1)S(1)} %get-tuple-element.28.refs_2_.after, s32[3,32]{1,0:T(4,128)S(1)} %bitcast.9), custom_call_target="tpu_custom_call" | custom-call | bytes 221184 | tf_op jit(solution)/shard_map/pallas_call | solution.py:52
  10.1 2.4 %collective-permute-done.6.side0.refs_5_.refs_9_ = bf16[2,48,1024]{2,1,0:T(8,128)(2,1)S(1)} collective-permute-done((bf16[2,48,1024]{2,1,0:T(8,128)(2,1)S(1)}, bf16[2,48,1024]{2,1,0:T(8,128)(2,1)S(1)}, u32[]{:S(2)}, u32[]{:S(2)}) %collective-permute-start.6) | collective-permute-done | bytes 196640 | tf_op jit(solution)/shard_map/ppermute | solution.py:36
  12.5 0.0 collective-permute-done.7.side1.refs_6_.refs_10_
  12.5 0.6 collective-permute-start.10
  13.1 0.4 collective-permute-start.9
  13.5 10.4 %collective-permute-done.10.refs_9_ = bf16[2,48,1024]{2,1,0:T(8,128)(2,1)S(1)} collective-permute-done((bf16[2,48,1024]{2,1,0:T(8,128)(2,1)S(1)}, bf16[2,48,1024]{2,1,0:T(8,128)(2,1)S(1)}, u32[]{:S(2)}, u32[]{:S(2)}) %collective-permute-start.10) | collective-permute-done | bytes 196640 | tf_op jit(solution)/shard_map/ppermute | solution.py:25
  23.9 0.0 collective-permute-start.8
  23.9 2.0 %shard_map.85 = (bf16[6,48,1024]{2,1,0:T(8,128)(2,1)S(1)}, bf16[2,48,1024]{2,1,0:T(8,128)(2,1)}, bf16[2,48,1024]{2,1,0:T(8,128)(2,1)}) custom-call(bf16[3,12,4,1024]{3,2,1,0:T(4,128)(2,1)} %bitcast.10, bf16[3,12,4,1024]{3,2,1,0:T(4,128)(2,1)} %bitcast.11, bf16[2,48,1024]{2,1,0:T(8,128)(2,1)S(1)} %get-tuple-element.28.refs_2_.after), custom_call_target="tpu_custom_call" | custom-call | bytes 1769472 | tf_op jit(solution)/shard_map/pallas_call | solution.py:52
  25.9 0.0 collective-permute-done.9.refs_8_
  25.9 0.6 collective-permute-start
  26.4 0.0 collective-permute-done.4.refs_0_.refs_3_
  26.4 0.4 collective-permute-start.1
  26.8 0.0 collective-permute-done.5.refs_1_.refs_4_
  26.8 1.7 %collective-permute-start.2 = (bf16[6,48,1024]{2,1,0:T(8,128)(2,1)S(1)}, bf16[6,48,1024]{2,1,0:T(8,128)(2,1)S(1)}, u32[]{:S(2)}, u32[]{:S(2)}) collective-permute-start(bf16[6,48,1024]{2,1,0:T(8,128)(2,1)S(1)} %get-tuple-element.29.refs_0_.refs_1_), channel_id=1, source_target_pairs={{0,16},{4,20},{8,24},{12,28},{16,0},{20,4},{24,8},{28,12},{1,17},{... | collective-permute-start | bytes 1769480 | tf_op jit(solution)/shard_map/ppermute | solution.py:25
  28.5 0.0 collective-permute-done.3.refs_2_
  28.5 1.6 %collective-permute-start.11 = (bf16[2,48,1024]{2,1,0:T(8,128)(2,1)S(1)}, bf16[2,48,1024]{2,1,0:T(8,128)(2,1)S(1)}, u32[]{:S(2)}, u32[]{:S(2)}) collective-permute-start(bf16[2,48,1024]{2,1,0:T(8,128)(2,1)S(1)} %get-tuple-element.34), channel_id=1, source_target_pairs={{0,1},{1,0},{2,3},{3,2},{4,5},{5,4},{6,7},{7,6},{8,9},{9,8},{10,11... | collective-permute-start | bytes 589832 | tf_op jit(solution)/shard_map/ppermute | solution.py:36
  30.2 0.0 collective-permute-done.8.refs_7_
  30.2 0.7 %collective-permute-start.12 = (bf16[2,48,1024]{2,1,0:T(8,128)(2,1)S(1)}, bf16[2,48,1024]{2,1,0:T(8,128)(2,1)S(1)}, u32[]{:S(2)}, u32[]{:S(2)}) collective-permute-start(bf16[2,48,1024]{2,1,0:T(8,128)(2,1)S(1)} %get-tuple-element.35), channel_id=1, source_target_pairs={{1,2},{2,1},{5,6},{6,5},{9,10},{10,9},{13,14},{14,13},{17,18},{18,... | collective-permute-start | bytes 589832 | tf_op jit(solution)/shard_map/ppermute | solution.py:36
  30.9 3.8 %shard_map.89 = (bf16[1,12,4,1024]{3,2,1,0:T(4,128)(2,1)S(1)}, bf16[1,12,4,1024]{3,2,1,0:T(4,128)(2,1)S(1)}, f32[1,4,8,48]{3,2,1,0:T(8,128)S(1)}) custom-call(bf16[6,48,1024]{2,1,0:T(8,128)(2,1)S(1)} %get-tuple-element.29.refs_0_.refs_1_, bf16[6,48,1024]{2,1,0:T(8,128)(2,1)S(1)} %get-tuple-element.27.refs_1_.refs_0_, ...), custom_call_target="tpu_custom_call" | custom-call | flops 452984832 | bytes 3170304 | tf_op jit(solution)/shard_map/pallas_call | solution.py:52
  34.7 0.3 collective-permute-done.11.refs_10_
  34.9 0.0 collective-permute-done.12.refs_11_
  34.9 6.0 %shard_map.90 = (bf16[3,12,4,1024]{3,2,1,0:T(4,128)(2,1)S(1)}, bf16[3,12,4,1024]{3,2,1,0:T(4,128)(2,1)S(1)}, f32[3,4,8,48]{3,2,1,0:T(8,128)S(1)}) custom-call(bf16[6,48,1024]{2,1,0:T(8,128)(2,1)S(1)} %get-tuple-element.29.refs_0_.refs_1_, bf16[6,48,1024]{2,1,0:T(8,128)(2,1)S(1)} %get-tuple-element.27.refs_1_.refs_0_, ...), custom_call_target="tpu_custom_call" | custom-call | flops 905969664 | bytes 5351424 | tf_op jit(solution)/shard_map/pallas_call | solution.py:52
  40.9 0.1 collective-permute-start.13
  41.0 1.5 %collective-permute-start.14 = (f32[3,4,8,48]{3,2,1,0:T(8,128)S(1)}, f32[3,4,8,48]{3,2,1,0:T(8,128)S(1)}, u32[]{:S(2)}, u32[]{:S(2)}) collective-permute-start(f32[3,4,8,48]{3,2,1,0:T(8,128)S(1)} %get-tuple-element.40.refs_5_), channel_id=1, source_target_pairs={{0,8},{4,12},{8,0},{12,4},{16,24},{20,28},{24,16},{28,20},{1,9},{5... | collective-permute-start | bytes 55304 | tf_op jit(solution)/shard_map/ppermute | solution.py:25
  42.5 0.0 collective-permute-done.refs_2_
  42.5 0.5 collective-permute-start.15
  43.0 0.0 collective-permute-done.1.refs_3_
  43.0 0.0 collective-permute-done.2.refs_4_
  43.0 0.0 collective-permute-done.13.refs_6_
  43.1 2.1 %collective-permute-done.14.refs_7_ = f32[3,4,8,48]{3,2,1,0:T(8,128)S(1)} collective-permute-done((f32[3,4,8,48]{3,2,1,0:T(8,128)S(1)}, f32[3,4,8,48]{3,2,1,0:T(8,128)S(1)}, u32[]{:S(2)}, u32[]{:S(2)}) %collective-permute-start.14) | collective-permute-done | bytes 18464 | tf_op jit(solution)/shard_map/ppermute | solution.py:25
  45.1 1.5 %collective-permute-done.15.refs_8_ = f32[3,4,8,48]{3,2,1,0:T(8,128)S(1)} collective-permute-done((f32[3,4,8,48]{3,2,1,0:T(8,128)S(1)}, f32[3,4,8,48]{3,2,1,0:T(8,128)S(1)}, u32[]{:S(2)}, u32[]{:S(2)}) %collective-permute-start.15) | collective-permute-done | bytes 18464 | tf_op jit(solution)/shard_map/ppermute | solution.py:25
  46.6 1.8 %shard_map.92 = (bf16[2,48,1024]{2,1,0:T(8,128)(2,1)S(1)}, bf16[2,48,1024]{2,1,0:T(8,128)(2,1)S(1)}) custom-call(bf16[6,48,1024]{2,1,0:T(8,128)(2,1)S(1)} %get-tuple-element.27.refs_1_.refs_0_, bf16[6,48,1024]{2,1,0:T(8,128)(2,1)S(1)} %get-tuple-element.29.refs_0_.refs_1_, bf16[6,48,1024]{2,1,0:T(8,128)(2,1)S(1)} %collective-permute-done.refs_2_, ...), custom_call_target="tpu_custom_call" | custom-call | flops 452984832 | bytes 3815424 | tf_op jit(solution)/shard_map/pallas_call | solution.py:52
  48.4 4.7 %collective-permute-start.16 = (bf16[2,48,1024]{2,1,0:T(8,128)(2,1)S(1)}, bf16[2,48,1024]{2,1,0:T(8,128)(2,1)S(1)}, u32[]{:S(2)}, u32[]{:S(2)}) collective-permute-start(bf16[2,48,1024]{2,1,0:T(8,128)(2,1)S(1)} %get-tuple-element.46), channel_id=1, source_target_pairs={{0,1},{1,0},{2,3},{3,2},{4,5},{5,4},{6,7},{7,6},{8,9},{9,8},{10,11... | collective-permute-start | bytes 589832 | tf_op jit(solution)/shard_map/ppermute | solution.py:36
  53.1 0.7 %collective-permute-start.17 = (bf16[2,48,1024]{2,1,0:T(8,128)(2,1)S(1)}, bf16[2,48,1024]{2,1,0:T(8,128)(2,1)S(1)}, u32[]{:S(2)}, u32[]{:S(2)}) collective-permute-start(bf16[2,48,1024]{2,1,0:T(8,128)(2,1)S(1)} %get-tuple-element.47), channel_id=1, source_target_pairs={{1,2},{2,1},{5,6},{6,5},{9,10},{10,9},{13,14},{14,13},{17,18},{18,... | collective-permute-start | bytes 589832 | tf_op jit(solution)/shard_map/ppermute | solution.py:36
  53.8 5.0 %shard_map.91 = (f32[6,48,1024]{2,1,0:T(8,128)S(1)}, bf16[3,12,4,1024]{3,2,1,0:T(4,128)(2,1)}, bf16[3,12,4,1024]{3,2,1,0:T(4,128)(2,1)}) custom-call(bf16[6,48,1024]{2,1,0:T(8,128)(2,1)S(1)} %get-tuple-element.27.refs_1_.refs_0_, bf16[6,48,1024]{2,1,0:T(8,128)(2,1)S(1)} %get-tuple-element.29.refs_0_.refs_1_, ...), custom_call_target="tpu_custom_call" | custom-call | flops 905969664 | bytes 5781504 | tf_op jit(solution)/shard_map/pallas_call | solution.py:52
  58.8 0.0 collective-permute-done.16.part0
  58.8 0.0 collective-permute-done.17.part1
  58.8 0.9 %shard_map.93 = (bf16[3,12,4,1024]{3,2,1,0:T(4,128)(2,1)}, bf16[3,12,4,1024]{3,2,1,0:T(4,128)(2,1)}) custom-call(f32[6,48,1024]{2,1,0:T(8,128)S(1)} %get-tuple-element.45.total, bf16[2,48,1024]{2,1,0:T(8,128)(2,1)S(1)} %collective-permute-done.16.part0, bf16[2,48,1024]{2,1,0:T(8,128)(2,1)S(1)} %collective-permute-done.17.part1), custom_call_target="tpu_custom_call" | custom-call | bytes 2162688 | tf_op jit(solution)/shard_map/pallas_call | solution.py:52
  (2 shorter events, 0.1 us)
Async XLA Ops:
  1.9 24.6 %collective-permute-start.4 = (bf16[6,48,1024]{2,1,0:T(8,128)(2,1)S(1)}, bf16[6,48,1024]{2,1,0:T(8,128)(2,1)S(1)}, u32[]{:S(2)}, u32[]{:S(2)}) collective-permute-start(bf16[6,48,1024]{2,1,0:T(8,128)(2,1)S(1)} %get-tuple-element.27.refs_1_.refs_0_), channel_id=1, source_target_pairs={{0,8},{4,12},{8,0},{12,4},{16,24},{20,28},{24,16},{28,20},{1,9},{5... | collective-permute-start | bytes 1769480 | tf_op jit(solution)/shard_map/ppermute | solution.py:25
  4.9 21.9 %collective-permute-start.5 = (bf16[6,48,1024]{2,1,0:T(8,128)(2,1)S(1)}, bf16[6,48,1024]{2,1,0:T(8,128)(2,1)S(1)}, u32[]{:S(2)}, u32[]{:S(2)}) collective-permute-start(bf16[6,48,1024]{2,1,0:T(8,128)(2,1)S(1)} %get-tuple-element.27.refs_1_.refs_0_), channel_id=1, source_target_pairs={{0,16},{4,20},{8,24},{12,28},{16,0},{20,4},{24,8},{28,12},{1,17},{... | collective-permute-start | bytes 1769480 | tf_op jit(solution)/shard_map/ppermute | solution.py:25
  6.4 6.1 %collective-permute-start.6 = (bf16[2,48,1024]{2,1,0:T(8,128)(2,1)S(1)}, bf16[2,48,1024]{2,1,0:T(8,128)(2,1)S(1)}, u32[]{:S(2)}, u32[]{:S(2)}) collective-permute-start(bf16[2,48,1024]{2,1,0:T(8,128)(2,1)S(1)} %get-tuple-element.28.refs_2_.after), channel_id=1, source_target_pairs={{0,1},{1,0},{2,3},{3,2},{4,5},{5,4},{6,7},{7,6},{8,9},{9,8},{10,11... | collective-permute-start | bytes 589832 | tf_op jit(solution)/shard_map/ppermute | solution.py:36
  8.0 4.5 %collective-permute-start.7 = (bf16[2,48,1024]{2,1,0:T(8,128)(2,1)S(1)}, bf16[2,48,1024]{2,1,0:T(8,128)(2,1)S(1)}, u32[]{:S(2)}, u32[]{:S(2)}) collective-permute-start(bf16[2,48,1024]{2,1,0:T(8,128)(2,1)S(1)} %get-tuple-element.30), channel_id=1, source_target_pairs={{1,2},{2,1},{5,6},{6,5},{9,10},{10,9},{13,14},{14,13},{17,18},{18,... | collective-permute-start | bytes 589832 | tf_op jit(solution)/shard_map/ppermute | solution.py:36
  8.7 19.9 %collective-permute-start.3 = (bf16[6,48,1024]{2,1,0:T(8,128)(2,1)S(1)}, bf16[6,48,1024]{2,1,0:T(8,128)(2,1)S(1)}, u32[]{:S(2)}, u32[]{:S(2)}) collective-permute-start(bf16[6,48,1024]{2,1,0:T(8,128)(2,1)S(1)} %get-tuple-element.27.refs_1_.refs_0_), channel_id=1, source_target_pairs={{0,4},{4,0},{8,12},{12,8},{16,20},{20,16},{24,28},{28,24},{1,5},{5... | collective-permute-start | bytes 1769480 | tf_op jit(solution)/shard_map/ppermute | solution.py:25
  8.7 0.7 %copy-start = (s32[32,3]{0,1:T(4,128)S(1)}, s32[32,3]{0,1:T(4,128)}, u32[]{:S(2)}) copy-start(s32[32,3]{0,1:T(4,128)} %param.9) | copy-start | bytes 1156
  12.5 11.4 %collective-permute-start.10 = (bf16[2,48,1024]{2,1,0:T(8,128)(2,1)S(1)}, bf16[2,48,1024]{2,1,0:T(8,128)(2,1)S(1)}, u32[]{:S(2)}, u32[]{:S(2)}) collective-permute-start(bf16[2,48,1024]{2,1,0:T(8,128)(2,1)S(1)} %get-tuple-element.33), channel_id=1, source_target_pairs={{0,16},{4,20},{8,24},{12,28},{16,0},{20,4},{24,8},{28,12},{1,17},{... | collective-permute-start | bytes 589832 | tf_op jit(solution)/shard_map/ppermute | solution.py:25
  13.1 12.8 %collective-permute-start.9 = (bf16[2,48,1024]{2,1,0:T(8,128)(2,1)S(1)}, bf16[2,48,1024]{2,1,0:T(8,128)(2,1)S(1)}, u32[]{:S(2)}, u32[]{:S(2)}) collective-permute-start(bf16[2,48,1024]{2,1,0:T(8,128)(2,1)S(1)} %get-tuple-element.33), channel_id=1, source_target_pairs={{0,8},{4,12},{8,0},{12,4},{16,24},{20,28},{24,16},{28,20},{1,9},{5... | collective-permute-start | bytes 589832 | tf_op jit(solution)/shard_map/ppermute | solution.py:25
  23.9 6.3 %collective-permute-start.8 = (bf16[4,48,1024]{2,1,0:T(8,128)(2,1)S(1)}, bf16[4,48,1024]{2,1,0:T(8,128)(2,1)S(1)}, u32[]{:S(2)}, u32[]{:S(2)}) collective-permute-start(bf16[4,48,1024]{2,1,0:T(8,128)(2,1)S(1)} %get-tuple-element.32), channel_id=1, source_target_pairs={{0,4},{4,0},{8,12},{12,8},{16,20},{20,16},{24,28},{28,24},{1,5},{5... | collective-permute-start | bytes 1179656 | tf_op jit(solution)/shard_map/ppermute | solution.py:25
  25.9 16.7 %collective-permute-start = (bf16[6,48,1024]{2,1,0:T(8,128)(2,1)S(1)}, bf16[6,48,1024]{2,1,0:T(8,128)(2,1)S(1)}, u32[]{:S(2)}, u32[]{:S(2)}) collective-permute-start(bf16[6,48,1024]{2,1,0:T(8,128)(2,1)S(1)} %get-tuple-element.29.refs_0_.refs_1_), channel_id=1, source_target_pairs={{0,4},{4,0},{8,12},{12,8},{16,20},{20,16},{24,28},{28,24},{1,5},{5... | collective-permute-start | bytes 1769480 | tf_op jit(solution)/shard_map/ppermute | solution.py:25
  26.4 16.6 %collective-permute-start.1 = (bf16[6,48,1024]{2,1,0:T(8,128)(2,1)S(1)}, bf16[6,48,1024]{2,1,0:T(8,128)(2,1)S(1)}, u32[]{:S(2)}, u32[]{:S(2)}) collective-permute-start(bf16[6,48,1024]{2,1,0:T(8,128)(2,1)S(1)} %get-tuple-element.29.refs_0_.refs_1_), channel_id=1, source_target_pairs={{0,8},{4,12},{8,0},{12,4},{16,24},{20,28},{24,16},{28,20},{1,9},{5... | collective-permute-start | bytes 1769480 | tf_op jit(solution)/shard_map/ppermute | solution.py:25
  26.8 16.2 %collective-permute-start.2 = (bf16[6,48,1024]{2,1,0:T(8,128)(2,1)S(1)}, bf16[6,48,1024]{2,1,0:T(8,128)(2,1)S(1)}, u32[]{:S(2)}, u32[]{:S(2)}) collective-permute-start(bf16[6,48,1024]{2,1,0:T(8,128)(2,1)S(1)} %get-tuple-element.29.refs_0_.refs_1_), channel_id=1, source_target_pairs={{0,16},{4,20},{8,24},{12,28},{16,0},{20,4},{24,8},{28,12},{1,17},{... | collective-permute-start | bytes 1769480 | tf_op jit(solution)/shard_map/ppermute | solution.py:25
  28.5 6.4 %collective-permute-start.11 = (bf16[2,48,1024]{2,1,0:T(8,128)(2,1)S(1)}, bf16[2,48,1024]{2,1,0:T(8,128)(2,1)S(1)}, u32[]{:S(2)}, u32[]{:S(2)}) collective-permute-start(bf16[2,48,1024]{2,1,0:T(8,128)(2,1)S(1)} %get-tuple-element.34), channel_id=1, source_target_pairs={{0,1},{1,0},{2,3},{3,2},{4,5},{5,4},{6,7},{7,6},{8,9},{9,8},{10,11... | collective-permute-start | bytes 589832 | tf_op jit(solution)/shard_map/ppermute | solution.py:36
  30.2 4.8 %collective-permute-start.12 = (bf16[2,48,1024]{2,1,0:T(8,128)(2,1)S(1)}, bf16[2,48,1024]{2,1,0:T(8,128)(2,1)S(1)}, u32[]{:S(2)}, u32[]{:S(2)}) collective-permute-start(bf16[2,48,1024]{2,1,0:T(8,128)(2,1)S(1)} %get-tuple-element.35), channel_id=1, source_target_pairs={{1,2},{2,1},{5,6},{6,5},{9,10},{10,9},{13,14},{14,13},{17,18},{18,... | collective-permute-start | bytes 589832 | tf_op jit(solution)/shard_map/ppermute | solution.py:36
  40.9 2.1 %collective-permute-start.13 = (f32[3,4,8,48]{3,2,1,0:T(8,128)S(1)}, f32[3,4,8,48]{3,2,1,0:T(8,128)S(1)}, u32[]{:S(2)}, u32[]{:S(2)}) collective-permute-start(f32[3,4,8,48]{3,2,1,0:T(8,128)S(1)} %get-tuple-element.40.refs_5_), channel_id=1, source_target_pairs={{0,4},{4,0},{8,12},{12,8},{16,20},{20,16},{24,28},{28,24},{1,5},{5... | collective-permute-start | bytes 55304 | tf_op jit(solution)/shard_map/ppermute | solution.py:25
  41.0 4.2 %collective-permute-start.14 = (f32[3,4,8,48]{3,2,1,0:T(8,128)S(1)}, f32[3,4,8,48]{3,2,1,0:T(8,128)S(1)}, u32[]{:S(2)}, u32[]{:S(2)}) collective-permute-start(f32[3,4,8,48]{3,2,1,0:T(8,128)S(1)} %get-tuple-element.40.refs_5_), channel_id=1, source_target_pairs={{0,8},{4,12},{8,0},{12,4},{16,24},{20,28},{24,16},{28,20},{1,9},{5... | collective-permute-start | bytes 55304 | tf_op jit(solution)/shard_map/ppermute | solution.py:25
  42.5 4.1 %collective-permute-start.15 = (f32[3,4,8,48]{3,2,1,0:T(8,128)S(1)}, f32[3,4,8,48]{3,2,1,0:T(8,128)S(1)}, u32[]{:S(2)}, u32[]{:S(2)}) collective-permute-start(f32[3,4,8,48]{3,2,1,0:T(8,128)S(1)} %get-tuple-element.40.refs_5_), channel_id=1, source_target_pairs={{0,16},{4,20},{8,24},{12,28},{16,0},{20,4},{24,8},{28,12},{1,17},{... | collective-permute-start | bytes 55304 | tf_op jit(solution)/shard_map/ppermute | solution.py:25
  48.4 10.4 %collective-permute-start.16 = (bf16[2,48,1024]{2,1,0:T(8,128)(2,1)S(1)}, bf16[2,48,1024]{2,1,0:T(8,128)(2,1)S(1)}, u32[]{:S(2)}, u32[]{:S(2)}) collective-permute-start(bf16[2,48,1024]{2,1,0:T(8,128)(2,1)S(1)} %get-tuple-element.46), channel_id=1, source_target_pairs={{0,1},{1,0},{2,3},{3,2},{4,5},{5,4},{6,7},{7,6},{8,9},{9,8},{10,11... | collective-permute-start | bytes 589832 | tf_op jit(solution)/shard_map/ppermute | solution.py:36
  53.1 5.7 %collective-permute-start.17 = (bf16[2,48,1024]{2,1,0:T(8,128)(2,1)S(1)}, bf16[2,48,1024]{2,1,0:T(8,128)(2,1)S(1)}, u32[]{:S(2)}, u32[]{:S(2)}) collective-permute-start(bf16[2,48,1024]{2,1,0:T(8,128)(2,1)S(1)} %get-tuple-element.47), channel_id=1, source_target_pairs={{1,2},{2,1},{5,6},{6,5},{9,10},{10,9},{13,14},{14,13},{17,18},{18,... | collective-permute-start | bytes 589832 | tf_op jit(solution)/shard_map/ppermute | solution.py:36

commit v3 on v2

--- a/solution.py
+++ b/solution.py
@@ -288,6 +288,122 @@
         return 0
 
     lax.fori_loop(0, width // PART, step, 0)
+
+
+def forward_edge_kernel(layout, kinds, carried, *refs):
+    qg = refs[layout["own"]]
+    rows = qg.shape[0] // 2
+    keys, values = (Pieces(refs, rows, *layout[name]) for name in ("k", "v"))
+    n_in = layout["n_in"]
+    mask = refs[n_in]
+    out, stats, raw_out, column_out = refs[n_in + 1 :][:4]
+    s_scr, p_scr = refs[-2:]
+    tokens, width = qg.shape[1:]
+    columns, frames = out.shape[1:3]
+    if carried:
+        for at, row in enumerate(carried):
+            out[row] = refs[n_in - 2][at]
+            stats[at] = refs[n_in - 1][at]
+    lane_head = lax.broadcasted_iota(jnp.int32, (tokens, PAIR), 1) // HEAD_DIM
+    lane = lax.broadcasted_iota(jnp.int32, (2 * tokens, 128), 1)
+    slot_of = lambda row: row if carried else row - 1
+    units = [(slot, pair) for slot in range(len(kinds)) for pair in range(PAIRS)]
+
+    def step(group, _):
+        starts = [pl.multiple_of(group * PART + pair * PAIR, PAIR) for pair in range(PAIRS)]
+        lanes_of = [pl.ds(start, PAIR) for start in starts]
+        for unit, (slot, pair) in enumerate(units):
+            lanes, kind = lanes_of[pair], kinds[slot]
+            row = row_of(kind, rows)
+            s_scr[unit] = nt(head_rows(qg[row, :, lanes] * SCALE, lane_head), keys.window(kind, lanes))
+        tops, totals = [], []
+        for unit, (slot, pair) in enumerate(units):
+            top_parts, total_parts = [], []
+            first = mask[0] if isinstance(kinds[slot], int) else mask[1 + int(kinds[slot])]
+            bias = jnp.concatenate([first, mask[0], mask[0]], axis=1)
+            bias = jnp.concatenate([bias] * (CHUNK // 8), axis=0)
+            for start in range(0, 2 * tokens, CHUNK):
+                scores = s_scr[unit, start : start + CHUNK, :] + bias
+                top = jnp.max(scores, axis=1, keepdims=True)
+                raw = jnp.exp(scores - top)
+                raw_out[group * len(units) + unit, start : start + CHUNK, :] = raw
+                p_scr[unit, start : start + CHUNK, :] = raw.astype(BF16)
+                top_parts.append(top)
+                total_parts.append(jnp.sum(raw, axis=1, keepdims=True))
+            tops.append(jnp.concatenate(top_parts, axis=0))
+            totals.append(jnp.concatenate(total_parts, axis=0))
+        cols = jnp.zeros((2 * tokens, 128), F32)
+        for unit, (slot, pair) in enumerate(units):
+            lanes, kind = lanes_of[pair], kinds[slot]
+            row = row_of(kind, rows)
+            scale = 1.0 / totals[unit]
+            wide = nn(p_scr[unit], values.window(kind, lanes)) * scale
+            attended = head_lanes(wide, lane_head).astype(BF16)
+            out[slot_of(row), :, :, lanes] = attended.reshape(columns, frames, PAIR)
+            prod = qg[rows + row, :, lanes].astype(F32) * attended.astype(F32)
+            delta = jnp.sum(head_rows(prod, lane_head), axis=1, keepdims=True)
+            for which, column in enumerate((scale, delta)):
+                column_out[group * len(units) + unit, which] = jnp.broadcast_to(column, (2 * tokens, 128))
+            cols = jnp.where(lane == 2 * unit, tops[unit] + jnp.log(totals[unit]), cols)
+            cols = jnp.where(lane == 2 * unit + 1, delta, cols)
+        turned = cols.T
+        for unit, (slot, pair) in enumerate(units):
+            for which in range(2):
+                line = turned[2 * unit + which : 2 * unit + which + 1]
+                for h in range(2):
+                    to = which * 2 * PAIRS + pair * 2 + h
+                    stats[len(carried) + slot, group, to : to + 1, :] = line[:, h * tokens : (h + 1) * tokens]
+        return 0
+
+    lax.fori_loop(0, width // PART, step, 0)
+
+
+def forward_grad_kernel(layout, kinds, carried, *refs):
+    qg = refs[layout["own"]]
+    rows = qg.shape[0] // 2
+    keys, values = (Pieces(refs, rows, *layout[name]) for name in ("k", "v"))
+    n_in = layout["n_in"]
+    inner_dq, raw_in, column_in = refs[n_in - 3 : n_in]
+    dq, d_scr, p_scr = refs[n_in:]
+    tokens, width = qg.shape[1:]
+    columns, frames = dq.shape[1:3]
+    window = d_scr.shape[2]
+    for at, row in enumerate(carried):
+        dq[row] = inner_dq[at]
+    lane_head = lax.broadcasted_iota(jnp.int32, (tokens, PAIR), 1) // HEAD_DIM
+    units = [(slot, pair) for slot in range(len(kinds)) for pair in range(PAIRS)]
+
+    def products(group):
+        for unit, (slot, pair) in enumerate(units):
+            lanes, kind = lanes_at(group, pair), kinds[slot]
+            row = row_of(kind, rows)
+            at = (group % 2) * len(units) + unit
+            d_scr[at] = nt(head_rows(qg[rows + row, :, lanes], lane_head), values.window(kind, lanes))
+
+    def finish(group):
+        base = (group % 2) * len(units)
+        for unit, (slot, pair) in enumerate(units):
+            held = group * len(units) + unit
+            for start in range(0, 2 * tokens, CHUNK):
+                part = slice(start, start + CHUNK)
+                delta = column_in[held, 1, part, :]
+                for low in range(0, window, 128):
+                    size = min(128, window - low)
+                    span = slice(low, low + size)
+                    value = raw_in[held, part, span] * (d_scr[base + unit, part, span] - delta[:, :size])
+                    p_scr[base + unit, part, span] = value.astype(BF16)
+        for unit, (slot, pair) in enumerate(units):
+            lanes, kind = lanes_at(group, pair), kinds[slot]
+            scale = column_in[group * len(units) + unit, 0] * SCALE
+            wide = nn(p_scr[base + unit], keys.window(kind, lanes)) * scale
+            grad_q = head_lanes(wide, lane_head).astype(BF16)
+            dq[row_of(kind, rows), :, :, lanes] = grad_q.reshape(columns, frames, PAIR)
+
+    products(0)
+    for group in range(width // PART):
+        if group + 1 < width // PART:
+            products(group + 1)
+        finish(group)
 
 
 def backward_kernel(layout, kinds, *refs):
@@ -470,12 +586,25 @@
         flops=work * inner, exps=exps * inner, scratch=scratches(RING, 2), limit=14 << 20,
     )
     rim_at = len(ins)
-    ins = ins + kv_rims + [core_rims] + k_rims_of + v_far + list(inner_out)
-    layout = {"n_in": len(ins), "own": 0, "k": gathered(1, rim_at, 0), "v": gathered(1, rim_at, 1)}
-    attended, dq, stats = call(
-        functools.partial(forward_kernel, layout, edge_kinds, inner_kinds),
-        [line(rows), line(rows), stat(rows)], ins + [mask_f],
-        flops=work * 2, exps=exps * 2, scratch=scratches(RING, 2), limit=14 << 20,
+    inner_att, inner_dq, inner_stats = inner_out
+    base = ins + kv_rims + [core_rims] + k_rims_of + v_far
+    found = {"own": 0, "k": gathered(1, rim_at, 0), "v": gathered(1, rim_at, 1)}
+    ins = base + [inner_att, inner_stats]
+    layout = {"n_in": len(ins), **found}
+    jobs = groups * PAIRS * 2
+    kept = [struct(jobs, 2 * tokens, window, dtype=F32), struct(jobs, 2, 2 * tokens, 128, dtype=F32)]
+    piece = lambda n, dtype: pltpu.VMEM((n, 2 * tokens, window), dtype)
+    attended, stats, *kept = call(
+        functools.partial(forward_edge_kernel, layout, edge_kinds, inner_kinds),
+        [line(rows), stat(rows)] + kept, ins + [mask_f],
+        flops=work, exps=exps * 2, scratch=[piece(2 * PAIRS, F32), piece(2 * PAIRS, BF16)], limit=10 << 20,
+    )
+    ins = base + [inner_dq] + kept
+    layout = {"n_in": len(ins), **found}
+    (dq,) = call(
+        functools.partial(forward_grad_kernel, layout, edge_kinds, inner_kinds),
+        [line(rows)], ins,
+        flops=work, scratch=[piece(4 * PAIRS, F32), piece(4 * PAIRS, BF16)], limit=10 << 20,
     )
     ss = [stats] + swaps(stats, bits)
 

time: 59.9 us -> 59.8 us (level)
  waiting for transfers between devices: 16.7 us -> 13.4 us
  starting transfers between devices: 20.2 us -> 22.6 us
  Pallas kernels: 21.3 us -> 22 us
    ppermute x12, waiting for transfers between devices: 14 us -> 9.43 us  [swap(): lax.ppermute(value, 'frame', [(i, i ^ 1 << bit) for i in range(size)])]
    ppermute x6, starting transfers between devices: 9.87 us -> 12.7 us  [exchange(): return lax.ppermute(value, 'space', pairs)]
    ppermute x6, waiting for transfers between devices: 2.71 us -> 3.97 us  [exchange(): return lax.ppermute(value, 'space', pairs)]
    pallas_call x10 -> x11, Pallas kernels: 21.3 us -> 22 us  [call(): pl.pallas_call(kernel, out_shape=tuple((o if i in to_hbm else pltpu.VMEM(...]
  transfers between devices with their start and end apart: 18 -> 18, of which waited for: 5 -> 6; matrix products, arithmetic and copies ran while one was open for 0% -> 0% of each run, Pallas kernels for 29% -> 31%
where the time goes in v3:
time: 59.8 us; the launch traced here: 59.5 us
  starting transfers between devices  22.6 us (38%)
  Pallas kernels  22 us (37%)
  waiting for transfers between devices  13.4 us (22%)
  between operations  0.77 us (1%)
  local copies, waits for them, and re-layouts  0.68 us (1%)
    pallas_call x11, Pallas kernels, call(): pl.pallas_call(kernel, out_shape=tuple((o if i in to_hbm else pltpu.VMEM(...  22 us
    ppermute x6, starting transfers between devices, exchange(): return lax.ppermute(value, 'space', pairs)  12.7 us
    ppermute x12, starting transfers between devices, swap(): lax.ppermute(value, 'frame', [(i, i ^ 1 << bit) for i in range(size)])  9.86 us
    ppermute x12, waiting for transfers between devices, swap(): lax.ppermute(value, 'frame', [(i, i ^ 1 << bit) for i in range(size)])  9.43 us
    ppermute x6, waiting for transfers between devices, exchange(): return lax.ppermute(value, 'space', pairs)  3.97 us
  transfers between devices with their start and end apart: 18, of which 6 were waited for; matrix products, arithmetic and copies ran while one was open for 0% of the time, Pallas kernels for 31%

profile of v3, /device:TPU:0, one launch (start us, length us, event | category | flops | bytes accessed | tf_op | source)
XLA Modules:
  0.0 59.5 jit_solution(13838357194494071304)
XLA Ops:
  0.6 1.2 %shard_map.84 = (bf16[6,48,1024]{2,1,0:T(8,128)(2,1)S(1)}, bf16[2,48,1024]{2,1,0:T(8,128)(2,1)S(1)}, bf16[2,48,1024]{2,1,0:T(8,128)(2,1)S(1)}) custom-call(bf16[3,12,4,1024]{3,2,1,0:T(4,128)(2,1)} %bitcast.12, bf16[3,12,4,1024]{3,2,1,0:T(4,128)(2,1)} %bitcast.13), custom_call_target="tpu_custom_call" | custom-call | bytes 1572864 | tf_op jit(solution)/shard_map/pallas_call | solution.py:52
  1.9 3.1 %collective-permute-start.5 = (bf16[6,48,1024]{2,1,0:T(8,128)(2,1)S(1)}, bf16[6,48,1024]{2,1,0:T(8,128)(2,1)S(1)}, u32[]{:S(2)}, u32[]{:S(2)}) collective-permute-start(bf16[6,48,1024]{2,1,0:T(8,128)(2,1)S(1)} %get-tuple-element.28.refs_1_.refs_0_), channel_id=1, source_target_pairs={{0,16},{4,20},{8,24},{12,28},{16,0},{20,4},{24,8},{28,12},{1,17},{... | collective-permute-start | bytes 1769480 | tf_op jit(solution)/shard_map/ppermute | solution.py:25
  4.9 1.5 %collective-permute-start.4 = (bf16[6,48,1024]{2,1,0:T(8,128)(2,1)S(1)}, bf16[6,48,1024]{2,1,0:T(8,128)(2,1)S(1)}, u32[]{:S(2)}, u32[]{:S(2)}) collective-permute-start(bf16[6,48,1024]{2,1,0:T(8,128)(2,1)S(1)} %get-tuple-element.28.refs_1_.refs_0_), channel_id=1, source_target_pairs={{0,8},{4,12},{8,0},{12,4},{16,24},{20,28},{24,16},{28,20},{1,9},{5... | collective-permute-start | bytes 1769480 | tf_op jit(solution)/shard_map/ppermute | solution.py:25
  6.4 0.7 %collective-permute-start.7 = (bf16[2,48,1024]{2,1,0:T(8,128)(2,1)S(1)}, bf16[2,48,1024]{2,1,0:T(8,128)(2,1)S(1)}, u32[]{:S(2)}, u32[]{:S(2)}) collective-permute-start(bf16[2,48,1024]{2,1,0:T(8,128)(2,1)S(1)} %get-tuple-element.31), channel_id=1, source_target_pairs={{1,2},{2,1},{5,6},{6,5},{9,10},{10,9},{13,14},{14,13},{17,18},{18,... | collective-permute-start | bytes 589832 | tf_op jit(solution)/shard_map/ppermute | solution.py:36
  7.1 4.5 %collective-permute-start.6 = (bf16[2,48,1024]{2,1,0:T(8,128)(2,1)S(1)}, bf16[2,48,1024]{2,1,0:T(8,128)(2,1)S(1)}, u32[]{:S(2)}, u32[]{:S(2)}) collective-permute-start(bf16[2,48,1024]{2,1,0:T(8,128)(2,1)S(1)} %get-tuple-element.29.refs_2_.after), channel_id=1, source_target_pairs={{0,1},{1,0},{2,3},{3,2},{4,5},{5,4},{6,7},{7,6},{8,9},{9,8},{10,11... | collective-permute-start | bytes 589832 | tf_op jit(solution)/shard_map/ppermute | solution.py:36
  11.5 0.0 copy-start
  11.5 0.7 %copy-done = s32[32,3]{0,1:T(4,128)S(1)} copy-done((s32[32,3]{0,1:T(4,128)S(1)}, s32[32,3]{0,1:T(4,128)}, u32[]{:S(2)}) %copy-start) | copy-done | bytes 408
  12.2 0.6 %shard_map.86 = (f32[3,8,192]{2,1,0:T(8,128)S(1)}, f32[1,8,192]{2,1,0:T(8,128)S(1)}) custom-call(bf16[2,48,1024]{2,1,0:T(8,128)(2,1)S(1)} %get-tuple-element.29.refs_2_.after, s32[3,32]{1,0:T(4,128)S(1)} %bitcast.9), custom_call_target="tpu_custom_call" | custom-call | bytes 221184 | tf_op jit(solution)/shard_map/pallas_call | solution.py:52
  12.9 0.0 collective-permute-done.7.side1.refs_6_.refs_10_
  12.9 2.7 %collective-permute-done.6.side0.refs_5_.refs_9_ = bf16[2,48,1024]{2,1,0:T(8,128)(2,1)S(1)} collective-permute-done((bf16[2,48,1024]{2,1,0:T(8,128)(2,1)S(1)}, bf16[2,48,1024]{2,1,0:T(8,128)(2,1)S(1)}, u32[]{:S(2)}, u32[]{:S(2)}) %collective-permute-start.6) | collective-permute-done | bytes 196640 | tf_op jit(solution)/shard_map/ppermute | solution.py:36
  15.6 0.6 collective-permute-start.10
  16.2 0.0 collective-permute-start.3
  16.2 0.5 collective-permute-start.9
  16.7 5.7 %collective-permute-done.10.refs_9_ = bf16[2,48,1024]{2,1,0:T(8,128)(2,1)S(1)} collective-permute-done((bf16[2,48,1024]{2,1,0:T(8,128)(2,1)S(1)}, bf16[2,48,1024]{2,1,0:T(8,128)(2,1)S(1)}, u32[]{:S(2)}, u32[]{:S(2)}) %collective-permute-start.10) | collective-permute-done | bytes 196640 | tf_op jit(solution)/shard_map/ppermute | solution.py:25
  22.5 0.0 collective-permute-start.8
  22.5 2.0 %shard_map.85 = (bf16[6,48,1024]{2,1,0:T(8,128)(2,1)S(1)}, bf16[2,48,1024]{2,1,0:T(8,128)(2,1)}, bf16[2,48,1024]{2,1,0:T(8,128)(2,1)}) custom-call(bf16[3,12,4,1024]{3,2,1,0:T(4,128)(2,1)} %bitcast.10, bf16[3,12,4,1024]{3,2,1,0:T(4,128)(2,1)} %bitcast.11, bf16[2,48,1024]{2,1,0:T(8,128)(2,1)S(1)} %get-tuple-element.29.refs_2_.after), custom_call_target="tpu_custom_call" | custom-call | bytes 1769472 | tf_op jit(solution)/shard_map/pallas_call | solution.py:52
  24.4 0.0 collective-permute-done.9.refs_8_
  24.4 1.8 %collective-permute-start.2 = (bf16[6,48,1024]{2,1,0:T(8,128)(2,1)S(1)}, bf16[6,48,1024]{2,1,0:T(8,128)(2,1)S(1)}, u32[]{:S(2)}, u32[]{:S(2)}) collective-permute-start(bf16[6,48,1024]{2,1,0:T(8,128)(2,1)S(1)} %get-tuple-element.30.refs_0_.refs_1_), channel_id=1, source_target_pairs={{0,16},{4,20},{8,24},{12,28},{16,0},{20,4},{24,8},{28,12},{1,17},{... | collective-permute-start | bytes 1769480 | tf_op jit(solution)/shard_map/ppermute | solution.py:25
  26.2 0.0 collective-permute-done.5.refs_1_.refs_4_
  26.2 1.5 %collective-permute-start.1 = (bf16[6,48,1024]{2,1,0:T(8,128)(2,1)S(1)}, bf16[6,48,1024]{2,1,0:T(8,128)(2,1)S(1)}, u32[]{:S(2)}, u32[]{:S(2)}) collective-permute-start(bf16[6,48,1024]{2,1,0:T(8,128)(2,1)S(1)} %get-tuple-element.30.refs_0_.refs_1_), channel_id=1, source_target_pairs={{0,8},{4,12},{8,0},{12,4},{16,24},{20,28},{24,16},{28,20},{1,9},{5... | collective-permute-start | bytes 1769480 | tf_op jit(solution)/shard_map/ppermute | solution.py:25
  27.7 0.0 collective-permute-done.4.refs_0_.refs_3_
  27.7 0.0 collective-permute-start
  27.8 0.0 collective-permute-done.8.refs_7_
  27.8 1.6 %collective-permute-start.11 = (bf16[2,48,1024]{2,1,0:T(8,128)(2,1)S(1)}, bf16[2,48,1024]{2,1,0:T(8,128)(2,1)S(1)}, u32[]{:S(2)}, u32[]{:S(2)}) collective-permute-start(bf16[2,48,1024]{2,1,0:T(8,128)(2,1)S(1)} %get-tuple-element.35), channel_id=1, source_target_pairs={{0,1},{1,0},{2,3},{3,2},{4,5},{5,4},{6,7},{7,6},{8,9},{9,8},{10,11... | collective-permute-start | bytes 589832 | tf_op jit(solution)/shard_map/ppermute | solution.py:36
  29.4 0.0 collective-permute-done.3.refs_2_
  29.4 0.7 %collective-permute-start.12 = (bf16[2,48,1024]{2,1,0:T(8,128)(2,1)S(1)}, bf16[2,48,1024]{2,1,0:T(8,128)(2,1)S(1)}, u32[]{:S(2)}, u32[]{:S(2)}) collective-permute-start(bf16[2,48,1024]{2,1,0:T(8,128)(2,1)S(1)} %get-tuple-element.36), channel_id=1, source_target_pairs={{1,2},{2,1},{5,6},{6,5},{9,10},{10,9},{13,14},{14,13},{17,18},{18,... | collective-permute-start | bytes 589832 | tf_op jit(solution)/shard_map/ppermute | solution.py:36
  30.1 3.8 %shard_map.89 = (bf16[1,12,4,1024]{3,2,1,0:T(4,128)(2,1)S(1)}, bf16[1,12,4,1024]{3,2,1,0:T(4,128)(2,1)S(1)}, f32[1,4,8,48]{3,2,1,0:T(8,128)S(1)}) custom-call(bf16[6,48,1024]{2,1,0:T(8,128)(2,1)S(1)} %get-tuple-element.30.refs_0_.refs_1_, bf16[6,48,1024]{2,1,0:T(8,128)(2,1)S(1)} %get-tuple-element.28.refs_1_.refs_0_, ...), custom_call_target="tpu_custom_call" | custom-call | flops 452984832 | bytes 3170304 | tf_op jit(solution)/shard_map/pallas_call | solution.py:52
  33.9 1.2 %collective-permute-done.11.refs_10_ = bf16[2,48,1024]{2,1,0:T(8,128)(2,1)S(1)} collective-permute-done((bf16[2,48,1024]{2,1,0:T(8,128)(2,1)S(1)}, bf16[2,48,1024]{2,1,0:T(8,128)(2,1)S(1)}, u32[]{:S(2)}, u32[]{:S(2)}) %collective-permute-start.11) | collective-permute-done | bytes 196640 | tf_op jit(solution)/shard_map/ppermute | solution.py:36
  35.2 0.0 collective-permute-done.12.refs_11_
  35.2 4.8 %shard_map.90 = (bf16[3,12,4,1024]{3,2,1,0:T(4,128)(2,1)S(1)}, f32[3,4,8,48]{3,2,1,0:T(8,128)S(1)}, f32[16,96,576]{2,1,0:T(8,128)S(1)}, f32[16,2,96,128]{3,2,1,0:T(8,128)S(1)}) custom-call(bf16[6,48,1024]{2,1,0:T(8,128)(2,1)S(1)} %get-tuple-element.30.refs_0_.refs_1_, bf16[6,48,1024]{2,1,0:T(8,128)(2,1)S(1)} %get-tuple-element.28.refs_1_.refs_0_, ...), custom_call_target="tpu_custom_call" | custom-call | flops 452984832 | bytes 10070016 | tf_op jit(solution)/shard_map/pallas_call | solution.py:52
  40.0 0.5 collective-permute-start.15
  40.5 0.4 collective-permute-start.14
  40.9 0.0 collective-permute-done.2.refs_4_
  40.9 0.0 collective-permute-start.13
  40.9 0.9 %collective-permute-done.1.refs_3_ = bf16[6,48,1024]{2,1,0:T(8,128)(2,1)S(1)} collective-permute-done((bf16[6,48,1024]{2,1,0:T(8,128)(2,1)S(1)}, bf16[6,48,1024]{2,1,0:T(8,128)(2,1)S(1)}, u32[]{:S(2)}, u32[]{:S(2)}) %collective-permute-start.1) | collective-permute-done | bytes 589856 | tf_op jit(solution)/shard_map/ppermute | solution.py:25
  41.7 0.0 collective-permute-done.refs_2_
  41.7 2.4 %collective-permute-done.15.refs_8_ = f32[3,4,8,48]{3,2,1,0:T(8,128)S(1)} collective-permute-done((f32[3,4,8,48]{3,2,1,0:T(8,128)S(1)}, f32[3,4,8,48]{3,2,1,0:T(8,128)S(1)}, u32[]{:S(2)}, u32[]{:S(2)}) %collective-permute-start.15) | collective-permute-done | bytes 18464 | tf_op jit(solution)/shard_map/ppermute | solution.py:25
  44.1 0.5 collective-permute-done.14.refs_7_
  44.6 0.0 collective-permute-done.13.refs_6_
  44.6 1.8 %shard_map.93 = (bf16[2,48,1024]{2,1,0:T(8,128)(2,1)S(1)}, bf16[2,48,1024]{2,1,0:T(8,128)(2,1)S(1)}) custom-call(bf16[6,48,1024]{2,1,0:T(8,128)(2,1)S(1)} %get-tuple-element.28.refs_1_.refs_0_, bf16[6,48,1024]{2,1,0:T(8,128)(2,1)S(1)} %get-tuple-element.30.refs_0_.refs_1_, bf16[6,48,1024]{2,1,0:T(8,128)(2,1)S(1)} %collective-permute-done.refs_2_, ...), custom_call_target="tpu_custom_call" | custom-call | flops 452984832 | bytes 3815424 | tf_op jit(solution)/shard_map/pallas_call | solution.py:52
  46.4 4.7 %collective-permute-start.16 = (bf16[2,48,1024]{2,1,0:T(8,128)(2,1)S(1)}, bf16[2,48,1024]{2,1,0:T(8,128)(2,1)S(1)}, u32[]{:S(2)}, u32[]{:S(2)}) collective-permute-start(bf16[2,48,1024]{2,1,0:T(8,128)(2,1)S(1)} %get-tuple-element.48), channel_id=1, source_target_pairs={{0,1},{1,0},{2,3},{3,2},{4,5},{5,4},{6,7},{7,6},{8,9},{9,8},{10,11... | collective-permute-start | bytes 589832 | tf_op jit(solution)/shard_map/ppermute | solution.py:36
  51.0 0.7 %collective-permute-start.17 = (bf16[2,48,1024]{2,1,0:T(8,128)(2,1)S(1)}, bf16[2,48,1024]{2,1,0:T(8,128)(2,1)S(1)}, u32[]{:S(2)}, u32[]{:S(2)}) collective-permute-start(bf16[2,48,1024]{2,1,0:T(8,128)(2,1)S(1)} %get-tuple-element.49), channel_id=1, source_target_pairs={{1,2},{2,1},{5,6},{6,5},{9,10},{10,9},{13,14},{14,13},{17,18},{18,... | collective-permute-start | bytes 589832 | tf_op jit(solution)/shard_map/ppermute | solution.py:36
  51.7 1.9 %shard_map.91.refs_12_ = bf16[3,12,4,1024]{3,2,1,0:T(4,128)(2,1)S(1)} custom-call(bf16[6,48,1024]{2,1,0:T(8,128)(2,1)S(1)} %get-tuple-element.30.refs_0_.refs_1_, bf16[6,48,1024]{2,1,0:T(8,128)(2,1)S(1)} %get-tuple-element.28.refs_1_.refs_0_, bf16[6,48,1024]{2,1,0:T(8,128)(2,1)S(1)} %collective-permute-done.3.refs_2_, ...), custom_call_target="tpu_custom_call" | custom-call | flops 452984832 | bytes 10027008 | tf_op jit(solution)/shard_map/pallas_call | solution.py:52
  53.6 5.0 %shard_map.92 = (f32[6,48,1024]{2,1,0:T(8,128)S(1)}, bf16[3,12,4,1024]{3,2,1,0:T(4,128)(2,1)}, bf16[3,12,4,1024]{3,2,1,0:T(4,128)(2,1)}) custom-call(bf16[6,48,1024]{2,1,0:T(8,128)(2,1)S(1)} %get-tuple-element.28.refs_1_.refs_0_, bf16[6,48,1024]{2,1,0:T(8,128)(2,1)S(1)} %get-tuple-element.30.refs_0_.refs_1_, ...), custom_call_target="tpu_custom_call" | custom-call | flops 905969664 | bytes 5781504 | tf_op jit(solution)/shard_map/pallas_call | solution.py:52
  58.6 0.0 collective-permute-done.16.part0
  58.6 0.0 collective-permute-done.17.part1
  58.6 0.9 %shard_map.94 = (bf16[3,12,4,1024]{3,2,1,0:T(4,128)(2,1)}, bf16[3,12,4,1024]{3,2,1,0:T(4,128)(2,1)}) custom-call(f32[6,48,1024]{2,1,0:T(8,128)S(1)} %get-tuple-element.47.total, bf16[2,48,1024]{2,1,0:T(8,128)(2,1)S(1)} %collective-permute-done.16.part0, bf16[2,48,1024]{2,1,0:T(8,128)(2,1)S(1)} %collective-permute-done.17.part1), custom_call_target="tpu_custom_call" | custom-call | bytes 2162688 | tf_op jit(solution)/shard_map/pallas_call | solution.py:52
  (2 shorter events, 0.1 us)
Async XLA Ops:
  1.9 24.4 %collective-permute-start.5 = (bf16[6,48,1024]{2,1,0:T(8,128)(2,1)S(1)}, bf16[6,48,1024]{2,1,0:T(8,128)(2,1)S(1)}, u32[]{:S(2)}, u32[]{:S(2)}) collective-permute-start(bf16[6,48,1024]{2,1,0:T(8,128)(2,1)S(1)} %get-tuple-element.28.refs_1_.refs_0_), channel_id=1, source_target_pairs={{0,16},{4,20},{8,24},{12,28},{16,0},{20,4},{24,8},{28,12},{1,17},{... | collective-permute-start | bytes 1769480 | tf_op jit(solution)/shard_map/ppermute | solution.py:25
  4.9 22.8 %collective-permute-start.4 = (bf16[6,48,1024]{2,1,0:T(8,128)(2,1)S(1)}, bf16[6,48,1024]{2,1,0:T(8,128)(2,1)S(1)}, u32[]{:S(2)}, u32[]{:S(2)}) collective-permute-start(bf16[6,48,1024]{2,1,0:T(8,128)(2,1)S(1)} %get-tuple-element.28.refs_1_.refs_0_), channel_id=1, source_target_pairs={{0,8},{4,12},{8,0},{12,4},{16,24},{20,28},{24,16},{28,20},{1,9},{5... | collective-permute-start | bytes 1769480 | tf_op jit(solution)/shard_map/ppermute | solution.py:25
  6.4 6.4 %collective-permute-start.7 = (bf16[2,48,1024]{2,1,0:T(8,128)(2,1)S(1)}, bf16[2,48,1024]{2,1,0:T(8,128)(2,1)S(1)}, u32[]{:S(2)}, u32[]{:S(2)}) collective-permute-start(bf16[2,48,1024]{2,1,0:T(8,128)(2,1)S(1)} %get-tuple-element.31), channel_id=1, source_target_pairs={{1,2},{2,1},{5,6},{6,5},{9,10},{10,9},{13,14},{14,13},{17,18},{18,... | collective-permute-start | bytes 589832 | tf_op jit(solution)/shard_map/ppermute | solution.py:36
  7.1 8.5 %collective-permute-start.6 = (bf16[2,48,1024]{2,1,0:T(8,128)(2,1)S(1)}, bf16[2,48,1024]{2,1,0:T(8,128)(2,1)S(1)}, u32[]{:S(2)}, u32[]{:S(2)}) collective-permute-start(bf16[2,48,1024]{2,1,0:T(8,128)(2,1)S(1)} %get-tuple-element.29.refs_2_.after), channel_id=1, source_target_pairs={{0,1},{1,0},{2,3},{3,2},{4,5},{5,4},{6,7},{7,6},{8,9},{9,8},{10,11... | collective-permute-start | bytes 589832 | tf_op jit(solution)/shard_map/ppermute | solution.py:36
  11.5 0.7 %copy-start = (s32[32,3]{0,1:T(4,128)S(1)}, s32[32,3]{0,1:T(4,128)}, u32[]{:S(2)}) copy-start(s32[32,3]{0,1:T(4,128)} %param.9) | copy-start | bytes 1156
  15.6 6.8 %collective-permute-start.10 = (bf16[2,48,1024]{2,1,0:T(8,128)(2,1)S(1)}, bf16[2,48,1024]{2,1,0:T(8,128)(2,1)S(1)}, u32[]{:S(2)}, u32[]{:S(2)}) collective-permute-start(bf16[2,48,1024]{2,1,0:T(8,128)(2,1)S(1)} %get-tuple-element.34), channel_id=1, source_target_pairs={{0,16},{4,20},{8,24},{12,28},{16,0},{20,4},{24,8},{28,12},{1,17},{... | collective-permute-start | bytes 589832 | tf_op jit(solution)/shard_map/ppermute | solution.py:25
  16.2 13.2 %collective-permute-start.3 = (bf16[6,48,1024]{2,1,0:T(8,128)(2,1)S(1)}, bf16[6,48,1024]{2,1,0:T(8,128)(2,1)S(1)}, u32[]{:S(2)}, u32[]{:S(2)}) collective-permute-start(bf16[6,48,1024]{2,1,0:T(8,128)(2,1)S(1)} %get-tuple-element.28.refs_1_.refs_0_), channel_id=1, source_target_pairs={{0,4},{4,0},{8,12},{12,8},{16,20},{20,16},{24,28},{28,24},{1,5},{5... | collective-permute-start | bytes 1769480 | tf_op jit(solution)/shard_map/ppermute | solution.py:25
  16.2 8.2 %collective-permute-start.9 = (bf16[2,48,1024]{2,1,0:T(8,128)(2,1)S(1)}, bf16[2,48,1024]{2,1,0:T(8,128)(2,1)S(1)}, u32[]{:S(2)}, u32[]{:S(2)}) collective-permute-start(bf16[2,48,1024]{2,1,0:T(8,128)(2,1)S(1)} %get-tuple-element.34), channel_id=1, source_target_pairs={{0,8},{4,12},{8,0},{12,4},{16,24},{20,28},{24,16},{28,20},{1,9},{5... | collective-permute-start | bytes 589832 | tf_op jit(solution)/shard_map/ppermute | solution.py:25
  22.5 5.3 %collective-permute-start.8 = (bf16[4,48,1024]{2,1,0:T(8,128)(2,1)S(1)}, bf16[4,48,1024]{2,1,0:T(8,128)(2,1)S(1)}, u32[]{:S(2)}, u32[]{:S(2)}) collective-permute-start(bf16[4,48,1024]{2,1,0:T(8,128)(2,1)S(1)} %get-tuple-element.33), channel_id=1, source_target_pairs={{0,4},{4,0},{8,12},{12,8},{16,20},{20,16},{24,28},{28,24},{1,5},{5... | collective-permute-start | bytes 1179656 | tf_op jit(solution)/shard_map/ppermute | solution.py:25
  24.4 16.4 %collective-permute-start.2 = (bf16[6,48,1024]{2,1,0:T(8,128)(2,1)S(1)}, bf16[6,48,1024]{2,1,0:T(8,128)(2,1)S(1)}, u32[]{:S(2)}, u32[]{:S(2)}) collective-permute-start(bf16[6,48,1024]{2,1,0:T(8,128)(2,1)S(1)} %get-tuple-element.30.refs_0_.refs_1_), channel_id=1, source_target_pairs={{0,16},{4,20},{8,24},{12,28},{16,0},{20,4},{24,8},{28,12},{1,17},{... | collective-permute-start | bytes 1769480 | tf_op jit(solution)/shard_map/ppermute | solution.py:25
  26.2 15.5 %collective-permute-start.1 = (bf16[6,48,1024]{2,1,0:T(8,128)(2,1)S(1)}, bf16[6,48,1024]{2,1,0:T(8,128)(2,1)S(1)}, u32[]{:S(2)}, u32[]{:S(2)}) collective-permute-start(bf16[6,48,1024]{2,1,0:T(8,128)(2,1)S(1)} %get-tuple-element.30.refs_0_.refs_1_), channel_id=1, source_target_pairs={{0,8},{4,12},{8,0},{12,4},{16,24},{20,28},{24,16},{28,20},{1,9},{5... | collective-permute-start | bytes 1769480 | tf_op jit(solution)/shard_map/ppermute | solution.py:25
  27.7 14.0 %collective-permute-start = (bf16[6,48,1024]{2,1,0:T(8,128)(2,1)S(1)}, bf16[6,48,1024]{2,1,0:T(8,128)(2,1)S(1)}, u32[]{:S(2)}, u32[]{:S(2)}) collective-permute-start(bf16[6,48,1024]{2,1,0:T(8,128)(2,1)S(1)} %get-tuple-element.30.refs_0_.refs_1_), channel_id=1, source_target_pairs={{0,4},{4,0},{8,12},{12,8},{16,20},{20,16},{24,28},{28,24},{1,5},{5... | collective-permute-start | bytes 1769480 | tf_op jit(solution)/shard_map/ppermute | solution.py:25
  27.8 7.4 %collective-permute-start.11 = (bf16[2,48,1024]{2,1,0:T(8,128)(2,1)S(1)}, bf16[2,48,1024]{2,1,0:T(8,128)(2,1)S(1)}, u32[]{:S(2)}, u32[]{:S(2)}) collective-permute-start(bf16[2,48,1024]{2,1,0:T(8,128)(2,1)S(1)} %get-tuple-element.35), channel_id=1, source_target_pairs={{0,1},{1,0},{2,3},{3,2},{4,5},{5,4},{6,7},{7,6},{8,9},{9,8},{10,11... | collective-permute-start | bytes 589832 | tf_op jit(solution)/shard_map/ppermute | solution.py:36
  29.4 5.7 %collective-permute-start.12 = (bf16[2,48,1024]{2,1,0:T(8,128)(2,1)S(1)}, bf16[2,48,1024]{2,1,0:T(8,128)(2,1)S(1)}, u32[]{:S(2)}, u32[]{:S(2)}) collective-permute-start(bf16[2,48,1024]{2,1,0:T(8,128)(2,1)S(1)} %get-tuple-element.36), channel_id=1, source_target_pairs={{1,2},{2,1},{5,6},{6,5},{9,10},{10,9},{13,14},{14,13},{17,18},{18,... | collective-permute-start | bytes 589832 | tf_op jit(solution)/shard_map/ppermute | solution.py:36
  40.0 4.1 %collective-permute-start.15 = (f32[3,4,8,48]{3,2,1,0:T(8,128)S(1)}, f32[3,4,8,48]{3,2,1,0:T(8,128)S(1)}, u32[]{:S(2)}, u32[]{:S(2)}) collective-permute-start(f32[3,4,8,48]{3,2,1,0:T(8,128)S(1)} %get-tuple-element.40.refs_5_), channel_id=1, source_target_pairs={{0,16},{4,20},{8,24},{12,28},{16,0},{20,4},{24,8},{28,12},{1,17},{... | collective-permute-start | bytes 55304 | tf_op jit(solution)/shard_map/ppermute | solution.py:25
  40.5 4.1 %collective-permute-start.14 = (f32[3,4,8,48]{3,2,1,0:T(8,128)S(1)}, f32[3,4,8,48]{3,2,1,0:T(8,128)S(1)}, u32[]{:S(2)}, u32[]{:S(2)}) collective-permute-start(f32[3,4,8,48]{3,2,1,0:T(8,128)S(1)} %get-tuple-element.40.refs_5_), channel_id=1, source_target_pairs={{0,8},{4,12},{8,0},{12,4},{16,24},{20,28},{24,16},{28,20},{1,9},{5... | collective-permute-start | bytes 55304 | tf_op jit(solution)/shard_map/ppermute | solution.py:25
  40.9 3.7 %collective-permute-start.13 = (f32[3,4,8,48]{3,2,1,0:T(8,128)S(1)}, f32[3,4,8,48]{3,2,1,0:T(8,128)S(1)}, u32[]{:S(2)}, u32[]{:S(2)}) collective-permute-start(f32[3,4,8,48]{3,2,1,0:T(8,128)S(1)} %get-tuple-element.40.refs_5_), channel_id=1, source_target_pairs={{0,4},{4,0},{8,12},{12,8},{16,20},{20,16},{24,28},{28,24},{1,5},{5... | collective-permute-start | bytes 55304 | tf_op jit(solution)/shard_map/ppermute | solution.py:25
  46.4 12.2 %collective-permute-start.16 = (bf16[2,48,1024]{2,1,0:T(8,128)(2,1)S(1)}, bf16[2,48,1024]{2,1,0:T(8,128)(2,1)S(1)}, u32[]{:S(2)}, u32[]{:S(2)}) collective-permute-start(bf16[2,48,1024]{2,1,0:T(8,128)(2,1)S(1)} %get-tuple-element.48), channel_id=1, source_target_pairs={{0,1},{1,0},{2,3},{3,2},{4,5},{5,4},{6,7},{7,6},{8,9},{9,8},{10,11... | collective-permute-start | bytes 589832 | tf_op jit(solution)/shard_map/ppermute | solution.py:36
  51.0 7.6 %collective-permute-start.17 = (bf16[2,48,1024]{2,1,0:T(8,128)(2,1)S(1)}, bf16[2,48,1024]{2,1,0:T(8,128)(2,1)S(1)}, u32[]{:S(2)}, u32[]{:S(2)}) collective-permute-start(bf16[2,48,1024]{2,1,0:T(8,128)(2,1)S(1)} %get-tuple-element.49), channel_id=1, source_target_pairs={{1,2},{2,1},{5,6},{6,5},{9,10},{10,9},{13,14},{14,13},{17,18},{18,... | collective-permute-start | bytes 589832 | tf_op jit(solution)/shard_map/ppermute | solution.py:36

commit v4 on v3

--- a/solution.py
+++ b/solution.py
@@ -16,6 +16,8 @@
 PART = PAIRS * PAIR
 CHUNK = 16
 RING = 4
+LOOP_GRAD = False
+LOOP_OWN = True
 BF16 = jnp.bfloat16
 F32 = jnp.float32
 
@@ -126,7 +128,26 @@
 
 def lanes_at(group, pair):
     start = group * PART + pair * PAIR
-    return slice(start, start + PAIR)
+    if isinstance(group, int):
+        return slice(start, start + PAIR)
+    return pl.ds(pl.multiple_of(start, PAIR), PAIR)
+
+
+def over_groups(groups, loop, products, finish):
+    if loop:
+
+        def step(group, _):
+            products(group)
+            finish(group)
+            return 0
+
+        lax.fori_loop(0, groups, step, 0)
+        return
+    products(0)
+    for group in range(groups):
+        if group + 1 < groups:
+            products(group + 1)
+        finish(group)
 
 
 def head_rows(value, lane_head):
@@ -377,11 +398,11 @@
         for unit, (slot, pair) in enumerate(units):
             lanes, kind = lanes_at(group, pair), kinds[slot]
             row = row_of(kind, rows)
-            at = (group % 2) * len(units) + unit
+            at = (0 if layout["loop"] else group % 2) * len(units) + unit
             d_scr[at] = nt(head_rows(qg[rows + row, :, lanes], lane_head), values.window(kind, lanes))
 
     def finish(group):
-        base = (group % 2) * len(units)
+        base = (0 if layout["loop"] else group % 2) * len(units)
         for unit, (slot, pair) in enumerate(units):
             held = group * len(units) + unit
             for start in range(0, 2 * tokens, CHUNK):
@@ -399,11 +420,7 @@
             grad_q = head_lanes(wide, lane_head).astype(BF16)
             dq[row_of(kind, rows), :, :, lanes] = grad_q.reshape(columns, frames, PAIR)
 
-    products(0)
-    for group in range(width // PART):
-        if group + 1 < width // PART:
-            products(group + 1)
-        finish(group)
+    over_groups(width // PART, layout["loop"], products, finish)
 
 
 def backward_kernel(layout, kinds, *refs):
@@ -459,7 +476,7 @@
         for unit, (kind, pair) in enumerate(units):
             lanes = lanes_at(group, pair)
             size = len(query_rows(kind)) * part
-            at = (group % 2) * len(units) + unit
+            at = (0 if layout["loop"] else group % 2) * len(units) + unit
             s_scr[at, :, :size] = nt(
                 head_rows(key_rows(kind, 0, lanes) * SCALE, lane_head), window(kind, 0, lanes)
             )
@@ -468,7 +485,7 @@
             )
 
     def finish(group):
-        base = (group % 2) * len(units)
+        base = (0 if layout["loop"] else group % 2) * len(units)
         stats = {
             kind: jnp.concatenate(
                 [ref[slot, group] for _, slot in query_rows(kind) for ref in stats_of], axis=1
@@ -501,11 +518,7 @@
                     row = row_of(kind, rows)
                     outs[0][tensor * rows + row, :, lanes] = value
 
-    products(0)
-    for group in range(width // PART):
-        if group + 1 < width // PART:
-            products(group + 1)
-        finish(group)
+    over_groups(width // PART, layout["loop"], products, finish)
     for copy in copies:
         copy.wait()
 
@@ -600,7 +613,7 @@
         flops=work, exps=exps * 2, scratch=[piece(2 * PAIRS, F32), piece(2 * PAIRS, BF16)], limit=10 << 20,
     )
     ins = base + [inner_dq] + kept
-    layout = {"n_in": len(ins), **found}
+    layout = {"n_in": len(ins), "loop": LOOP_GRAD, **found}
     (dq,) = call(
         functools.partial(forward_grad_kernel, layout, edge_kinds, inner_kinds),
         [line(rows)], ins,
@@ -609,7 +622,7 @@
     ss = [stats] + swaps(stats, bits)
 
     ins = [kv] + qgs + ss + kv_rims
-    layout = {"n_in": len(ins), "count": count, "frames": frames}
+    layout = {"n_in": len(ins), "count": count, "loop": False}
     edge = struct(2, tokens, width)
     parts = call(
         functools.partial(backward_kernel, layout, ["r0", "r1"]),
@@ -619,7 +632,7 @@
     parts = [exchange(value, side) for side, value in enumerate(parts)]
     full = struct(rows, columns, frames, width)
     ins = ins + [attended, dq]
-    layout = {"n_in": len(ins), "count": count, "frames": frames, "held": 2}
+    layout = {"n_in": len(ins), "count": count, "loop": LOOP_OWN, "held": 2}
     total, attended, dq = call(
         functools.partial(backward_kernel, layout, inner_kinds + edge_kinds),
         [struct(2 * rows, tokens, width, dtype=F32), full, full], ins + [mask_b], to_hbm=(1, 2),

time: 59.8 us -> 59.6 us (level)
  transfers between devices with their start and end apart: 18 -> 18, of which waited for: 6 -> 6; matrix products, arithmetic and copies ran while one was open for 0% -> 0% of each run, Pallas kernels for 31% -> 30%
where the time goes in v4:
time: 59.6 us; the launch traced here: 59.3 us
  starting transfers between devices  22.6 us (38%)
  Pallas kernels  21.9 us (37%)
  waiting for transfers between devices  13.4 us (22%)
  between operations  0.77 us (1%)
  local copies, waits for them, and re-layouts  0.68 us (1%)
    pallas_call x11, Pallas kernels, call(): pl.pallas_call(kernel, out_shape=tuple((o if i in to_hbm else pltpu.VMEM(...  21.9 us
    ppermute x6, starting transfers between devices, exchange(): return lax.ppermute(value, 'space', pairs)  12.7 us
    ppermute x12, starting transfers between devices, swap(): lax.ppermute(value, 'frame', [(i, i ^ 1 << bit) for i in range(size)])  9.86 us
    ppermute x12, waiting for transfers between devices, swap(): lax.ppermute(value, 'frame', [(i, i ^ 1 << bit) for i in range(size)])  9.43 us
    ppermute x6, waiting for transfers between devices, exchange(): return lax.ppermute(value, 'space', pairs)  3.97 us
  transfers between devices with their start and end apart: 18, of which 6 were waited for; matrix products, arithmetic and copies ran while one was open for 0% of the time, Pallas kernels for 30%

profile of v4, /device:TPU:0, one launch (start us, length us, event | category | flops | bytes accessed | tf_op | source)
XLA Modules:
  0.0 59.3 jit_solution(10378660125508793192)
XLA Ops:
  0.6 1.2 %shard_map.84 = (bf16[6,48,1024]{2,1,0:T(8,128)(2,1)S(1)}, bf16[2,48,1024]{2,1,0:T(8,128)(2,1)S(1)}, bf16[2,48,1024]{2,1,0:T(8,128)(2,1)S(1)}) custom-call(bf16[3,12,4,1024]{3,2,1,0:T(4,128)(2,1)} %bitcast.12, bf16[3,12,4,1024]{3,2,1,0:T(4,128)(2,1)} %bitcast.13), custom_call_target="tpu_custom_call" | custom-call | bytes 1572864 | tf_op jit(solution)/shard_map/pallas_call | solution.py:54
  1.9 3.1 %collective-permute-start.5 = (bf16[6,48,1024]{2,1,0:T(8,128)(2,1)S(1)}, bf16[6,48,1024]{2,1,0:T(8,128)(2,1)S(1)}, u32[]{:S(2)}, u32[]{:S(2)}) collective-permute-start(bf16[6,48,1024]{2,1,0:T(8,128)(2,1)S(1)} %get-tuple-element.28.refs_1_.refs_0_), channel_id=1, source_target_pairs={{0,16},{4,20},{8,24},{12,28},{16,0},{20,4},{24,8},{28,12},{1,17},{... | collective-permute-start | bytes 1769480 | tf_op jit(solution)/shard_map/ppermute | solution.py:27
  4.9 1.5 %collective-permute-start.4 = (bf16[6,48,1024]{2,1,0:T(8,128)(2,1)S(1)}, bf16[6,48,1024]{2,1,0:T(8,128)(2,1)S(1)}, u32[]{:S(2)}, u32[]{:S(2)}) collective-permute-start(bf16[6,48,1024]{2,1,0:T(8,128)(2,1)S(1)} %get-tuple-element.28.refs_1_.refs_0_), channel_id=1, source_target_pairs={{0,8},{4,12},{8,0},{12,4},{16,24},{20,28},{24,16},{28,20},{1,9},{5... | collective-permute-start | bytes 1769480 | tf_op jit(solution)/shard_map/ppermute | solution.py:27
  6.4 0.7 %collective-permute-start.7 = (bf16[2,48,1024]{2,1,0:T(8,128)(2,1)S(1)}, bf16[2,48,1024]{2,1,0:T(8,128)(2,1)S(1)}, u32[]{:S(2)}, u32[]{:S(2)}) collective-permute-start(bf16[2,48,1024]{2,1,0:T(8,128)(2,1)S(1)} %get-tuple-element.31), channel_id=1, source_target_pairs={{1,2},{2,1},{5,6},{6,5},{9,10},{10,9},{13,14},{14,13},{17,18},{18,... | collective-permute-start | bytes 589832 | tf_op jit(solution)/shard_map/ppermute | solution.py:38
  7.1 4.5 %collective-permute-start.6 = (bf16[2,48,1024]{2,1,0:T(8,128)(2,1)S(1)}, bf16[2,48,1024]{2,1,0:T(8,128)(2,1)S(1)}, u32[]{:S(2)}, u32[]{:S(2)}) collective-permute-start(bf16[2,48,1024]{2,1,0:T(8,128)(2,1)S(1)} %get-tuple-element.29.refs_2_.after), channel_id=1, source_target_pairs={{0,1},{1,0},{2,3},{3,2},{4,5},{5,4},{6,7},{7,6},{8,9},{9,8},{10,11... | collective-permute-start | bytes 589832 | tf_op jit(solution)/shard_map/ppermute | solution.py:38
  11.5 0.0 copy-start
  11.5 0.7 %copy-done = s32[32,3]{0,1:T(4,128)S(1)} copy-done((s32[32,3]{0,1:T(4,128)S(1)}, s32[32,3]{0,1:T(4,128)}, u32[]{:S(2)}) %copy-start) | copy-done | bytes 408
  12.2 0.6 %shard_map.86 = (f32[3,8,192]{2,1,0:T(8,128)S(1)}, f32[1,8,192]{2,1,0:T(8,128)S(1)}) custom-call(bf16[2,48,1024]{2,1,0:T(8,128)(2,1)S(1)} %get-tuple-element.29.refs_2_.after, s32[3,32]{1,0:T(4,128)S(1)} %bitcast.9), custom_call_target="tpu_custom_call" | custom-call | bytes 221184 | tf_op jit(solution)/shard_map/pallas_call | solution.py:54
  12.9 0.0 collective-permute-done.7.side1.refs_6_.refs_10_
  12.9 2.7 %collective-permute-done.6.side0.refs_5_.refs_9_ = bf16[2,48,1024]{2,1,0:T(8,128)(2,1)S(1)} collective-permute-done((bf16[2,48,1024]{2,1,0:T(8,128)(2,1)S(1)}, bf16[2,48,1024]{2,1,0:T(8,128)(2,1)S(1)}, u32[]{:S(2)}, u32[]{:S(2)}) %collective-permute-start.6) | collective-permute-done | bytes 196640 | tf_op jit(solution)/shard_map/ppermute | solution.py:38
  15.6 0.6 collective-permute-start.10
  16.2 0.0 collective-permute-start.3
  16.2 0.5 collective-permute-start.9
  16.7 5.7 %collective-permute-done.10.refs_9_ = bf16[2,48,1024]{2,1,0:T(8,128)(2,1)S(1)} collective-permute-done((bf16[2,48,1024]{2,1,0:T(8,128)(2,1)S(1)}, bf16[2,48,1024]{2,1,0:T(8,128)(2,1)S(1)}, u32[]{:S(2)}, u32[]{:S(2)}) %collective-permute-start.10) | collective-permute-done | bytes 196640 | tf_op jit(solution)/shard_map/ppermute | solution.py:27
  22.5 0.0 collective-permute-start.8
  22.5 2.0 %shard_map.85 = (bf16[6,48,1024]{2,1,0:T(8,128)(2,1)S(1)}, bf16[2,48,1024]{2,1,0:T(8,128)(2,1)}, bf16[2,48,1024]{2,1,0:T(8,128)(2,1)}) custom-call(bf16[3,12,4,1024]{3,2,1,0:T(4,128)(2,1)} %bitcast.10, bf16[3,12,4,1024]{3,2,1,0:T(4,128)(2,1)} %bitcast.11, bf16[2,48,1024]{2,1,0:T(8,128)(2,1)S(1)} %get-tuple-element.29.refs_2_.after), custom_call_target="tpu_custom_call" | custom-call | bytes 1769472 | tf_op jit(solution)/shard_map/pallas_call | solution.py:54
  24.4 0.0 collective-permute-done.9.refs_8_
  24.4 1.8 %collective-permute-start.2 = (bf16[6,48,1024]{2,1,0:T(8,128)(2,1)S(1)}, bf16[6,48,1024]{2,1,0:T(8,128)(2,1)S(1)}, u32[]{:S(2)}, u32[]{:S(2)}) collective-permute-start(bf16[6,48,1024]{2,1,0:T(8,128)(2,1)S(1)} %get-tuple-element.30.refs_0_.refs_1_), channel_id=1, source_target_pairs={{0,16},{4,20},{8,24},{12,28},{16,0},{20,4},{24,8},{28,12},{1,17},{... | collective-permute-start | bytes 1769480 | tf_op jit(solution)/shard_map/ppermute | solution.py:27
  26.2 0.0 collective-permute-done.5.refs_1_.refs_4_
  26.2 1.5 %collective-permute-start.1 = (bf16[6,48,1024]{2,1,0:T(8,128)(2,1)S(1)}, bf16[6,48,1024]{2,1,0:T(8,128)(2,1)S(1)}, u32[]{:S(2)}, u32[]{:S(2)}) collective-permute-start(bf16[6,48,1024]{2,1,0:T(8,128)(2,1)S(1)} %get-tuple-element.30.refs_0_.refs_1_), channel_id=1, source_target_pairs={{0,8},{4,12},{8,0},{12,4},{16,24},{20,28},{24,16},{28,20},{1,9},{5... | collective-permute-start | bytes 1769480 | tf_op jit(solution)/shard_map/ppermute | solution.py:27
  27.7 0.0 collective-permute-done.4.refs_0_.refs_3_
  27.7 0.0 collective-permute-start
  27.8 0.0 collective-permute-done.8.refs_7_
  27.8 1.6 %collective-permute-start.11 = (bf16[2,48,1024]{2,1,0:T(8,128)(2,1)S(1)}, bf16[2,48,1024]{2,1,0:T(8,128)(2,1)S(1)}, u32[]{:S(2)}, u32[]{:S(2)}) collective-permute-start(bf16[2,48,1024]{2,1,0:T(8,128)(2,1)S(1)} %get-tuple-element.35), channel_id=1, source_target_pairs={{0,1},{1,0},{2,3},{3,2},{4,5},{5,4},{6,7},{7,6},{8,9},{9,8},{10,11... | collective-permute-start | bytes 589832 | tf_op jit(solution)/shard_map/ppermute | solution.py:38
  29.4 0.0 collective-permute-done.3.refs_2_
  29.4 0.7 %collective-permute-start.12 = (bf16[2,48,1024]{2,1,0:T(8,128)(2,1)S(1)}, bf16[2,48,1024]{2,1,0:T(8,128)(2,1)S(1)}, u32[]{:S(2)}, u32[]{:S(2)}) collective-permute-start(bf16[2,48,1024]{2,1,0:T(8,128)(2,1)S(1)} %get-tuple-element.36), channel_id=1, source_target_pairs={{1,2},{2,1},{5,6},{6,5},{9,10},{10,9},{13,14},{14,13},{17,18},{18,... | collective-permute-start | bytes 589832 | tf_op jit(solution)/shard_map/ppermute | solution.py:38
  30.1 3.8 %shard_map.89 = (bf16[1,12,4,1024]{3,2,1,0:T(4,128)(2,1)S(1)}, bf16[1,12,4,1024]{3,2,1,0:T(4,128)(2,1)S(1)}, f32[1,4,8,48]{3,2,1,0:T(8,128)S(1)}) custom-call(bf16[6,48,1024]{2,1,0:T(8,128)(2,1)S(1)} %get-tuple-element.30.refs_0_.refs_1_, bf16[6,48,1024]{2,1,0:T(8,128)(2,1)S(1)} %get-tuple-element.28.refs_1_.refs_0_, ...), custom_call_target="tpu_custom_call" | custom-call | flops 452984832 | bytes 3170304 | tf_op jit(solution)/shard_map/pallas_call | solution.py:54
  33.9 1.2 %collective-permute-done.11.refs_10_ = bf16[2,48,1024]{2,1,0:T(8,128)(2,1)S(1)} collective-permute-done((bf16[2,48,1024]{2,1,0:T(8,128)(2,1)S(1)}, bf16[2,48,1024]{2,1,0:T(8,128)(2,1)S(1)}, u32[]{:S(2)}, u32[]{:S(2)}) %collective-permute-start.11) | collective-permute-done | bytes 196640 | tf_op jit(solution)/shard_map/ppermute | solution.py:38
  35.2 0.0 collective-permute-done.12.refs_11_
  35.2 4.8 %shard_map.90 = (bf16[3,12,4,1024]{3,2,1,0:T(4,128)(2,1)S(1)}, f32[3,4,8,48]{3,2,1,0:T(8,128)S(1)}, f32[16,96,576]{2,1,0:T(8,128)S(1)}, f32[16,2,96,128]{3,2,1,0:T(8,128)S(1)}) custom-call(bf16[6,48,1024]{2,1,0:T(8,128)(2,1)S(1)} %get-tuple-element.30.refs_0_.refs_1_, bf16[6,48,1024]{2,1,0:T(8,128)(2,1)S(1)} %get-tuple-element.28.refs_1_.refs_0_, ...), custom_call_target="tpu_custom_call" | custom-call | flops 452984832 | bytes 10070016 | tf_op jit(solution)/shard_map/pallas_call | solution.py:54
  40.0 0.5 collective-permute-start.15
  40.5 0.4 collective-permute-start.14
  40.9 0.0 collective-permute-done.2.refs_4_
  40.9 0.0 collective-permute-start.13
  40.9 0.9 %collective-permute-done.1.refs_3_ = bf16[6,48,1024]{2,1,0:T(8,128)(2,1)S(1)} collective-permute-done((bf16[6,48,1024]{2,1,0:T(8,128)(2,1)S(1)}, bf16[6,48,1024]{2,1,0:T(8,128)(2,1)S(1)}, u32[]{:S(2)}, u32[]{:S(2)}) %collective-permute-start.1) | collective-permute-done | bytes 589856 | tf_op jit(solution)/shard_map/ppermute | solution.py:27
  41.7 0.0 collective-permute-done.refs_2_
  41.7 2.4 %collective-permute-done.15.refs_8_ = f32[3,4,8,48]{3,2,1,0:T(8,128)S(1)} collective-permute-done((f32[3,4,8,48]{3,2,1,0:T(8,128)S(1)}, f32[3,4,8,48]{3,2,1,0:T(8,128)S(1)}, u32[]{:S(2)}, u32[]{:S(2)}) %collective-permute-start.15) | collective-permute-done | bytes 18464 | tf_op jit(solution)/shard_map/ppermute | solution.py:27
  44.1 0.5 collective-permute-done.14.refs_7_
  44.6 0.0 collective-permute-done.13.refs_6_
  44.6 1.8 %shard_map.93 = (bf16[2,48,1024]{2,1,0:T(8,128)(2,1)S(1)}, bf16[2,48,1024]{2,1,0:T(8,128)(2,1)S(1)}) custom-call(bf16[6,48,1024]{2,1,0:T(8,128)(2,1)S(1)} %get-tuple-element.28.refs_1_.refs_0_, bf16[6,48,1024]{2,1,0:T(8,128)(2,1)S(1)} %get-tuple-element.30.refs_0_.refs_1_, bf16[6,48,1024]{2,1,0:T(8,128)(2,1)S(1)} %collective-permute-done.refs_2_, ...), custom_call_target="tpu_custom_call" | custom-call | flops 452984832 | bytes 3815424 | tf_op jit(solution)/shard_map/pallas_call | solution.py:54
  46.4 4.7 %collective-permute-start.16 = (bf16[2,48,1024]{2,1,0:T(8,128)(2,1)S(1)}, bf16[2,48,1024]{2,1,0:T(8,128)(2,1)S(1)}, u32[]{:S(2)}, u32[]{:S(2)}) collective-permute-start(bf16[2,48,1024]{2,1,0:T(8,128)(2,1)S(1)} %get-tuple-element.48), channel_id=1, source_target_pairs={{0,1},{1,0},{2,3},{3,2},{4,5},{5,4},{6,7},{7,6},{8,9},{9,8},{10,11... | collective-permute-start | bytes 589832 | tf_op jit(solution)/shard_map/ppermute | solution.py:38
  51.0 0.7 %collective-permute-start.17 = (bf16[2,48,1024]{2,1,0:T(8,128)(2,1)S(1)}, bf16[2,48,1024]{2,1,0:T(8,128)(2,1)S(1)}, u32[]{:S(2)}, u32[]{:S(2)}) collective-permute-start(bf16[2,48,1024]{2,1,0:T(8,128)(2,1)S(1)} %get-tuple-element.49), channel_id=1, source_target_pairs={{1,2},{2,1},{5,6},{6,5},{9,10},{10,9},{13,14},{14,13},{17,18},{18,... | collective-permute-start | bytes 589832 | tf_op jit(solution)/shard_map/ppermute | solution.py:38
  51.7 1.9 %shard_map.91.refs_12_ = bf16[3,12,4,1024]{3,2,1,0:T(4,128)(2,1)S(1)} custom-call(bf16[6,48,1024]{2,1,0:T(8,128)(2,1)S(1)} %get-tuple-element.30.refs_0_.refs_1_, bf16[6,48,1024]{2,1,0:T(8,128)(2,1)S(1)} %get-tuple-element.28.refs_1_.refs_0_, bf16[6,48,1024]{2,1,0:T(8,128)(2,1)S(1)} %collective-permute-done.3.refs_2_, ...), custom_call_target="tpu_custom_call" | custom-call | flops 452984832 | bytes 10027008 | tf_op jit(solution)/shard_map/pallas_call | solution.py:54
  53.6 4.8 %shard_map.92 = (f32[6,48,1024]{2,1,0:T(8,128)S(1)}, bf16[3,12,4,1024]{3,2,1,0:T(4,128)(2,1)}, bf16[3,12,4,1024]{3,2,1,0:T(4,128)(2,1)}) custom-call(bf16[6,48,1024]{2,1,0:T(8,128)(2,1)S(1)} %get-tuple-element.28.refs_1_.refs_0_, bf16[6,48,1024]{2,1,0:T(8,128)(2,1)S(1)} %get-tuple-element.30.refs_0_.refs_1_, ...), custom_call_target="tpu_custom_call" | custom-call | flops 905969664 | bytes 5781504 | tf_op jit(solution)/shard_map/pallas_call | solution.py:54
  58.4 0.0 collective-permute-done.16.part0
  58.5 0.0 collective-permute-done.17.part1
  58.5 0.9 %shard_map.94 = (bf16[3,12,4,1024]{3,2,1,0:T(4,128)(2,1)}, bf16[3,12,4,1024]{3,2,1,0:T(4,128)(2,1)}) custom-call(f32[6,48,1024]{2,1,0:T(8,128)S(1)} %get-tuple-element.47.total, bf16[2,48,1024]{2,1,0:T(8,128)(2,1)S(1)} %collective-permute-done.16.part0, bf16[2,48,1024]{2,1,0:T(8,128)(2,1)S(1)} %collective-permute-done.17.part1), custom_call_target="tpu_custom_call" | custom-call | bytes 2162688 | tf_op jit(solution)/shard_map/pallas_call | solution.py:54
  (2 shorter events, 0.1 us)
Async XLA Ops:
  1.9 24.4 %collective-permute-start.5 = (bf16[6,48,1024]{2,1,0:T(8,128)(2,1)S(1)}, bf16[6,48,1024]{2,1,0:T(8,128)(2,1)S(1)}, u32[]{:S(2)}, u32[]{:S(2)}) collective-permute-start(bf16[6,48,1024]{2,1,0:T(8,128)(2,1)S(1)} %get-tuple-element.28.refs_1_.refs_0_), channel_id=1, source_target_pairs={{0,16},{4,20},{8,24},{12,28},{16,0},{20,4},{24,8},{28,12},{1,17},{... | collective-permute-start | bytes 1769480 | tf_op jit(solution)/shard_map/ppermute | solution.py:27
  4.9 22.8 %collective-permute-start.4 = (bf16[6,48,1024]{2,1,0:T(8,128)(2,1)S(1)}, bf16[6,48,1024]{2,1,0:T(8,128)(2,1)S(1)}, u32[]{:S(2)}, u32[]{:S(2)}) collective-permute-start(bf16[6,48,1024]{2,1,0:T(8,128)(2,1)S(1)} %get-tuple-element.28.refs_1_.refs_0_), channel_id=1, source_target_pairs={{0,8},{4,12},{8,0},{12,4},{16,24},{20,28},{24,16},{28,20},{1,9},{5... | collective-permute-start | bytes 1769480 | tf_op jit(solution)/shard_map/ppermute | solution.py:27
  6.4 6.4 %collective-permute-start.7 = (bf16[2,48,1024]{2,1,0:T(8,128)(2,1)S(1)}, bf16[2,48,1024]{2,1,0:T(8,128)(2,1)S(1)}, u32[]{:S(2)}, u32[]{:S(2)}) collective-permute-start(bf16[2,48,1024]{2,1,0:T(8,128)(2,1)S(1)} %get-tuple-element.31), channel_id=1, source_target_pairs={{1,2},{2,1},{5,6},{6,5},{9,10},{10,9},{13,14},{14,13},{17,18},{18,... | collective-permute-start | bytes 589832 | tf_op jit(solution)/shard_map/ppermute | solution.py:38
  7.1 8.5 %collective-permute-start.6 = (bf16[2,48,1024]{2,1,0:T(8,128)(2,1)S(1)}, bf16[2,48,1024]{2,1,0:T(8,128)(2,1)S(1)}, u32[]{:S(2)}, u32[]{:S(2)}) collective-permute-start(bf16[2,48,1024]{2,1,0:T(8,128)(2,1)S(1)} %get-tuple-element.29.refs_2_.after), channel_id=1, source_target_pairs={{0,1},{1,0},{2,3},{3,2},{4,5},{5,4},{6,7},{7,6},{8,9},{9,8},{10,11... | collective-permute-start | bytes 589832 | tf_op jit(solution)/shard_map/ppermute | solution.py:38
  11.5 0.7 %copy-start = (s32[32,3]{0,1:T(4,128)S(1)}, s32[32,3]{0,1:T(4,128)}, u32[]{:S(2)}) copy-start(s32[32,3]{0,1:T(4,128)} %param.9) | copy-start | bytes 1156
  15.6 6.8 %collective-permute-start.10 = (bf16[2,48,1024]{2,1,0:T(8,128)(2,1)S(1)}, bf16[2,48,1024]{2,1,0:T(8,128)(2,1)S(1)}, u32[]{:S(2)}, u32[]{:S(2)}) collective-permute-start(bf16[2,48,1024]{2,1,0:T(8,128)(2,1)S(1)} %get-tuple-element.34), channel_id=1, source_target_pairs={{0,16},{4,20},{8,24},{12,28},{16,0},{20,4},{24,8},{28,12},{1,17},{... | collective-permute-start | bytes 589832 | tf_op jit(solution)/shard_map/ppermute | solution.py:27
  16.2 13.2 %collective-permute-start.3 = (bf16[6,48,1024]{2,1,0:T(8,128)(2,1)S(1)}, bf16[6,48,1024]{2,1,0:T(8,128)(2,1)S(1)}, u32[]{:S(2)}, u32[]{:S(2)}) collective-permute-start(bf16[6,48,1024]{2,1,0:T(8,128)(2,1)S(1)} %get-tuple-element.28.refs_1_.refs_0_), channel_id=1, source_target_pairs={{0,4},{4,0},{8,12},{12,8},{16,20},{20,16},{24,28},{28,24},{1,5},{5... | collective-permute-start | bytes 1769480 | tf_op jit(solution)/shard_map/ppermute | solution.py:27
  16.2 8.2 %collective-permute-start.9 = (bf16[2,48,1024]{2,1,0:T(8,128)(2,1)S(1)}, bf16[2,48,1024]{2,1,0:T(8,128)(2,1)S(1)}, u32[]{:S(2)}, u32[]{:S(2)}) collective-permute-start(bf16[2,48,1024]{2,1,0:T(8,128)(2,1)S(1)} %get-tuple-element.34), channel_id=1, source_target_pairs={{0,8},{4,12},{8,0},{12,4},{16,24},{20,28},{24,16},{28,20},{1,9},{5... | collective-permute-start | bytes 589832 | tf_op jit(solution)/shard_map/ppermute | solution.py:27
  22.5 5.3 %collective-permute-start.8 = (bf16[4,48,1024]{2,1,0:T(8,128)(2,1)S(1)}, bf16[4,48,1024]{2,1,0:T(8,128)(2,1)S(1)}, u32[]{:S(2)}, u32[]{:S(2)}) collective-permute-start(bf16[4,48,1024]{2,1,0:T(8,128)(2,1)S(1)} %get-tuple-element.33), channel_id=1, source_target_pairs={{0,4},{4,0},{8,12},{12,8},{16,20},{20,16},{24,28},{28,24},{1,5},{5... | collective-permute-start | bytes 1179656 | tf_op jit(solution)/shard_map/ppermute | solution.py:27
  24.4 16.4 %collective-permute-start.2 = (bf16[6,48,1024]{2,1,0:T(8,128)(2,1)S(1)}, bf16[6,48,1024]{2,1,0:T(8,128)(2,1)S(1)}, u32[]{:S(2)}, u32[]{:S(2)}) collective-permute-start(bf16[6,48,1024]{2,1,0:T(8,128)(2,1)S(1)} %get-tuple-element.30.refs_0_.refs_1_), channel_id=1, source_target_pairs={{0,16},{4,20},{8,24},{12,28},{16,0},{20,4},{24,8},{28,12},{1,17},{... | collective-permute-start | bytes 1769480 | tf_op jit(solution)/shard_map/ppermute | solution.py:27
  26.2 15.5 %collective-permute-start.1 = (bf16[6,48,1024]{2,1,0:T(8,128)(2,1)S(1)}, bf16[6,48,1024]{2,1,0:T(8,128)(2,1)S(1)}, u32[]{:S(2)}, u32[]{:S(2)}) collective-permute-start(bf16[6,48,1024]{2,1,0:T(8,128)(2,1)S(1)} %get-tuple-element.30.refs_0_.refs_1_), channel_id=1, source_target_pairs={{0,8},{4,12},{8,0},{12,4},{16,24},{20,28},{24,16},{28,20},{1,9},{5... | collective-permute-start | bytes 1769480 | tf_op jit(solution)/shard_map/ppermute | solution.py:27
  27.7 14.0 %collective-permute-start = (bf16[6,48,1024]{2,1,0:T(8,128)(2,1)S(1)}, bf16[6,48,1024]{2,1,0:T(8,128)(2,1)S(1)}, u32[]{:S(2)}, u32[]{:S(2)}) collective-permute-start(bf16[6,48,1024]{2,1,0:T(8,128)(2,1)S(1)} %get-tuple-element.30.refs_0_.refs_1_), channel_id=1, source_target_pairs={{0,4},{4,0},{8,12},{12,8},{16,20},{20,16},{24,28},{28,24},{1,5},{5... | collective-permute-start | bytes 1769480 | tf_op jit(solution)/shard_map/ppermute | solution.py:27
  27.8 7.4 %collective-permute-start.11 = (bf16[2,48,1024]{2,1,0:T(8,128)(2,1)S(1)}, bf16[2,48,1024]{2,1,0:T(8,128)(2,1)S(1)}, u32[]{:S(2)}, u32[]{:S(2)}) collective-permute-start(bf16[2,48,1024]{2,1,0:T(8,128)(2,1)S(1)} %get-tuple-element.35), channel_id=1, source_target_pairs={{0,1},{1,0},{2,3},{3,2},{4,5},{5,4},{6,7},{7,6},{8,9},{9,8},{10,11... | collective-permute-start | bytes 589832 | tf_op jit(solution)/shard_map/ppermute | solution.py:38
  29.4 5.7 %collective-permute-start.12 = (bf16[2,48,1024]{2,1,0:T(8,128)(2,1)S(1)}, bf16[2,48,1024]{2,1,0:T(8,128)(2,1)S(1)}, u32[]{:S(2)}, u32[]{:S(2)}) collective-permute-start(bf16[2,48,1024]{2,1,0:T(8,128)(2,1)S(1)} %get-tuple-element.36), channel_id=1, source_target_pairs={{1,2},{2,1},{5,6},{6,5},{9,10},{10,9},{13,14},{14,13},{17,18},{18,... | collective-permute-start | bytes 589832 | tf_op jit(solution)/shard_map/ppermute | solution.py:38
  40.0 4.1 %collective-permute-start.15 = (f32[3,4,8,48]{3,2,1,0:T(8,128)S(1)}, f32[3,4,8,48]{3,2,1,0:T(8,128)S(1)}, u32[]{:S(2)}, u32[]{:S(2)}) collective-permute-start(f32[3,4,8,48]{3,2,1,0:T(8,128)S(1)} %get-tuple-element.40.refs_5_), channel_id=1, source_target_pairs={{0,16},{4,20},{8,24},{12,28},{16,0},{20,4},{24,8},{28,12},{1,17},{... | collective-permute-start | bytes 55304 | tf_op jit(solution)/shard_map/ppermute | solution.py:27
  40.5 4.1 %collective-permute-start.14 = (f32[3,4,8,48]{3,2,1,0:T(8,128)S(1)}, f32[3,4,8,48]{3,2,1,0:T(8,128)S(1)}, u32[]{:S(2)}, u32[]{:S(2)}) collective-permute-start(f32[3,4,8,48]{3,2,1,0:T(8,128)S(1)} %get-tuple-element.40.refs_5_), channel_id=1, source_target_pairs={{0,8},{4,12},{8,0},{12,4},{16,24},{20,28},{24,16},{28,20},{1,9},{5... | collective-permute-start | bytes 55304 | tf_op jit(solution)/shard_map/ppermute | solution.py:27
  40.9 3.7 %collective-permute-start.13 = (f32[3,4,8,48]{3,2,1,0:T(8,128)S(1)}, f32[3,4,8,48]{3,2,1,0:T(8,128)S(1)}, u32[]{:S(2)}, u32[]{:S(2)}) collective-permute-start(f32[3,4,8,48]{3,2,1,0:T(8,128)S(1)} %get-tuple-element.40.refs_5_), channel_id=1, source_target_pairs={{0,4},{4,0},{8,12},{12,8},{16,20},{20,16},{24,28},{28,24},{1,5},{5... | collective-permute-start | bytes 55304 | tf_op jit(solution)/shard_map/ppermute | solution.py:27
  46.4 12.1 %collective-permute-start.16 = (bf16[2,48,1024]{2,1,0:T(8,128)(2,1)S(1)}, bf16[2,48,1024]{2,1,0:T(8,128)(2,1)S(1)}, u32[]{:S(2)}, u32[]{:S(2)}) collective-permute-start(bf16[2,48,1024]{2,1,0:T(8,128)(2,1)S(1)} %get-tuple-element.48), channel_id=1, source_target_pairs={{0,1},{1,0},{2,3},{3,2},{4,5},{5,4},{6,7},{7,6},{8,9},{9,8},{10,11... | collective-permute-start | bytes 589832 | tf_op jit(solution)/shard_map/ppermute | solution.py:38
  51.0 7.4 %collective-permute-start.17 = (bf16[2,48,1024]{2,1,0:T(8,128)(2,1)S(1)}, bf16[2,48,1024]{2,1,0:T(8,128)(2,1)S(1)}, u32[]{:S(2)}, u32[]{:S(2)}) collective-permute-start(bf16[2,48,1024]{2,1,0:T(8,128)(2,1)S(1)} %get-tuple-element.49), channel_id=1, source_target_pairs={{1,2},{2,1},{5,6},{6,5},{9,10},{10,9},{13,14},{14,13},{17,18},{18,... | collective-permute-start | bytes 589832 | tf_op jit(solution)/shard_map/ppermute | solution.py:38
